TPU v7x, 256 devices: a whole 4x4x8 slice. The times are simulated.
256 devices in a mesh: gx: 8 (over z), gy: 4 (over x_hi, core), gz: 8 (over x_lo, y).
Axes of the slice: x: 4 (x_hi: 2, x_lo: 2; x = x_hi * 2 + x_lo), y: 4, z: 8, core: 2. Of those that a mesh axis runs over, the one named last changes fastest.
Arguments:
- velocity: float32 [3, 128, 32, 1024], P(None, 'gx', 'gy', 'gz'), may hold values from -6 to 6
- acoustic: float32 [8192, 4, 512], P(('gx', 'gy', 'gz')), may hold values from -6 to 6
- projection: float32 [64, 512], replicated, may hold values from -0.75 to 0.75
- owner_index: int32 [8192, 1], P(('gx', 'gy', 'gz')), may hold values from 0 to 31; in each aligned block of 32 rows (0 to 31, 32 to 63, ...) at most 2 rows name the same one
- slot_element: int32 [256, 64], P(('gx', 'gy', 'gz')), may hold values from 0 to 31
- element_cell: int32 [256, 32], P(('gx', 'gy', 'gz')), may hold values from 0 to 31, each once within a row
Outputs:
- velocity_out: float32 [3, 128, 32, 1024], P(None, 'gx', 'gy', 'gz')
- acoustic_out: float32 [8192, 4, 512], P(('gx', 'gy', 'gz'))
Inputs may be any that keep to these rules, and one draw needn't show every extreme that they name: `owner_index`: owners are numbered gy index times 8 plus gz index within the sender's gx plane; among one device's 32 rows no owner appears more than 2 times. Slot q of a device feeds its stored element slot_element[q]. `element_cell`: each row is a permutation of the brick cells of one device.
All inputs are finite; a program needn't handle non-finite values.
Results may differ from a plain program's by a relative error of at most 0.0019.
Values may be sent and summed in bfloat16 or wider, within the bound.
No kernel may reach another device: no remote copies, remote signals or barrier semaphores. Data moves between devices by JAX's collectives and lax.ppermute only.
A program may use at most 128 MiB of HBM per device.

v0:
```python
import jax
import jax.numpy as jnp
import numpy as np
from jax import lax
from jax.experimental import pallas as pl
from jax.experimental.pallas import tpu as pltpu
from jax.sharding import PartitionSpec as P

F32 = jnp.float32
BF = jnp.bfloat16
ORDER = 7
K = ORDER + 1
LANES = 128
ROWS = K**3
FACE = K * K
FLOW_STEP = 0.1
VISCOSITY = 0.05
WAVE_STEP = 0.02
SOURCE_GAIN = 25.0
LIFT = WAVE_STEP * 0.5 * ORDER * (ORDER + 1) / 2.0
XV = 48
YV = 144
ZV = 32


def legendre_table(points, order):
    columns = [points * 0.0 + 1.0, points]
    for degree in range(2, order + 1):
        columns.append(
            ((2 * degree - 1) * points * columns[degree - 1] - (degree - 1) * columns[degree - 2])
            / degree
        )
    return np.stack(columns, axis=1)


def lobatto_tables(order):
    point_count = order + 1
    points = -np.cos(np.pi * np.arange(point_count) / order)
    for _ in range(60):
        legendre = legendre_table(points, order)
        points = points - (points * legendre[:, order] - legendre[:, order - 1]) / (
            point_count * legendre[:, order]
        )
    legendre = legendre_table(points, order)
    highest = legendre[:, order]
    spacing = points[:, None] - points[None, :] + np.eye(point_count)
    derivative = highest[:, None] / (highest[None, :] * spacing)
    derivative = derivative * (1.0 - np.eye(point_count))
    derivative[0, 0] = -order * point_count / 4.0
    derivative[order, order] = order * point_count / 4.0
    return derivative


DERIV = lobatto_tables(ORDER) * (-WAVE_STEP)


def split2(value):
    high = value.astype(BF)
    return high, (value - high.astype(F32)).astype(BF)


def nn(a, b):
    return lax.dot_general(a, b, (((1,), (0,)), ((), ())), preferred_element_type=F32)


def nt(a, b):
    return lax.dot_general(a, b, (((1,), (1,)), ((), ())), preferred_element_type=F32)


def tn(a, b):
    return lax.dot_general(a, b, (((0,), (0,)), ((), ())), preferred_element_type=F32)


def iota(shape, axis):
    return lax.broadcasted_iota(jnp.int32, shape, axis)


def roll(value, shift, axis):
    size = value.shape[axis]
    return pltpu.roll(value, shift % size, axis)


def call(kernel, out_shape, *args, scratch=(), flops=10**6, moved=10**6):
    return pl.pallas_call(
        kernel,
        out_shape=out_shape,
        in_specs=[pl.BlockSpec(memory_space=pltpu.VMEM)] * len(args),
        out_specs=jax.tree.map(lambda _: pl.BlockSpec(memory_space=pltpu.VMEM), out_shape),
        scratch_shapes=list(scratch),
        compiler_params=pltpu.CompilerParams(vmem_limit_bytes=16 * 2**20),
        cost_estimate=pl.CostEstimate(flops=flops, bytes_accessed=moved, transcendentals=0),
    )(*args)


def shape(*dims, dtype=F32):
    return jax.ShapeDtypeStruct(dims, dtype)


def stored_rows(acoustic_ref, first, last):
    return jnp.concatenate([acoustic_ref[:, v, first:last] for v in range(4)], axis=0)


def cell_matrix(cell_ref):
    cell = jnp.concatenate([cell_ref[...]] * 4, axis=1)
    cell = jnp.broadcast_to(cell, (LANES, LANES))
    row, column = iota((LANES, LANES), 0), iota((LANES, LANES), 1)
    return (cell == row % 32) & (row // 32 == column // 32)


def start_kernel(velocity_ref, acoustic_ref, cell_ref, low_ref, high_ref):
    place = jnp.where(cell_matrix(cell_ref), 1.0, 0.0).astype(BF)
    faces = jnp.concatenate(
        [stored_rows(acoustic_ref, 0, FACE), stored_rows(acoustic_ref, ROWS - FACE, ROWS)], axis=1
    )
    brick = nn(place, faces.astype(BF))
    turned = jnp.transpose(brick).astype(BF)
    low_ref[XV:, :] = turned[:FACE]
    high_ref[XV:, :] = turned[FACE:]
    for c in range(3):
        low_ref[c * 16 : c * 16 + 16, :] = velocity_ref[c, 0:16, :].astype(BF)
        high_ref[c * 16 : c * 16 + 16, :] = velocity_ref[c, 112:128, :].astype(BF)


def prepare_kernel(
    acoustic_ref,
    cell_ref,
    projection_ref,
    state_ref,
    ylow_ref,
    yhigh_ref,
    zlow_ref,
    zhigh_ref,
    back_ref,
    table_ref,
):
    chosen = jnp.where(cell_matrix(cell_ref), 1.0, 0.0)
    place = chosen.astype(BF)
    back_ref[...] = jnp.transpose(chosen).astype(BF)
    high, low = split2(stored_rows(acoustic_ref, 0, ROWS))
    brick = nn(place, high) + nn(place, low)
    state_ref[...] = jnp.transpose(brick)
    for a in range(K):
        ylow_ref[a * K : a * K + K, :] = state_ref[a * FACE : a * FACE + K, :]
        yhigh_ref[a * K : a * K + K, :] = state_ref[a * FACE + FACE - K : a * FACE + FACE, :]
    zlow_ref[...] = state_ref[pl.ds(0, FACE, stride=K), :]
    zhigh_ref[...] = state_ref[pl.ds(K - 1, FACE, stride=K), :]
    high, low = split2(projection_ref[...])
    row, column = iota((64, 64), 0), iota((64, 64), 1)
    order = jnp.where(column == (row % 16) * 4 + row // 16, 1.0, 0.0).astype(BF)
    high, low = nn(order, high), nn(order, low)
    table_ref[...] = jnp.transpose(jnp.concatenate([high, low, high], axis=0)).astype(BF)


def y_kernel(velocity_ref, xlow_ref, xhigh_ref, ylow_ref, yhigh_ref, low_ref, high_ref, wide):
    for c in range(3):
        wide[c, 0:16, :] = xlow_ref[c * 16 : c * 16 + 16, :].astype(F32)
        wide[c, 16:144, :] = velocity_ref[c]
        wide[c, 144:160, :] = xhigh_ref[c * 16 : c * 16 + 16, :].astype(F32)
    for out, first, trace in ((low_ref, 0, ylow_ref), (high_ref, 6, yhigh_ref)):
        pieces = []
        for y in range(2):
            for c in range(3):
                pieces.append(wide[c, pl.ds(first + y, 20, stride=8), :])
                pieces.append(jnp.zeros((4, LANES), F32))
        out[0:YV, :] = jnp.concatenate(pieces, axis=0).astype(BF)
        out[YV:, :] = trace[...].astype(BF)


def z_kernel(
    velocity_ref,
    xlow_ref,
    xhigh_ref,
    ylow_ref,
    yhigh_ref,
    zlow_ref,
    zhigh_ref,
    wide_ref,
    own_ref,
    low_ref,
    high_ref,
    held,
):
    held[0] = ylow_ref[0:YV, :].astype(F32)
    held[1] = yhigh_ref[0:YV, :].astype(F32)
    for c in range(3):
        low = xlow_ref[c * 16 : c * 16 + 16, :].astype(F32)
        high = xhigh_ref[c * 16 : c * 16 + 16, :].astype(F32)
        for x in range(2):
            wide_ref[c, x, 2:10, :] = low[x * 8 : x * 8 + 8]
            wide_ref[c, 18 + x, 2:10, :] = high[x * 8 : x * 8 + 8]
        for x in range(16):
            wide_ref[c, 2 + x, 2:10, :] = velocity_ref[c, x * 8 : x * 8 + 8, :]
        for y in range(2):
            for side in range(2):
                rows = held[side, y * 72 + c * 24 : y * 72 + c * 24 + 20, :]
                wide_ref[c, :, y + 10 * side, :] = rows
        wide_ref[c, :, 12:16, :] = jnp.zeros((20, 4, LANES), F32)
    row, column = iota((16, LANES), 0), iota((16, LANES), 1)
    picks = ((row < 2) & (column == row)) | ((row >= 2) & (row < 4) & (column == row + 124))
    picks = jnp.where(picks, 1.0, 0.0).astype(BF)
    for c in range(3):
        rows = wide_ref[c].reshape(320, LANES).astype(BF)
        own = nt(picks, rows)
        own_ref[c, :, 0:320] = own[0:8]
        own_ref[c, :, 320:384] = jnp.zeros((8, 64), F32)
    for out, first, trace in ((low_ref, 0, zlow_ref), (high_ref, 2, zhigh_ref)):
        pieces = []
        for c in range(3):
            for j in range(3):
                pieces.append(own_ref[c, first : first + 2, j * 128 : j * 128 + 128])
        pieces.append(jnp.zeros((ZV - 18, LANES), F32))
        out[0:ZV, :] = jnp.concatenate(pieces, axis=0).astype(BF)
        out[ZV:, :] = trace[...].astype(BF)


def differences(low, high):
    return [[high[a][c] - low[a][c] for c in range(3)] for a in range(3)]


def moved_on(centre, low, high, diff):
    scaled = [(-0.5 * FLOW_STEP) * centre[a] for a in range(3)]
    out = []
    for c in range(3):
        spread = (low[0][c] + high[0][c]) + (low[1][c] + high[1][c]) + (low[2][c] + high[2][c])
        carried = scaled[0] * diff[0][c] + scaled[1] * diff[1][c] + scaled[2] * diff[2][c]
        out.append(
            (1.0 - 6.0 * FLOW_STEP * VISCOSITY) * centre[c]
            + (FLOW_STEP * VISCOSITY) * spread
            + carried
        )
    return out


def lamb(centre, diff):
    w = [diff[1][2] - diff[2][1], diff[2][0] - diff[0][2], diff[0][1] - diff[1][0]]
    return [
        w[1] * centre[2] - w[2] * centre[1],
        w[2] * centre[0] - w[0] * centre[2],
        w[0] * centre[1] - w[1] * centre[0],
    ]


def flow_kernel(
    wide_ref,
    own_ref,
    zlow_ref,
    zhigh_ref,
    place_ref,
    out_ref,
    volume_ref,
    ends,
    halo,
    middle,
    sums,
):
    low = zlow_ref[0:ZV, :].astype(F32)
    high = zhigh_ref[0:ZV, :].astype(F32)
    for c in range(3):
        for j in range(3):
            lane = slice(j * 128, j * 128 + 128)
            at = 2 * (3 * c + j)
            ends[c, 0:2, lane] = low[at : at + 2]
            ends[c, 2:6, lane] = own_ref[c, 0:4, lane]
            ends[c, 6:8, lane] = high[at : at + 2]
    row, column = iota((16, LANES), 0), iota((16, LANES), 1)
    spots = ((row == 1) & (column == 0)) | ((row == 6) & (column == 127))
    spots = jnp.where(spots, 1.0, 0.0).astype(BF)
    zeros = jnp.zeros((8, 384), F32)

    def spread_out(values, level):
        for c in range(3):
            both = jnp.concatenate([values[c], zeros], axis=0).astype(BF)
            halo[level, c] = tn(both, spots)[0:320].reshape(20, 16, LANES)

    edge = [ends[c] for c in range(3)]
    spread_out(edge, 0)
    edge_low = [
        [roll(e, 16, 1) for e in edge],
        [roll(e, 1, 1) for e in edge],
        [roll(e, 1, 0) for e in edge],
    ]
    edge_high = [
        [roll(e, -16, 1) for e in edge],
        [roll(e, -1, 1) for e in edge],
        [roll(e, -1, 0) for e in edge],
    ]
    spread_out(
        moved_on(edge, edge_low, edge_high, differences(edge_low, edge_high)), 1
    )

    def along_z(values, edges):
        lane = iota(values[0].shape, values[0].ndim - 1)
        axis = values[0].ndim - 1
        low = [jnp.where(lane == 0, h, roll(v, 1, axis)) for v, h in zip(values, edges)]
        high = [jnp.where(lane == 127, h, roll(v, -1, axis)) for v, h in zip(values, edges)]
        return low, high

    def plane(source, x, level, y):
        centre = [source[c, x, y, :] for c in range(3)]
        zlow, zhigh = along_z(centre, [halo[level, c, x, y, :] for c in range(3)])
        up = slice(y.start + 1, y.stop + 1)
        down = slice(y.start - 1, y.stop - 1)
        low = [
            [source[c, x - 1, y, :] for c in range(3)],
            [source[c, x, down, :] for c in range(3)],
            zlow,
        ]
        high = [
            [source[c, x + 1, y, :] for c in range(3)],
            [source[c, x, up, :] for c in range(3)],
            zhigh,
        ]
        return centre, low, high

    inner = slice(2, 10)
    for y in (1, 10):
        def line(source, first, at):
            return [source[c, first : first + 16, at, :] for c in range(3)]

        centre = line(wide_ref, 2, y)
        zlow, zhigh = along_z(
            centre, [halo[0, c, 2:18, y, :] for c in range(3)]
        )
        low = [line(wide_ref, 1, y), line(wide_ref, 2, y - 1), zlow]
        high = [line(wide_ref, 3, y), line(wide_ref, 2, y + 1), zhigh]
        new = moved_on(centre, low, high, differences(low, high))
        for c in range(3):
            middle[c, 2:18, y, :] = new[c]

    def add_lamb(parts, x, step):
        i, a = (x // 2) // 4, (x // 2) % 4
        for c in range(3):
            at = ((step * 3 + c) * 4 + a) * 8
            sums[i, at : at + 8, :] = parts[c]

    held = None
    for x in range(1, 19):
        centre, low, high = plane(wide_ref, x, 0, inner)
        diff = differences(low, high)
        new = moved_on(centre, low, high, diff)
        for c in range(3):
            middle[c, x, inner, :] = new[c]
        if 2 <= x < 18:
            parts = lamb(centre, diff)
            if x % 2 == 0:
                held = parts
            else:
                add_lamb([p + h for p, h in zip(parts, held)], x - 2, 0)
    for x in range(2, 18):
        centre, low, high = plane(middle, x, 1, inner)
        diff = differences(low, high)
        new = moved_on(centre, low, high, diff)
        for c in range(3):
            out_ref[c, (x - 2) * 8 : (x - 2) * 8 + 8, :] = new[c]
        parts = lamb(centre, diff)
        if x % 2 == 0:
            held = parts
        else:
            add_lamb([p + h for p, h in zip(parts, held)], x - 2, 1)
    both = []
    for i in range(2):
        both.append(sums[i, pl.ds(0, 96, stride=2), :] + sums[i, pl.ds(1, 96, stride=2), :])
    pairs = jnp.concatenate(both, axis=1)
    pairs = jnp.concatenate([pairs, jnp.zeros((32, 256), F32)], axis=0)
    high, low = split2(pairs)
    place = place_ref[...]
    volume_ref[...] = ((nt(place, high) + nt(place, low)) * (1.0 / 16.0)).astype(BF)


def swapped(value, axis):
    kind = iota(value.shape, value.ndim - 1) // 32
    shift = 32 * (1 + axis)
    last = value.ndim - 1
    return jnp.where(
        kind == 0,
        roll(value, -shift, last),
        jnp.where(kind == 1 + axis, roll(value, shift, last), 0.0),
    )


def outer(axis, own_low, own_high, from_low, from_high):
    if axis == 0:
        return from_low, from_high
    lane = iota(own_low.shape, 1)
    if axis == 1:
        part = (lane // 16) % 2
        low = jnp.where(part == 1, from_low, own_high)
        high = jnp.where(part == 0, from_high, own_low)

        def turn(v):
            return jnp.where(part == 0, roll(v, -16, 1), roll(v, 16, 1))

        return turn(low), turn(high)
    part = lane % 16
    low = jnp.where(part == 15, from_low, own_high)
    high = jnp.where(part == 0, from_high, own_low)
    return (
        jnp.where(part == 0, roll(low, -15, 1), roll(low, 1, 1)),
        jnp.where(part == 15, roll(high, 15, 1), roll(high, -1, 1)),
    )


def lifts(axis, own_low, own_high, from_low, from_high):
    low, high = outer(axis, own_low, own_high, from_low, from_high)
    low, high = own_low - low, own_high - high
    return -LIFT * (swapped(low, axis) + low), LIFT * (swapped(high, axis) - high)


def face_pair(ref, axis):
    if axis == 0:
        return ref[0:FACE, :], ref[ROWS - FACE : ROWS, :]
    if axis == 1:
        low = [ref[a * FACE : a * FACE + K, :] for a in range(K)]
        high = [ref[a * FACE + FACE - K : a * FACE + FACE, :] for a in range(K)]
        return jnp.concatenate(low, axis=0), jnp.concatenate(high, axis=0)
    return ref[pl.ds(0, FACE, stride=K), :], ref[pl.ds(K - 1, FACE, stride=K), :]


def add_pair(ref, axis, low, high):
    if axis == 0:
        ref[0:FACE, :] += low
        ref[ROWS - FACE : ROWS, :] += high
    elif axis == 1:
        for a in range(K):
            ref[a * FACE : a * FACE + K, :] += low[a * K : a * K + K]
            ref[a * FACE + FACE - K : a * FACE + FACE, :] += high[a * K : a * K + K]
    else:
        ref[pl.ds(0, FACE, stride=K), :] += low
        ref[pl.ds(K - 1, FACE, stride=K), :] += high


def volume_part(state_ref, out_ref, column_ref, extra_ref=None):
    for a in range(K):
        rows = [state_ref[a * FACE + b * K : a * FACE + b * K + K, :] for b in range(K)]
        along_y = [swapped(r, 1) for r in rows]
        along_z = [swapped(r, 2) for r in rows]
        for b in range(K):
            total = rows[b]
            at = a * FACE + b * K
            if extra_ref is not None:
                total = total - extra_ref[at : at + K, :]
            for m in range(K):
                total = total + float(DERIV[b, m]) * along_y[m]
            for m in range(K):
                total = total + column_ref[m * K : m * K + K, :] * jnp.broadcast_to(
                    along_z[b][m : m + 1, :], (K, LANES)
                )
            out_ref[at : at + K, :] = total
    for b in range(K):
        rows = [
            swapped(state_ref[a * FACE + b * K : a * FACE + b * K + K, :], 0) for a in range(K)
        ]
        for a in range(K):
            at = a * FACE + b * K
            total = out_ref[at : at + K, :]
            for m in range(K):
                total = total + float(DERIV[a, m]) * rows[m]
            out_ref[at : at + K, :] = total


def first_kernel(
    state_ref, column_ref, xlow_ref, xhigh_ref, ylow_ref, yhigh_ref, out_ref
):
    volume_part(state_ref, out_ref, column_ref)
    for axis, low, high, skip in ((0, xlow_ref, xhigh_ref, XV), (1, ylow_ref, yhigh_ref, YV)):
        pair = face_pair(state_ref, axis)
        pair = lifts(axis, *pair, low[skip:, :].astype(F32), high[skip:, :].astype(F32))
        add_pair(out_ref, axis, *pair)


def source_kernel(
    arrived_ref,
    gather_ref,
    table_ref,
    base_ref,
    zown_low_ref,
    zown_high_ref,
    zlow_ref,
    zhigh_ref,
    state_ref,
    extra_ref,
    xl_ref,
    xh_ref,
    yl_ref,
    yh_ref,
    zl_ref,
    zh_ref,
):
    summed = tn(arrived_ref[...], gather_ref[...])
    kind = iota((16, LANES), 1) // 32
    steps = []
    for t in range(2):
        rows = []
        for z in range(4):
            total = jnp.zeros((16, LANES), F32)
            for c in range(3):
                at = t * 48 + c * 16
                total = jnp.where(
                    kind == 1 + c, summed[at : at + 16, z * 128 : z * 128 + 128], total
                )
            rows.append(total)
        steps.append(jnp.concatenate(rows, axis=0))
    high, low = split2(jnp.concatenate(steps, axis=1))
    source = nn(table_ref[...], jnp.concatenate([high, high, low], axis=0))
    source = (WAVE_STEP * SOURCE_GAIN) * source
    state_ref[...] = base_ref[...] - source[:, 0:LANES]
    extra_ref[...] = source[:, LANES:]
    pair = lifts(
        2,
        zown_low_ref[...],
        zown_high_ref[...],
        zlow_ref[ZV:, :].astype(F32),
        zhigh_ref[ZV:, :].astype(F32),
    )
    add_pair(state_ref, 2, *pair)
    for axis, outs in enumerate(((xl_ref, xh_ref), (yl_ref, yh_ref), (zl_ref, zh_ref))):
        low, high = face_pair(state_ref, axis)
        outs[0][...] = low.astype(BF)
        outs[1][...] = high.astype(BF)


def second_kernel(state_ref, extra_ref, column_ref, out_ref):
    volume_part(state_ref, out_ref, column_ref, extra_ref)


def last_kernel(
    base_ref, state_ref, back_ref, xl_ref, xh_ref, yl_ref, yh_ref, zl_ref, zh_ref, out_ref, total
):
    total[...] = base_ref[...]
    for axis, (low, high) in enumerate(((xl_ref, xh_ref), (yl_ref, yh_ref), (zl_ref, zh_ref))):
        pair = face_pair(state_ref, axis)
        pair = lifts(axis, *pair, low[...].astype(F32), high[...].astype(F32))
        add_pair(total, axis, *pair)
    high, low = split2(jnp.transpose(total[...]))
    back = back_ref[...]
    rows = nn(back, high) + nn(back, low)
    for v in range(4):
        out_ref[:, v, :] = rows[v * 32 : v * 32 + 32, :]


def both_ways(low, high, axis):
    count = lax.axis_size(axis)
    up = [(i, (i + 1) % count) for i in range(count)]
    down = [(b, a) for a, b in up]
    return lax.ppermute(high, axis, up), lax.ppermute(low, axis, down)


def placement(owner_index):
    owners = owner_index[:, 0]
    order = jnp.arange(32, dtype=jnp.int32)
    same = (owners[:, None] == owners[None, :]) & (order[None, :] < order[:, None])
    slots = owners * 2 + jnp.sum(same.astype(jnp.int32), axis=1)
    row, column = iota((256, 256), 0), iota((256, 256), 1)
    wanted = (row // 8) * 2 + row % 2
    fits = (jnp.repeat(slots, 8)[None, :] == wanted) & ((column % 8) // 2 == (row % 8) // 2)
    return fits.astype(BF)


def gathering(slot_element, element_cell):
    element = jnp.arange(32, dtype=jnp.int32)
    named = slot_element[0][:, None] == element[None, :]
    targets = jnp.sum(jnp.where(named, element_cell, 0), axis=1)
    targets = jnp.broadcast_to(targets.reshape(32, 1, 2), (32, 4, 2)).reshape(256)
    row, column = iota((256, 512), 0), iota((256, 512), 1)
    fits = (targets[:, None] == column % 32) & (column // 128 == (row % 8) // 2)
    return fits.astype(BF)


def on_device(velocity, acoustic, projection, owner_index, slot_element, element_cell):
    velocity = velocity.reshape(3, 128, LANES)
    face = shape(FACE, LANES, dtype=BF)
    state = shape(ROWS, LANES)
    column = jnp.asarray(
        np.broadcast_to(DERIV.T.reshape(FACE, 1), (FACE, LANES)), F32
    )
    send = shape(XV + FACE, LANES, dtype=BF)
    xlow, xhigh = call(start_kernel, (send, send), velocity, acoustic, element_cell)
    xlow, xhigh = both_ways(xlow, xhigh, "gx")
    trace = shape(FACE, LANES)
    first, yown_low, yown_high, zown_low, zown_high, back, table = call(
        prepare_kernel,
        (state, trace, trace, trace, trace, shape(LANES, LANES, dtype=BF), shape(ROWS, 192, dtype=BF)),
        acoustic,
        element_cell,
        projection,
    )
    place = placement(owner_index)
    gather = gathering(slot_element, element_cell)
    send = shape(YV + FACE, LANES, dtype=BF)
    ylow, yhigh = call(
        y_kernel,
        (send, send),
        velocity,
        xlow,
        xhigh,
        yown_low,
        yown_high,
        scratch=[pltpu.VMEM((3, 160, LANES), F32)],
    )
    ylow, yhigh = both_ways(ylow, yhigh, "gy")
    send = shape(ZV + FACE, LANES, dtype=BF)
    wide, own, zlow, zhigh = call(
        z_kernel,
        (shape(3, 20, 16, LANES), shape(3, 8, 384), send, send),
        velocity,
        xlow,
        xhigh,
        ylow,
        yhigh,
        zown_low,
        zown_high,
        scratch=[pltpu.VMEM((2, YV, LANES), F32)],
    )
    zlow, zhigh = both_ways(zlow, zhigh, "gz")
    base = call(first_kernel, state, first, column, xlow, xhigh, ylow, yhigh)
    flow, volumes = call(
        flow_kernel,
        (shape(3, 128, LANES), shape(256, LANES, dtype=BF)),
        wide,
        own,
        zlow,
        zhigh,
        place,
        scratch=[
            pltpu.VMEM((3, 8, 384), F32),
            pltpu.VMEM((2, 3, 20, 16, LANES), F32),
            pltpu.VMEM((3, 20, 16, LANES), F32),
            pltpu.VMEM((2, 192, LANES), F32),
        ],
    )
    arrived = lax.all_to_all(
        volumes.reshape(32, 8, LANES), ("gy", "gz"), split_axis=0, concat_axis=0, tiled=True
    ).reshape(256, LANES)
    state1, extra, *faces = call(
        source_kernel,
        (state, state) + (face,) * 6,
        arrived,
        gather,
        table,
        base,
        zown_low,
        zown_high,
        zlow,
        zhigh,
    )
    got = []
    for at, axis in ((4, "gz"), (2, "gy"), (0, "gx")):
        got = list(both_ways(faces[at], faces[at + 1], axis)) + got
    base = call(second_kernel, state, state1, extra, column)
    out = call(
        last_kernel,
        shape(*acoustic.shape),
        base,
        state1,
        back,
        *got,
        scratch=[pltpu.VMEM((ROWS, LANES), F32)],
    )
    return flow.reshape(3, 16, 8, LANES), out


def solution(mesh):
    whole = P(("gx", "gy", "gz"), None, None)
    rows = P(("gx", "gy", "gz"), None)
    flow = P(None, "gx", "gy", "gz")
    return jax.shard_map(
        on_device,
        mesh=mesh,
        in_specs=(flow, whole, P(), rows, rows, rows),
        out_specs=(flow, whole),
        check_vma=False,
    )
```

profile of v0, /device:TPU:24, one launch (start us, length us, event | category | flops | bytes accessed | tf_op | source)
XLA Modules:
  0.0 54.6 jit_solution(17308464379947146164)
XLA Ops:
  0.6 0.6 %copy-done.6 = s32[1,32]{1,0:T(1,128)S(1)} copy-done((s32[1,32]{1,0:T(1,128)S(1)}, s32[1,32]{1,0:T(1,128)}, u32[]{:S(2)}) %copy-start.6) | copy-done | bytes 152
  1.3 0.9 %copy-done = f32[3,16,8,128]{3,2,1,0:T(8,128)S(1)} copy-done((f32[3,16,8,128]{3,2,1,0:T(8,128)S(1)}, f32[3,16,8,128]{3,2,1,0:T(8,128)}, u32[]{:S(2)}) %copy-start) | copy-done | bytes 196632
  2.2 0.9 %copy-done.2 = f32[32,4,512]{2,1,0:T(4,128)S(1)} copy-done((f32[32,4,512]{2,1,0:T(4,128)S(1)}, f32[32,4,512]{2,1,0:T(4,128)}, u32[]{:S(2)}) %copy-start.2) | copy-done | bytes 262168
  3.5 2.0 %collective-permute-start = (bf16[112,128]{1,0:T(8,128)(2,1)S(1)}, bf16[112,128]{1,0:T(8,128)(2,1)S(1)}, u32[]{:S(2)}, u32[]{:S(2)}) collective-permute-start(bf16[112,128]{1,0:T(8,128)(2,1)S(1)} %get-tuple-element.27), channel_id=1, source_target_pairs={{0,32},{32,64},{64,96},{96,128},{128,160},{160,192},{192,224},{224... | collective-permute-start | bytes 86024 | tf_op jit(solution)/shard_map/ppermute | solution.py:545
  5.5 4.0 %collective-permute-start.1 = (bf16[112,128]{1,0:T(8,128)(2,1)S(1)}, bf16[112,128]{1,0:T(8,128)(2,1)S(1)}, u32[]{:S(2)}, u32[]{:S(2)}) collective-permute-start(bf16[112,128]{1,0:T(8,128)(2,1)S(1)} %get-tuple-element.28), channel_id=1, source_target_pairs={{32,0},{64,32},{96,64},{128,96},{160,128},{192,160},{224,192},{0,2... | collective-permute-start | bytes 86024 | tf_op jit(solution)/shard_map/ppermute | solution.py:545
  10.0 0.6 %fusion.20.place_ref = bf16[256,256]{1,0:T(8,128)(2,1)S(1)} fusion(s32[256]{0:T(256)S(1)} %get-tuple-element.54, s32[256]{0:T(256)S(1)} %get-tuple-element.55, s32[256]{0:T(256)S(1)} %get-tuple-element.52, s32[256]{0:T(256)S(1)} %get-tuple-element.58, s32[256]{0:T(256)S(1)} %get-tuple-element.53, s32[256]{0:T(256)S(1)} %get-tuple-element.59, s32[256]{0:T(256)S(1)} %eq.64, ...), kind=kLoop, calls=%fused_computation.43 | loop fusion | flops 2621440 | bytes 139008 | tf_op jit(solution)/shard_map/convert_element_type | solution.py:556
  10.6 0.5 shard_map.87
  11.7 3.2 %collective-permute-start.3 = (bf16[208,128]{1,0:T(8,128)(2,1)S(1)}, bf16[208,128]{1,0:T(8,128)(2,1)S(1)}, u32[]{:S(2)}, u32[]{:S(2)}) collective-permute-start(bf16[208,128]{1,0:T(8,128)(2,1)S(1)} %get-tuple-element.32), channel_id=1, source_target_pairs={{8,0},{16,8},{24,16},{0,24},{9,1},{17,9},{25,17},{1,25},{10,2},{18... | collective-permute-start | bytes 159752 | tf_op jit(solution)/shard_map/ppermute | solution.py:545
  14.9 1.8 %collective-permute-done.2.ylow_ref = bf16[208,128]{1,0:T(8,128)(2,1)S(1)} collective-permute-done((bf16[208,128]{1,0:T(8,128)(2,1)S(1)}, bf16[208,128]{1,0:T(8,128)(2,1)S(1)}, u32[]{:S(2)}, u32[]{:S(2)}) %collective-permute-start.2) | collective-permute-done | bytes 53280 | tf_op jit(solution)/shard_map/ppermute | solution.py:545
  17.0 1.2 %collective-permute-start.4 = (bf16[96,128]{1,0:T(8,128)(2,1)S(1)}, bf16[96,128]{1,0:T(8,128)(2,1)S(1)}, u32[]{:S(2)}, u32[]{:S(2)}) collective-permute-start(bf16[96,128]{1,0:T(8,128)(2,1)S(1)} %get-tuple-element.37), channel_id=1, source_target_pairs={{0,1},{1,2},{2,3},{3,4},{4,5},{5,6},{6,7},{7,0},{8,9},{9,10},{10,1... | collective-permute-start | bytes 73736 | tf_op jit(solution)/shard_map/ppermute | solution.py:545
  18.2 0.9 %collective-permute-start.5 = (bf16[96,128]{1,0:T(8,128)(2,1)S(1)}, bf16[96,128]{1,0:T(8,128)(2,1)S(1)}, u32[]{:S(2)}, u32[]{:S(2)}) collective-permute-start(bf16[96,128]{1,0:T(8,128)(2,1)S(1)} %get-tuple-element.38), channel_id=1, source_target_pairs={{1,0},{2,1},{3,2},{4,3},{5,4},{6,5},{7,6},{0,7},{9,8},{10,9},{11,1... | collective-permute-start | bytes 73736 | tf_op jit(solution)/shard_map/ppermute | solution.py:545
  19.4 1.5 %collective-permute-done.4.zlow_ref = bf16[96,128]{1,0:T(8,128)(2,1)S(1)} collective-permute-done((bf16[96,128]{1,0:T(8,128)(2,1)S(1)}, bf16[96,128]{1,0:T(8,128)(2,1)S(1)}, u32[]{:S(2)}, u32[]{:S(2)}) %collective-permute-start.4) | collective-permute-done | bytes 24608 | tf_op jit(solution)/shard_map/ppermute | solution.py:545
  20.9 3.3 %collective-permute-done.5.zhigh_ref = bf16[96,128]{1,0:T(8,128)(2,1)S(1)} collective-permute-done((bf16[96,128]{1,0:T(8,128)(2,1)S(1)}, bf16[96,128]{1,0:T(8,128)(2,1)S(1)}, u32[]{:S(2)}, u32[]{:S(2)}) %collective-permute-start.5) | collective-permute-done | bytes 24608 | tf_op jit(solution)/shard_map/ppermute | solution.py:545
  24.2 1.8 %shard_map.90 = (f32[3,128,128]{2,1,0:T(8,128)}, bf16[256,128]{1,0:T(8,128)(2,1)}) custom-call(f32[3,20,16,128]{3,2,1,0:T(8,128)S(1)} %get-tuple-element.35.wide_ref, f32[3,8,384]{2,1,0:T(8,128)S(1)} %get-tuple-element.36.own_ref, bf16[96,128]{1,0:T(8,128)(2,1)S(1)} %collective-permute-done.4.zlow_ref, bf16[96,128]{1,0:T(8,128)(2,1)S(1)} %collective-permute-done.5.zhigh_ref, ...), custom_call_target="tpu_custom_call" | custom-call | flops 1000000 | bytes 1000000 | tf_op jit(solution)/shard_map/pallas_call | solution.py:84
  25.9 6.8 %all-to-all-start = ((bf16[32,8,128]{2,1,0:T(8,128)(2,1)}), bf16[32,8,128]{2,1,0:T(8,128)(2,1)S(1)}, u32[]{:S(2)}, u32[]{:S(2)}) async-start(bf16[32,8,128]{2,1,0:T(8,128)(2,1)} %bitcast.3), calls=%async_computation | async-start | bytes 131072 | tf_op jit(solution)/shard_map/all_to_all | solution.py:631
  33.5 0.7 %shard_map.91.base_ref = f32[512,128]{1,0:T(8,128)S(1)} custom-call(f32[512,128]{1,0:T(8,128)S(1)} %get-tuple-element.42.state_ref, f32[64,128]{1,0:T(8,128)S(1)} %copy-done.4, bf16[112,128]{1,0:T(8,128)(2,1)S(1)} %collective-permute-done.xlow_ref, bf16[112,128]{1,0:T(8,128)(2,1)S(1)} %collective-permute-done.1.xhigh_ref, ...), custom_call_target="tpu_custom_call" | custom-call | flops 1000000 | bytes 1000000 | tf_op jit(solution)/shard_map/pallas_call | solution.py:84
  34.2 4.3 %all-to-all-done = bf16[32,8,128]{2,1,0:T(8,128)(2,1)S(1)} async-done(((bf16[32,8,128]{2,1,0:T(8,128)(2,1)}), bf16[32,8,128]{2,1,0:T(8,128)(2,1)S(1)}, u32[]{:S(2)}, u32[]{:S(2)}) %all-to-all-start) | async-done | bytes 65568 | tf_op jit(solution)/shard_map/all_to_all | solution.py:631
  39.1 3.2 %collective-permute-start.7 = (bf16[64,128]{1,0:T(8,128)(2,1)S(1)}, bf16[64,128]{1,0:T(8,128)(2,1)S(1)}, u32[]{:S(2)}, u32[]{:S(2)}) collective-permute-start(bf16[64,128]{1,0:T(8,128)(2,1)S(1)} %get-tuple-element.47), channel_id=1, source_target_pairs={{32,0},{64,32},{96,64},{128,96},{160,128},{192,160},{224,192},{0,2... | collective-permute-start | bytes 49160 | tf_op jit(solution)/shard_map/ppermute | solution.py:545
  42.3 3.2 %collective-permute-start.9 = (bf16[64,128]{1,0:T(8,128)(2,1)S(1)}, bf16[64,128]{1,0:T(8,128)(2,1)S(1)}, u32[]{:S(2)}, u32[]{:S(2)}) collective-permute-start(bf16[64,128]{1,0:T(8,128)(2,1)S(1)} %get-tuple-element.49), channel_id=1, source_target_pairs={{8,0},{16,8},{24,16},{0,24},{9,1},{17,9},{25,17},{1,25},{10,2},{18... | collective-permute-start | bytes 49160 | tf_op jit(solution)/shard_map/ppermute | solution.py:545
  45.6 1.9 %collective-permute-start.10 = (bf16[64,128]{1,0:T(8,128)(2,1)S(1)}, bf16[64,128]{1,0:T(8,128)(2,1)S(1)}, u32[]{:S(2)}, u32[]{:S(2)}) collective-permute-start(bf16[64,128]{1,0:T(8,128)(2,1)S(1)} %get-tuple-element.50), channel_id=1, source_target_pairs={{0,1},{1,2},{2,3},{3,4},{4,5},{5,6},{6,7},{7,0},{8,9},{9,10},{10,1... | collective-permute-start | bytes 49160 | tf_op jit(solution)/shard_map/ppermute | solution.py:545
  47.6 0.6 %shard_map.93.base_ref = f32[512,128]{1,0:T(8,128)S(1)} custom-call(f32[512,128]{1,0:T(8,128)S(1)} %get-tuple-element.43.state_ref, f32[512,128]{1,0:T(8,128)S(1)} %get-tuple-element.44.extra_ref, f32[64,128]{1,0:T(8,128)S(1)} %copy-done.4), custom_call_target="tpu_custom_call" | custom-call | flops 1000000 | bytes 1000000 | tf_op jit(solution)/shard_map/pallas_call | solution.py:84
  48.2 1.1 %collective-permute-done.10.zl_ref = bf16[64,128]{1,0:T(8,128)(2,1)S(1)} collective-permute-done((bf16[64,128]{1,0:T(8,128)(2,1)S(1)}, bf16[64,128]{1,0:T(8,128)(2,1)S(1)}, u32[]{:S(2)}, u32[]{:S(2)}) %collective-permute-start.10) | collective-permute-done | bytes 16416 | tf_op jit(solution)/shard_map/ppermute | solution.py:545
  49.3 4.0 %collective-permute-done.11.zh_ref = bf16[64,128]{1,0:T(8,128)(2,1)S(1)} collective-permute-done((bf16[64,128]{1,0:T(8,128)(2,1)S(1)}, bf16[64,128]{1,0:T(8,128)(2,1)S(1)}, u32[]{:S(2)}, u32[]{:S(2)}) %collective-permute-start.11) | collective-permute-done | bytes 16416 | tf_op jit(solution)/shard_map/ppermute | solution.py:545
  53.3 1.3 %shard_map.94 = f32[32,4,512]{2,1,0:T(4,128)} custom-call(f32[512,128]{1,0:T(8,128)S(1)} %shard_map.93.base_ref, f32[512,128]{1,0:T(8,128)S(1)} %get-tuple-element.43.state_ref, bf16[128,128]{1,0:T(8,128)(2,1)S(1)} %get-tuple-element.45.back_ref, bf16[64,128]{1,0:T(8,128)(2,1)S(1)} %collective-permute-done.6.xl_ref, ...), custom_call_target="tpu_custom_call" | custom-call | flops 1000000 | bytes 1000000 | tf_op jit(solution)/shard_map/pallas_call | solution.py:84
  (47 shorter events, 3.3 us)
Async XLA Ops:
  0.6 0.7 %copy-start.6 = (s32[1,32]{1,0:T(1,128)S(1)}, s32[1,32]{1,0:T(1,128)}, u32[]{:S(2)}) copy-start(s32[1,32]{1,0:T(1,128)} %cell_ref.3) | copy-start | bytes 388
  1.3 0.9 %copy-start = (f32[3,16,8,128]{3,2,1,0:T(8,128)S(1)}, f32[3,16,8,128]{3,2,1,0:T(8,128)}, u32[]{:S(2)}) copy-start(f32[3,16,8,128]{3,2,1,0:T(8,128)} %param.7) | copy-start | bytes 589828
  2.2 0.9 %copy-start.2 = (f32[32,4,512]{2,1,0:T(4,128)S(1)}, f32[32,4,512]{2,1,0:T(4,128)}, u32[]{:S(2)}) copy-start(f32[32,4,512]{2,1,0:T(4,128)} %acoustic_ref.3) | copy-start | bytes 786436
  3.2 6.4 %copy-start.7 = (s32[32,1]{0,1:T(1,128)S(1)}, s32[32,1]{0,1:T(1,128)}, u32[]{:S(2)}) copy-start(s32[32,1]{0,1:T(1,128)} %param.10) | copy-start | bytes 388
  3.2 6.7 %copy-start.8 = (s32[1,64]{1,0:T(1,128)S(1)}, s32[1,64]{1,0:T(1,128)}, u32[]{:S(2)}) copy-start(s32[1,64]{1,0:T(1,128)} %param.11) | copy-start | bytes 772
  3.2 7.4 %copy-start.3 = (f32[32,4,512]{2,1,0:T(4,128)S(1)}, f32[32,4,512]{2,1,0:T(4,128)}, u32[]{:S(2)}) copy-start(f32[32,4,512]{2,1,0:T(4,128)} %acoustic_ref.3) | copy-start | bytes 786436
  3.5 7.1 %copy-start.5 = (f32[64,512]{1,0:T(8,128)S(1)}, f32[64,512]{1,0:T(8,128)}, u32[]{:S(2)}) copy-start(f32[64,512]{1,0:T(8,128)} %projection_ref.1) | copy-start | bytes 393220
  3.5 7.8 %collective-permute-start = (bf16[112,128]{1,0:T(8,128)(2,1)S(1)}, bf16[112,128]{1,0:T(8,128)(2,1)S(1)}, u32[]{:S(2)}, u32[]{:S(2)}) collective-permute-start(bf16[112,128]{1,0:T(8,128)(2,1)S(1)} %get-tuple-element.27), channel_id=1, source_target_pairs={{0,32},{32,64},{64,96},{96,128},{128,160},{160,192},{192,224},{224... | collective-permute-start | bytes 86024 | tf_op jit(solution)/shard_map/ppermute | solution.py:545
  5.5 5.8 %collective-permute-start.1 = (bf16[112,128]{1,0:T(8,128)(2,1)S(1)}, bf16[112,128]{1,0:T(8,128)(2,1)S(1)}, u32[]{:S(2)}, u32[]{:S(2)}) collective-permute-start(bf16[112,128]{1,0:T(8,128)(2,1)S(1)} %get-tuple-element.28), channel_id=1, source_target_pairs={{32,0},{64,32},{96,64},{128,96},{160,128},{192,160},{224,192},{0,2... | collective-permute-start | bytes 86024 | tf_op jit(solution)/shard_map/ppermute | solution.py:545
  10.6 0.9 %copy-start.1 = (f32[3,16,8,128]{3,2,1,0:T(8,128)S(1)}, f32[3,16,8,128]{3,2,1,0:T(8,128)}, u32[]{:S(2)}) copy-start(f32[3,16,8,128]{3,2,1,0:T(8,128)} %param.7) | copy-start | bytes 589828
  11.6 5.1 %collective-permute-start.2 = (bf16[208,128]{1,0:T(8,128)(2,1)S(1)}, bf16[208,128]{1,0:T(8,128)(2,1)S(1)}, u32[]{:S(2)}, u32[]{:S(2)}) collective-permute-start(bf16[208,128]{1,0:T(8,128)(2,1)S(1)} %get-tuple-element.31), channel_id=1, source_target_pairs={{0,8},{8,16},{16,24},{24,0},{1,9},{9,17},{17,25},{25,1},{2,10},{10... | collective-permute-start | bytes 159752 | tf_op jit(solution)/shard_map/ppermute | solution.py:545
  11.7 5.1 %collective-permute-start.3 = (bf16[208,128]{1,0:T(8,128)(2,1)S(1)}, bf16[208,128]{1,0:T(8,128)(2,1)S(1)}, u32[]{:S(2)}, u32[]{:S(2)}) collective-permute-start(bf16[208,128]{1,0:T(8,128)(2,1)S(1)} %get-tuple-element.32), channel_id=1, source_target_pairs={{8,0},{16,8},{24,16},{0,24},{9,1},{17,9},{25,17},{1,25},{10,2},{18... | collective-permute-start | bytes 159752 | tf_op jit(solution)/shard_map/ppermute | solution.py:545
  17.0 3.9 %collective-permute-start.4 = (bf16[96,128]{1,0:T(8,128)(2,1)S(1)}, bf16[96,128]{1,0:T(8,128)(2,1)S(1)}, u32[]{:S(2)}, u32[]{:S(2)}) collective-permute-start(bf16[96,128]{1,0:T(8,128)(2,1)S(1)} %get-tuple-element.37), channel_id=1, source_target_pairs={{0,1},{1,2},{2,3},{3,4},{4,5},{5,6},{6,7},{7,0},{8,9},{9,10},{10,1... | collective-permute-start | bytes 73736 | tf_op jit(solution)/shard_map/ppermute | solution.py:545
  18.2 5.9 %collective-permute-start.5 = (bf16[96,128]{1,0:T(8,128)(2,1)S(1)}, bf16[96,128]{1,0:T(8,128)(2,1)S(1)}, u32[]{:S(2)}, u32[]{:S(2)}) collective-permute-start(bf16[96,128]{1,0:T(8,128)(2,1)S(1)} %get-tuple-element.38), channel_id=1, source_target_pairs={{1,0},{2,1},{3,2},{4,3},{5,4},{6,5},{7,6},{0,7},{9,8},{10,9},{11,1... | collective-permute-start | bytes 73736 | tf_op jit(solution)/shard_map/ppermute | solution.py:545
  25.9 12.6 %all-to-all-start = ((bf16[32,8,128]{2,1,0:T(8,128)(2,1)}), bf16[32,8,128]{2,1,0:T(8,128)(2,1)S(1)}, u32[]{:S(2)}, u32[]{:S(2)}) async-start(bf16[32,8,128]{2,1,0:T(8,128)(2,1)} %bitcast.3), calls=%async_computation | async-start | bytes 131072 | tf_op jit(solution)/shard_map/all_to_all | solution.py:631
  32.8 0.8 %copy-start.4 = (f32[64,128]{1,0:T(8,128)S(1)}, f32[64,128]{1,0:T(8,128)}, u32[]{:S(2)}) copy-start(f32[64,128]{1,0:T(8,128)} %constant.106.clone.column_ref) | copy-start | bytes 98308
  39.0 8.5 %collective-permute-start.6 = (bf16[64,128]{1,0:T(8,128)(2,1)S(1)}, bf16[64,128]{1,0:T(8,128)(2,1)S(1)}, u32[]{:S(2)}, u32[]{:S(2)}) collective-permute-start(bf16[64,128]{1,0:T(8,128)(2,1)S(1)} %get-tuple-element.46), channel_id=1, source_target_pairs={{0,32},{32,64},{64,96},{96,128},{128,160},{160,192},{192,224},{224... | collective-permute-start | bytes 49160 | tf_op jit(solution)/shard_map/ppermute | solution.py:545
  39.1 9.1 %collective-permute-start.7 = (bf16[64,128]{1,0:T(8,128)(2,1)S(1)}, bf16[64,128]{1,0:T(8,128)(2,1)S(1)}, u32[]{:S(2)}, u32[]{:S(2)}) collective-permute-start(bf16[64,128]{1,0:T(8,128)(2,1)S(1)} %get-tuple-element.47), channel_id=1, source_target_pairs={{32,0},{64,32},{96,64},{128,96},{160,128},{192,160},{224,192},{0,2... | collective-permute-start | bytes 49160 | tf_op jit(solution)/shard_map/ppermute | solution.py:545
  42.3 5.9 %collective-permute-start.8 = (bf16[64,128]{1,0:T(8,128)(2,1)S(1)}, bf16[64,128]{1,0:T(8,128)(2,1)S(1)}, u32[]{:S(2)}, u32[]{:S(2)}) collective-permute-start(bf16[64,128]{1,0:T(8,128)(2,1)S(1)} %get-tuple-element.48), channel_id=1, source_target_pairs={{0,8},{8,16},{16,24},{24,0},{1,9},{9,17},{17,25},{25,1},{2,10},{10... | collective-permute-start | bytes 49160 | tf_op jit(solution)/shard_map/ppermute | solution.py:545
  42.3 5.9 %collective-permute-start.9 = (bf16[64,128]{1,0:T(8,128)(2,1)S(1)}, bf16[64,128]{1,0:T(8,128)(2,1)S(1)}, u32[]{:S(2)}, u32[]{:S(2)}) collective-permute-start(bf16[64,128]{1,0:T(8,128)(2,1)S(1)} %get-tuple-element.49), channel_id=1, source_target_pairs={{8,0},{16,8},{24,16},{0,24},{9,1},{17,9},{25,17},{1,25},{10,2},{18... | collective-permute-start | bytes 49160 | tf_op jit(solution)/shard_map/ppermute | solution.py:545
  45.6 3.7 %collective-permute-start.10 = (bf16[64,128]{1,0:T(8,128)(2,1)S(1)}, bf16[64,128]{1,0:T(8,128)(2,1)S(1)}, u32[]{:S(2)}, u32[]{:S(2)}) collective-permute-start(bf16[64,128]{1,0:T(8,128)(2,1)S(1)} %get-tuple-element.50), channel_id=1, source_target_pairs={{0,1},{1,2},{2,3},{3,4},{4,5},{5,6},{6,7},{7,0},{8,9},{9,10},{10,1... | collective-permute-start | bytes 49160 | tf_op jit(solution)/shard_map/ppermute | solution.py:545
  47.5 5.8 %collective-permute-start.11 = (bf16[64,128]{1,0:T(8,128)(2,1)S(1)}, bf16[64,128]{1,0:T(8,128)(2,1)S(1)}, u32[]{:S(2)}, u32[]{:S(2)}) collective-permute-start(bf16[64,128]{1,0:T(8,128)(2,1)S(1)} %get-tuple-element.51), channel_id=1, source_target_pairs={{1,0},{2,1},{3,2},{4,3},{5,4},{6,5},{7,6},{0,7},{9,8},{10,9},{11,1... | collective-permute-start | bytes 49160 | tf_op jit(solution)/shard_map/ppermute | solution.py:545
where the time goes:
time: 54.9 us; the launch traced here: 54.6 us
  starting transfers between devices  26.9 us (49%)
  waiting for transfers between devices  16.1 us (29%)
  Pallas kernels  5.91 us (11%)
  local copies, waits for them, and re-layouts  3.73 us (7%)
  other arithmetic  1.12 us (2%)
  between operations  0.87 us (2%)
    ppermute x12, starting transfers between devices, both_ways(): return (lax.ppermute(high, axis, up), lax.ppermute(low, axis, down))  20 us
    ppermute x12, waiting for transfers between devices, both_ways(): return (lax.ppermute(high, axis, up), lax.ppermute(low, axis, down))  11.8 us
    all_to_all x1, starting transfers between devices, on_device(): lax.all_to_all(volumes.reshape(32, 8, LANES), ('gy', 'gz'), split_axis=0,...  6.83 us
    pallas_call x9, Pallas kernels, call(): pl.pallas_call(kernel, out_shape=out_shape, in_specs=[pl.BlockSpec(memory...  5.91 us
    all_to_all x1, waiting for transfers between devices, on_device(): lax.all_to_all(volumes.reshape(32, 8, LANES), ('gy', 'gz'), split_axis=0,...  4.32 us
    unnamed x18, local copies, waits for them, and re-layouts  3.32 us
  transfers between devices with their start and end apart: 13, of which 7 were waited for; matrix products, arithmetic and copies ran while one was open for 3% of the time, Pallas kernels for 3%

commit v1 on v0

v1 whole, which is shorter than its diff:
```python
import jax
import jax.numpy as jnp
import numpy as np
from jax import lax
from jax.experimental import pallas as pl
from jax.experimental.pallas import tpu as pltpu
from jax.sharding import PartitionSpec as P

F32 = jnp.float32
BF = jnp.bfloat16
ORDER = 7
K = ORDER + 1
LANES = 128
ROWS = K**3
FACE = K * K
FLOW_STEP = 0.1
VISCOSITY = 0.05
WAVE_STEP = 0.02
SOURCE_GAIN = 25.0
GAIN = WAVE_STEP * SOURCE_GAIN
LIFT = WAVE_STEP * 0.5 * ORDER * (ORDER + 1) / 2.0
XV = 48
YV = 144
ZV = 32


def legendre_table(points, order):
    columns = [points * 0.0 + 1.0, points]
    for degree in range(2, order + 1):
        columns.append(
            ((2 * degree - 1) * points * columns[degree - 1] - (degree - 1) * columns[degree - 2])
            / degree
        )
    return np.stack(columns, axis=1)


def lobatto_tables(order):
    point_count = order + 1
    points = -np.cos(np.pi * np.arange(point_count) / order)
    for _ in range(60):
        legendre = legendre_table(points, order)
        points = points - (points * legendre[:, order] - legendre[:, order - 1]) / (
            point_count * legendre[:, order]
        )
    legendre = legendre_table(points, order)
    highest = legendre[:, order]
    spacing = points[:, None] - points[None, :] + np.eye(point_count)
    derivative = highest[:, None] / (highest[None, :] * spacing)
    derivative = derivative * (1.0 - np.eye(point_count))
    derivative[0, 0] = -order * point_count / 4.0
    derivative[order, order] = order * point_count / 4.0
    return derivative


DERIV = lobatto_tables(ORDER) * (-WAVE_STEP)


def split2(value):
    high = value.astype(BF)
    return high, (value - high.astype(F32)).astype(BF)


def nn(a, b):
    return lax.dot_general(a, b, (((1,), (0,)), ((), ())), preferred_element_type=F32)


def nt(a, b):
    return lax.dot_general(a, b, (((1,), (1,)), ((), ())), preferred_element_type=F32)


def tn(a, b):
    return lax.dot_general(a, b, (((0,), (0,)), ((), ())), preferred_element_type=F32)


def iota(shape, axis):
    return lax.broadcasted_iota(jnp.int32, shape, axis)


def roll(value, shift, axis):
    size = value.shape[axis]
    return pltpu.roll(value, shift % size, axis)


def call(
    kernel, out_shape, *args, scratch=(), far_in=(), far_out=(), alias={}, flops=10**6, moved=10**6
):
    near, far = pl.BlockSpec(memory_space=pltpu.VMEM), pl.BlockSpec(memory_space=pl.ANY)
    outs = [far if i in far_out else near for i in range(len(jax.tree.leaves(out_shape)))]
    return pl.pallas_call(
        kernel,
        out_shape=out_shape,
        in_specs=[far if i in far_in else near for i in range(len(args))],
        out_specs=tuple(outs) if isinstance(out_shape, tuple) else outs[0],
        scratch_shapes=list(scratch),
        input_output_aliases=alias,
        compiler_params=pltpu.CompilerParams(vmem_limit_bytes=16 * 2**20),
        cost_estimate=pl.CostEstimate(flops=flops, bytes_accessed=moved, transcendentals=0),
    )(*args)


def shape(*dims, dtype=F32):
    return jax.ShapeDtypeStruct(dims, dtype)


def stored_rows(acoustic_ref):
    return jnp.concatenate([acoustic_ref[:, v, :] for v in range(4)], axis=0)


def cell_matrix(cell_ref):
    cell = jnp.concatenate([cell_ref[...]] * 4, axis=1)
    cell = jnp.broadcast_to(cell, (LANES, LANES))
    row, column = iota((LANES, LANES), 0), iota((LANES, LANES), 1)
    return (cell == row % 32) & (row // 32 == column // 32)


def swapped(value, axis):
    kind = iota(value.shape, value.ndim - 1) // 32
    shift = 32 * (1 + axis)
    last = value.ndim - 1
    return jnp.where(
        kind == 0,
        roll(value, -shift, last),
        jnp.where(kind == 1 + axis, roll(value, shift, last), 0.0),
    )


def low_lift(axis, jump):
    return -LIFT * (swapped(jump, axis) + jump)


def high_lift(axis, jump):
    return LIFT * (swapped(jump, axis) - jump)


def cut_of(axis, dims):
    lane = iota(dims, 1)
    if axis == 1:
        part = (lane // 16) % 2
        return part == 0, part == 1
    part = lane % 16
    return part == 0, part == 15


def outer(axis, own_low, own_high, near):
    at_low, at_high = cut_of(axis, own_low.shape)
    low = jnp.where(at_high, near, own_high)
    high = jnp.where(at_low, near, own_low)
    wrap = 16 if axis == 1 else 15
    step = 16 if axis == 1 else 1
    return (
        jnp.where(at_low, roll(low, -wrap, 1), roll(low, step, 1)),
        jnp.where(at_high, roll(high, wrap, 1), roll(high, -step, 1)),
    )


def facing(axis, own_low, own_high):
    at_low, at_high = cut_of(axis, own_low.shape)
    wrap = 16 if axis == 1 else 15
    return jnp.where(at_high, roll(own_low, wrap, 1), roll(own_high, -wrap, 1))


def near_lift(axis, near, own_low, own_high):
    _, at_high = cut_of(axis, near.shape)
    jump = near - facing(axis, own_low, own_high)
    return jnp.where(at_high, high_lift(axis, jump), low_lift(axis, jump))


def inside_lifts(axis, own_low, own_high):
    at_low, at_high = cut_of(axis, own_low.shape)
    low, high = outer(axis, own_low, own_high, own_low)
    low = jnp.where(at_low, 0.0, own_low - low)
    high = jnp.where(at_high, 0.0, own_high - high)
    return low_lift(axis, low), high_lift(axis, high)


def boundary_lifts(axis, own_low, own_high, near):
    at_low, at_high = cut_of(axis, own_low.shape)
    low, high = outer(axis, own_low, own_high, near)
    low = jnp.where(at_low, own_low - low, 0.0)
    high = jnp.where(at_high, own_high - high, 0.0)
    return low_lift(axis, low), high_lift(axis, high)


def face_pair(ref, axis):
    if axis == 0:
        return ref[0:FACE, :], ref[ROWS - FACE : ROWS, :]
    if axis == 1:
        low = [ref[a * FACE : a * FACE + K, :] for a in range(K)]
        high = [ref[a * FACE + FACE - K : a * FACE + FACE, :] for a in range(K)]
        return jnp.concatenate(low, axis=0), jnp.concatenate(high, axis=0)
    return ref[pl.ds(0, FACE, stride=K), :], ref[pl.ds(K - 1, FACE, stride=K), :]


def add_pair(ref, axis, low, high):
    if axis == 0:
        ref[0:FACE, :] += low
        ref[ROWS - FACE : ROWS, :] += high
    elif axis == 1:
        for a in range(K):
            ref[a * FACE : a * FACE + K, :] += low[a * K : a * K + K]
            ref[a * FACE + FACE - K : a * FACE + FACE, :] += high[a * K : a * K + K]
    else:
        ref[pl.ds(0, FACE, stride=K), :] += low
        ref[pl.ds(K - 1, FACE, stride=K), :] += high


def volume_part(state_ref, out_ref, column_ref, extra_ref=None):
    for a in range(K):
        rows = [state_ref[a * FACE + b * K : a * FACE + b * K + K, :] for b in range(K)]
        along_y = [swapped(r, 1) for r in rows]
        along_z = [swapped(r, 2) for r in rows]
        for b in range(K):
            total = rows[b]
            at = a * FACE + b * K
            if extra_ref is not None:
                total = total - extra_ref[at : at + K, :]
            for m in range(K):
                total = total + float(DERIV[b, m]) * along_y[m]
            for m in range(K):
                total = total + column_ref[m * K : m * K + K, :] * jnp.broadcast_to(
                    along_z[b][m : m + 1, :], (K, LANES)
                )
            out_ref[at : at + K, :] = total
    for b in range(K):
        rows = [
            swapped(state_ref[a * FACE + b * K : a * FACE + b * K + K, :], 0) for a in range(K)
        ]
        for a in range(K):
            at = a * FACE + b * K
            total = out_ref[at : at + K, :]
            for m in range(K):
                total = total + float(DERIV[a, m]) * rows[m]
            out_ref[at : at + K, :] = total


def start_kernel(velocity_ref, acoustic_ref, cell_ref, low_ref, high_ref, flow, wave, sems):
    copies = []
    for side, tile in ((0, 0), (1, 3)):
        copies.append((acoustic_ref.at[:, :, tile * LANES : tile * LANES + LANES], wave.at[side]))
    for side, first in ((0, 0), (1, 112)):
        copies.append((velocity_ref.at[:, first : first + 16, :], flow.at[side]))
    copies = [pltpu.make_async_copy(a, b, sems.at[i]) for i, (a, b) in enumerate(copies)]
    for copy in copies:
        copy.start()
    place = jnp.where(cell_matrix(cell_ref), 1.0, 0.0).astype(BF)
    for copy in copies:
        copy.wait()
    faces = jnp.concatenate(
        [
            jnp.where(iota((32, LANES), 1) < FACE, wave[0, :, v, :], wave[1, :, v, :])
            for v in range(4)
        ],
        axis=0,
    )
    turned = jnp.transpose(nn(place, faces.astype(BF))).astype(BF)
    low_ref[XV:, :] = turned[:FACE]
    high_ref[XV:, :] = turned[FACE:]
    for c in range(3):
        low_ref[c * 16 : c * 16 + 16, :] = flow[0, c].astype(BF)
        high_ref[c * 16 : c * 16 + 16, :] = flow[1, c].astype(BF)


def prepare_kernel(
    acoustic_ref,
    cell_ref,
    projection_ref,
    column_ref,
    state_ref,
    base_ref,
    back_ref,
    table_ref,
    faces_ref,
    scratch,
):
    chosen = jnp.where(cell_matrix(cell_ref), 1.0, 0.0)
    place = chosen.astype(BF)
    back_ref[...] = jnp.transpose(chosen).astype(BF)
    high, low = split2(stored_rows(acoustic_ref))
    state_ref[...] = jnp.transpose(nn(place, high) + nn(place, low))
    high, low = split2(projection_ref[...])
    row, column = iota((64, 64), 0), iota((64, 64), 1)
    order = jnp.where(column == (row % 16) * 4 + row // 16, 1.0, 0.0).astype(BF)
    high, low = nn(order, high), nn(order, low)
    whole = jnp.concatenate([high, low, high, jnp.zeros((64, ROWS), F32)], axis=0)
    scratch[0] = jnp.transpose(whole[0:LANES])
    scratch[1] = jnp.transpose(whole[LANES:])
    for i in range(2):
        lane = slice(i * LANES, i * LANES + LANES)
        table_ref[:, lane] = scratch[i].astype(BF)
        for axis in range(3):
            for side, face in enumerate(face_pair(scratch.at[i], axis)):
                faces_ref[2 * axis + side, :, lane] = face.astype(BF)
    volume_part(state_ref, base_ref, column_ref)
    for axis in (1, 2):
        add_pair(base_ref, axis, *inside_lifts(axis, *face_pair(state_ref, axis)))


def y_kernel(
    velocity_ref,
    xlow_ref,
    xhigh_ref,
    state_ref,
    base_ref,
    targets_ref,
    low_ref,
    high_ref,
    out_ref,
    wide,
):
    for c in range(3):
        wide[c, 0:16, :] = xlow_ref[c * 16 : c * 16 + 16, :].astype(F32)
        wide[c, 16:144, :] = velocity_ref[c]
        wide[c, 144:160, :] = xhigh_ref[c * 16 : c * 16 + 16, :].astype(F32)
    own_low, own_high = face_pair(state_ref, 0)
    out_ref[...] = base_ref[...]
    add_pair(
        out_ref,
        0,
        low_lift(0, own_low - xlow_ref[XV:, :].astype(F32)),
        high_lift(0, own_high - xhigh_ref[XV:, :].astype(F32)),
    )
    traces, bases = face_pair(state_ref, 1), face_pair(out_ref, 1)
    spare = jnp.concatenate([targets_ref[...], jnp.zeros((3, LANES), F32)], axis=0)
    for side, (out, first) in enumerate(((low_ref, 0), (high_ref, 6))):
        pieces = []
        for y in range(2):
            for c in range(3):
                pieces.append(wide[c, pl.ds(first + y, 20, stride=8), :])
                pieces.append(spare)
        out[0:YV, :] = jnp.concatenate(pieces, axis=0).astype(BF)
        out[YV : YV + FACE, :] = traces[side].astype(BF)
        out[YV + FACE :, :] = bases[side].astype(BF)


def joined(axis, low, high):
    _, at_high = cut_of(axis, low.shape)
    return jnp.where(at_high, low.astype(F32), high.astype(F32))


def z_kernel(
    velocity_ref,
    xlow_ref,
    xhigh_ref,
    ylow_ref,
    yhigh_ref,
    state_ref,
    base_ref,
    targets_ref,
    wide_ref,
    own_ref,
    low_ref,
    high_ref,
    out_ref,
    near_ref,
    held,
):
    held[0] = ylow_ref[0:YV, :].astype(F32)
    held[1] = yhigh_ref[0:YV, :].astype(F32)
    for c in range(3):
        low = xlow_ref[c * 16 : c * 16 + 16, :].astype(F32)
        high = xhigh_ref[c * 16 : c * 16 + 16, :].astype(F32)
        for x in range(2):
            wide_ref[c, x, 2:10, :] = low[x * 8 : x * 8 + 8]
            wide_ref[c, 18 + x, 2:10, :] = high[x * 8 : x * 8 + 8]
        for x in range(16):
            wide_ref[c, 2 + x, 2:10, :] = velocity_ref[c, x * 8 : x * 8 + 8, :]
        for y in range(2):
            for side in range(2):
                rows = held[side, y * 72 + c * 24 : y * 72 + c * 24 + 20, :]
                wide_ref[c, :, y + 10 * side, :] = rows
        wide_ref[c, :, 12:16, :] = jnp.zeros((20, 4, LANES), F32)
    row, column = iota((16, LANES), 0), iota((16, LANES), 1)
    picks = ((row < 2) & (column == row)) | ((row >= 2) & (row < 4) & (column == row + 124))
    picks = jnp.where(picks, 1.0, 0.0).astype(BF)
    for c in range(3):
        rows = wide_ref[c].reshape(320, LANES).astype(BF)
        own = nt(picks, rows)
        own_ref[c, :, 0:320] = own[0:8]
        own_ref[c, :, 320:384] = jnp.zeros((8, 64), F32)
    near_ref[0:FACE, :] = joined(1, ylow_ref[YV : YV + FACE, :], yhigh_ref[YV : YV + FACE, :])
    near_ref[FACE:, :] = joined(1, ylow_ref[YV + FACE :, :], yhigh_ref[YV + FACE :, :])
    out_ref[...] = base_ref[...]
    add_pair(out_ref, 1, *boundary_lifts(1, *face_pair(state_ref, 1), near_ref[0:FACE, :]))
    traces, bases = face_pair(state_ref, 2), face_pair(out_ref, 2)
    for side, (out, first) in enumerate(((low_ref, 0), (high_ref, 2))):
        pieces = []
        for c in range(3):
            for j in range(3):
                pieces.append(own_ref[c, first : first + 2, j * 128 : j * 128 + 128])
        pieces += [targets_ref[...], jnp.zeros((5, LANES), F32)]
        pieces.append(near_ref[pl.ds(side * (K - 1), K, stride=K), :])
        out[0:ZV, :] = jnp.concatenate(pieces, axis=0).astype(BF)
        out[ZV : ZV + FACE, :] = traces[side].astype(BF)
        out[ZV + FACE :, :] = bases[side].astype(BF)


def differences(low, high):
    return [[high[a][c] - low[a][c] for c in range(3)] for a in range(3)]


def moved_on(centre, low, high, diff):
    scaled = [(-0.5 * FLOW_STEP) * centre[a] for a in range(3)]
    out = []
    for c in range(3):
        spread = (low[0][c] + high[0][c]) + (low[1][c] + high[1][c]) + (low[2][c] + high[2][c])
        carried = scaled[0] * diff[0][c] + scaled[1] * diff[1][c] + scaled[2] * diff[2][c]
        out.append(
            (1.0 - 6.0 * FLOW_STEP * VISCOSITY) * centre[c]
            + (FLOW_STEP * VISCOSITY) * spread
            + carried
        )
    return out


def lamb(centre, diff):
    w = [diff[1][2] - diff[2][1], diff[2][0] - diff[0][2], diff[0][1] - diff[1][0]]
    return [
        w[1] * centre[2] - w[2] * centre[1],
        w[2] * centre[0] - w[0] * centre[2],
        w[0] * centre[1] - w[1] * centre[0],
    ]


def flow_kernel(
    wide_ref,
    own_ref,
    zlow_ref,
    zhigh_ref,
    place_ref,
    out_ref,
    volume_ref,
    ends,
    halo,
    middle,
    sums,
):
    low = zlow_ref[0:ZV, :].astype(F32)
    high = zhigh_ref[0:ZV, :].astype(F32)
    for c in range(3):
        for j in range(3):
            lane = slice(j * 128, j * 128 + 128)
            at = 2 * (3 * c + j)
            ends[c, 0:2, lane] = low[at : at + 2]
            ends[c, 2:6, lane] = own_ref[c, 0:4, lane]
            ends[c, 6:8, lane] = high[at : at + 2]
    row, column = iota((16, LANES), 0), iota((16, LANES), 1)
    spots = ((row == 1) & (column == 0)) | ((row == 6) & (column == 127))
    spots = jnp.where(spots, 1.0, 0.0).astype(BF)
    zeros = jnp.zeros((8, 384), F32)

    def spread_out(values, level):
        for c in range(3):
            both = jnp.concatenate([values[c], zeros], axis=0).astype(BF)
            halo[level, c] = tn(both, spots)[0:320].reshape(20, 16, LANES)

    edge = [ends[c] for c in range(3)]
    spread_out(edge, 0)
    edge_low = [
        [roll(e, 16, 1) for e in edge],
        [roll(e, 1, 1) for e in edge],
        [roll(e, 1, 0) for e in edge],
    ]
    edge_high = [
        [roll(e, -16, 1) for e in edge],
        [roll(e, -1, 1) for e in edge],
        [roll(e, -1, 0) for e in edge],
    ]
    spread_out(
        moved_on(edge, edge_low, edge_high, differences(edge_low, edge_high)), 1
    )

    def along_z(values, edges):
        lane = iota(values[0].shape, values[0].ndim - 1)
        axis = values[0].ndim - 1
        low = [jnp.where(lane == 0, h, roll(v, 1, axis)) for v, h in zip(values, edges)]
        high = [jnp.where(lane == 127, h, roll(v, -1, axis)) for v, h in zip(values, edges)]
        return low, high

    def plane(source, x, level, y):
        centre = [source[c, x, y, :] for c in range(3)]
        zlow, zhigh = along_z(centre, [halo[level, c, x, y, :] for c in range(3)])
        up = slice(y.start + 1, y.stop + 1)
        down = slice(y.start - 1, y.stop - 1)
        low = [
            [source[c, x - 1, y, :] for c in range(3)],
            [source[c, x, down, :] for c in range(3)],
            zlow,
        ]
        high = [
            [source[c, x + 1, y, :] for c in range(3)],
            [source[c, x, up, :] for c in range(3)],
            zhigh,
        ]
        return centre, low, high

    inner = slice(2, 10)
    for y in (1, 10):
        def line(source, first, at):
            return [source[c, first : first + 16, at, :] for c in range(3)]

        centre = line(wide_ref, 2, y)
        zlow, zhigh = along_z(
            centre, [halo[0, c, 2:18, y, :] for c in range(3)]
        )
        low = [line(wide_ref, 1, y), line(wide_ref, 2, y - 1), zlow]
        high = [line(wide_ref, 3, y), line(wide_ref, 2, y + 1), zhigh]
        new = moved_on(centre, low, high, differences(low, high))
        for c in range(3):
            middle[c, 2:18, y, :] = new[c]

    def add_lamb(parts, x, step):
        i, a = (x // 2) // 4, (x // 2) % 4
        for c in range(3):
            at = ((step * 3 + c) * 4 + a) * 8
            sums[i, at : at + 8, :] = parts[c]

    held = None
    for x in range(1, 19):
        centre, low, high = plane(wide_ref, x, 0, inner)
        diff = differences(low, high)
        new = moved_on(centre, low, high, diff)
        for c in range(3):
            middle[c, x, inner, :] = new[c]
        if 2 <= x < 18:
            parts = lamb(centre, diff)
            if x % 2 == 0:
                held = parts
            else:
                add_lamb([p + h for p, h in zip(parts, held)], x - 2, 0)
    for x in range(2, 18):
        centre, low, high = plane(middle, x, 1, inner)
        diff = differences(low, high)
        new = moved_on(centre, low, high, diff)
        for c in range(3):
            out_ref[c, (x - 2) * 8 : (x - 2) * 8 + 8, :] = new[c]
        parts = lamb(centre, diff)
        if x % 2 == 0:
            held = parts
        else:
            add_lamb([p + h for p, h in zip(parts, held)], x - 2, 1)
    both = []
    for i in range(2):
        both.append(sums[i, pl.ds(0, 96, stride=2), :] + sums[i, pl.ds(1, 96, stride=2), :])
    pairs = jnp.concatenate(both, axis=1)
    pairs = jnp.concatenate([pairs, jnp.zeros((32, 256), F32)], axis=0)
    high, low = split2(pairs)
    place = place_ref[...]
    volumes = (nt(place, high) + nt(place, low)) * (1.0 / 16.0)
    lane = iota((256, LANES), 1)
    twice = jnp.where(lane < 48, volumes, roll(volumes, 48, 1)).reshape(4, 8, 8, LANES)
    left = iota((8, 8, LANES), 2) < 48
    for y in range(4):
        part = slice(y * 8, y * 8 + 8)
        volume_ref[part, 0:8, :] = volumes[y * 64 : y * 64 + 64].reshape(8, 8, LANES).astype(BF)
        rows = jnp.where(left, twice[(y + 3) % 4], twice[(y + 1) % 4])
        volume_ref[part, 8:16, :] = rows.astype(BF)
        lower = jnp.concatenate([twice[y, 7:8], twice[y, 0:7]], axis=0)
        upper = jnp.concatenate([twice[y, 1:8], twice[y, 0:1]], axis=0)
        volume_ref[part, 16:24, :] = jnp.where(left, lower, upper).astype(BF)


def gather_matrix(targets, second=None, chosen=None):
    row, column = iota((256, LANES), 0), iota((256, LANES), 1)
    slots = jnp.where(column == (row // 8) * 2 + row % 2, 1.0, 0.0).astype(BF)

    def named(line):
        return nt(slots, jnp.broadcast_to(line, (LANES, LANES)).astype(BF))

    cells = named(targets)
    if second is not None:
        cells = jnp.where(chosen, cells, named(second))
    fits = cells == (column % 32).astype(F32)
    return [
        jnp.where(fits & ((row % 8) // 2 == z), 1.0, 0.0).astype(BF) for z in range(4)
    ]


def near_kernel(
    state_ref,
    base_ref,
    near_ref,
    targets_ref,
    ylow_ref,
    yhigh_ref,
    zlow_ref,
    zhigh_ref,
    out_ref,
    sides_ref,
    gather_ref,
):
    znear = joined(2, zlow_ref[ZV : ZV + FACE, :], zhigh_ref[ZV : ZV + FACE, :])
    own_y, own_z = face_pair(state_ref, 1), face_pair(state_ref, 2)
    out_ref[...] = base_ref[...]
    add_pair(out_ref, 2, *boundary_lifts(2, *own_z, znear))
    ynear = near_ref[0:FACE, :]
    sides_ref[0:FACE, :] = near_ref[FACE:, :] + near_lift(1, ynear, *own_y)
    zbase = joined(2, zlow_ref[ZV + FACE :, :], zhigh_ref[ZV + FACE :, :])
    sides_ref[FACE:, :] = zbase + near_lift(2, znear, *own_z)
    from_low = zlow_ref[0:ZV, :].astype(F32)[24:32]
    from_high = zhigh_ref[0:ZV, :].astype(F32)[24:32]
    at_low, at_high = cut_of(2, (K, LANES))
    jump = near_ref[pl.ds(0, K, stride=K), :] - roll(from_low, -15, 1)
    sides_ref[pl.ds(0, K, stride=K), :] += jnp.where(at_low, low_lift(2, jump), 0.0)
    jump = near_ref[pl.ds(K - 1, K, stride=K), :] - roll(from_high, 15, 1)
    sides_ref[pl.ds(K - 1, K, stride=K), :] += jnp.where(at_high, high_lift(2, jump), 0.0)

    def line(ref, at):
        return ref[0:32, :].astype(F32)[at : at + 1]

    groups = [
        gather_matrix(targets_ref[...]),
        gather_matrix(line(ylow_ref, 20), line(yhigh_ref, 20), cut_of(1, (256, LANES))[1]),
        gather_matrix(line(zlow_ref, 18), line(zhigh_ref, 18), cut_of(2, (256, LANES))[1]),
    ]
    for g, parts in enumerate(groups):
        for z in range(4):
            gather_ref[g, :, z * LANES : z * LANES + LANES] = parts[z]


def stacked(summed, starts):
    kind = iota((16, LANES), 1) // 32
    blocks = []
    for start in starts:
        rows = []
        for z in range(4):
            total = jnp.zeros((16, LANES), F32)
            for c in range(3):
                total = jnp.where(kind == 1 + c, start(summed, c, z), total)
            rows.append(total)
        blocks.append(jnp.concatenate(rows, axis=0))
    high, low = split2(jnp.concatenate(blocks, axis=1) if len(blocks) > 1 else blocks[0])
    return jnp.concatenate([high, high, low, jnp.zeros_like(low)], axis=0)


def at_rows(first):
    def pick(summed, c, z):
        at = first + c * 16
        return summed[at : at + 16, z * LANES : z * LANES + LANES]

    return pick


def by_side(axis):
    def pick(summed, c, z):
        _, at_high = cut_of(axis, (16, LANES))
        return jnp.where(at_high, at_rows(0)(summed, c, z), at_rows(48)(summed, c, z))

    return pick


def send_kernel(arrived_ref, gather_ref, faces_ref, base_ref, low_ref, high_ref, cells_ref):
    rows = arrived_ref[:, 0:8, :].reshape(256, LANES)
    summed = tn(rows, gather_ref[0])
    cells = stacked(summed, (at_rows(0), at_rows(48)))
    cells_ref[...] = cells
    for side, (out, face) in enumerate(zip((low_ref, high_ref), face_pair(base_ref, 0))):
        out[...] = (face - GAIN * nn(faces_ref[side], cells[:, 0:LANES])).astype(BF)


def second_kernel(
    arrived_ref,
    gather_ref,
    table_ref,
    faces_ref,
    cells_ref,
    base_ref,
    sides_ref,
    column_ref,
    back_ref,
    flow_ref,
    out_ref,
    ends_ref,
    flow_out_ref,
    state,
    extra,
    total,
    rows_held,
    sem,
):
    flow_out_ref[...] = flow_ref[...]
    source = GAIN * nn(table_ref[...], cells_ref[...])
    state[...] = base_ref[...] - source[:, 0:LANES]
    extra[...] = source[:, LANES:]
    near = []
    for axis in (1, 2):
        rows = arrived_ref[:, 8 * axis : 8 * axis + 8, :].reshape(256, LANES)
        cells = stacked(tn(rows, gather_ref[axis]), (by_side(axis),))
        at_low, at_high = cut_of(axis, (FACE, LANES))
        face = jnp.where(
            at_high,
            nn(faces_ref[2 * axis + 1], cells),
            nn(faces_ref[2 * axis], cells),
        )
        near.append(sides_ref[(axis - 1) * FACE : axis * FACE, :] - GAIN * face)
    volume_part(state, total, column_ref, extra)
    for axis in (1, 2):
        own_low, own_high = face_pair(state, axis)
        low, high = outer(axis, own_low, own_high, near[axis - 1])
        add_pair(total, axis, low_lift(axis, own_low - low), high_lift(axis, own_high - high))
    own_low, own_high = face_pair(state, 0)
    add_pair(total, 0, low_lift(0, own_low), high_lift(0, own_high))
    high, low = split2(jnp.transpose(total[...]))
    back = back_ref[...]
    rows = nn(back, high) + nn(back, low)
    ends_ref[0] = rows[:, 0:LANES]
    ends_ref[1] = rows[:, 3 * LANES :]
    for v in range(4):
        rows_held[:, v, :] = rows[v * 32 : v * 32 + 32, :]
    copy = pltpu.make_async_copy(rows_held, out_ref, sem)
    copy.start()
    copy.wait()


def last_kernel(
    main_ref, ends_ref, back_ref, low_ref, high_ref, out_ref, held, sems
):
    low, high = low_ref[...].astype(F32), high_ref[...].astype(F32)
    parts = jnp.concatenate([-low_lift(0, low), -high_lift(0, high)], axis=0)
    high, low = split2(jnp.transpose(parts))
    back = back_ref[...]
    rows = nn(back, high) + nn(back, low)
    left = iota((LANES, LANES), 1) < FACE
    copies = []
    for side, tile in ((0, 0), (1, 3)):
        total = ends_ref[side] + jnp.where(left if side == 0 else ~left, rows, 0.0)
        for v in range(4):
            held[side, :, v, :] = total[v * 32 : v * 32 + 32, :]
        copies.append(
            pltpu.make_async_copy(
                held.at[side],
                out_ref.at[:, :, tile * LANES : tile * LANES + LANES],
                sems.at[side],
            )
        )
        copies[-1].start()
    for copy in copies:
        copy.wait()


def both_ways(low, high, axis):
    count = lax.axis_size(axis)
    up = [(i, (i + 1) % count) for i in range(count)]
    down = [(b, a) for a, b in up]
    return lax.ppermute(high, axis, up), lax.ppermute(low, axis, down)


def placement(owner_index):
    owners = owner_index[:, 0]
    order = jnp.arange(32, dtype=jnp.int32)
    same = (owners[:, None] == owners[None, :]) & (order[None, :] < order[:, None])
    slots = owners * 2 + jnp.sum(same.astype(jnp.int32), axis=1)
    row, column = iota((256, 256), 0), iota((256, 256), 1)
    wanted = (row // 8) * 2 + row % 2
    fits = (jnp.repeat(slots, 8)[None, :] == wanted) & ((column % 8) // 2 == (row % 8) // 2)
    return fits.astype(BF)


def slot_cells(slot_element, element_cell):
    element = jnp.arange(32, dtype=jnp.int32)
    named = slot_element[0][:, None] == element[None, :]
    targets = jnp.sum(jnp.where(named, element_cell, 0), axis=1).astype(F32)
    return jnp.concatenate([targets, jnp.zeros((64,), F32)])[None, :]


def on_device(velocity, acoustic, projection, owner_index, slot_element, element_cell):
    velocity = velocity.reshape(3, 128, LANES)
    face = shape(FACE, LANES, dtype=BF)
    state = shape(ROWS, LANES)
    column = jnp.asarray(np.broadcast_to(DERIV.T.reshape(FACE, 1), (FACE, LANES)), F32)
    send = shape(XV + FACE, LANES, dtype=BF)
    xlow, xhigh = call(
        start_kernel,
        (send, send),
        velocity,
        acoustic,
        element_cell,
        far_in=(0, 1),
        scratch=[
            pltpu.VMEM((2, 3, 16, LANES), F32),
            pltpu.VMEM((2, 32, 4, LANES), F32),
            pltpu.SemaphoreType.DMA((4,)),
        ],
    )
    xlow, xhigh = both_ways(xlow, xhigh, "gx")
    first, base, back, table, faces = call(
        prepare_kernel,
        (
            state,
            state,
            shape(LANES, LANES, dtype=BF),
            shape(ROWS, 256, dtype=BF),
            shape(6, FACE, 256, dtype=BF),
        ),
        acoustic,
        element_cell,
        projection,
        column,
        scratch=[pltpu.VMEM((2, ROWS, LANES), F32)],
    )
    place = placement(owner_index)
    targets = slot_cells(slot_element, element_cell)
    send = shape(YV + 2 * FACE, LANES, dtype=BF)
    ylow, yhigh, base = call(
        y_kernel,
        (send, send, state),
        velocity,
        xlow,
        xhigh,
        first,
        base,
        targets,
        scratch=[pltpu.VMEM((3, 160, LANES), F32)],
    )
    ylow, yhigh = both_ways(ylow, yhigh, "gy")
    send = shape(ZV + 2 * FACE, LANES, dtype=BF)
    wide, own, zlow, zhigh, base, near = call(
        z_kernel,
        (shape(3, 20, 16, LANES), shape(3, 8, 384), send, send, state, shape(2 * FACE, LANES)),
        velocity,
        xlow,
        xhigh,
        ylow,
        yhigh,
        first,
        base,
        targets,
        scratch=[pltpu.VMEM((2, YV, LANES), F32)],
    )
    zlow, zhigh = both_ways(zlow, zhigh, "gz")
    flow, volumes = call(
        flow_kernel,
        (shape(3, 128, LANES), shape(32, 24, LANES, dtype=BF)),
        wide,
        own,
        zlow,
        zhigh,
        place,
        scratch=[
            pltpu.VMEM((3, 8, 384), F32),
            pltpu.VMEM((2, 3, 20, 16, LANES), F32),
            pltpu.VMEM((3, 20, 16, LANES), F32),
            pltpu.VMEM((2, 192, LANES), F32),
        ],
    )
    arrived = lax.all_to_all(volumes, ("gy", "gz"), split_axis=0, concat_axis=0, tiled=True)
    base, sides, gather = call(
        near_kernel,
        (state, shape(2 * FACE, LANES), shape(3, 256, 512, dtype=BF)),
        first,
        base,
        near,
        targets,
        ylow,
        yhigh,
        zlow,
        zhigh,
    )
    low, high, cells = call(
        send_kernel, (face, face, shape(256, 256, dtype=BF)), arrived, gather, faces, base
    )
    low, high = both_ways(low, high, "gx")
    main, ends, flow = call(
        second_kernel,
        (shape(*acoustic.shape), shape(2, LANES, LANES), shape(3, 128, LANES)),
        arrived,
        gather,
        table,
        faces,
        cells,
        base,
        sides,
        column,
        back,
        flow,
        far_out=(0,),
        scratch=[pltpu.VMEM((ROWS, LANES), F32)] * 3
        + [pltpu.VMEM(acoustic.shape, F32), pltpu.SemaphoreType.DMA],
    )
    out = call(
        last_kernel,
        shape(*acoustic.shape),
        main,
        ends,
        back,
        low,
        high,
        far_in=(0,),
        far_out=(0,),
        alias={0: 0},
        scratch=[pltpu.VMEM((2, 32, 4, LANES), F32), pltpu.SemaphoreType.DMA((2,))],
    )
    return flow.reshape(3, 16, 8, LANES), out


def solution(mesh):
    whole = P(("gx", "gy", "gz"), None, None)
    rows = P(("gx", "gy", "gz"), None)
    flow = P(None, "gx", "gy", "gz")
    return jax.shard_map(
        on_device,
        mesh=mesh,
        in_specs=(flow, whole, P(), rows, rows, rows),
        out_specs=(flow, whole),
        check_vma=False,
    )
```

time: 54.9 us -> 50.7 us (0.923)
  the two profiles are of different devices: /device:TPU:24 before, /device:TPU:1 now
where the time goes in v1:
time: 50.7 us; the launch traced here: 50.5 us
  starting transfers between devices  23.4 us (46%)
  waiting for transfers between devices  13.9 us (27%)
  Pallas kernels  8.76 us (17%)
  local copies, waits for them, and re-layouts  2.71 us (5%)
  other arithmetic  0.84 us (2%)
  between operations  0.83 us (2%)
    ppermute x8, starting transfers between devices, both_ways(): return (lax.ppermute(high, axis, up), lax.ppermute(low, axis, down))  17 us
    pallas_call x9, Pallas kernels, call(): pl.pallas_call(kernel, out_shape=out_shape, in_specs=[far if i in far_in...  8.76 us
    all_to_all x1, waiting for transfers between devices, on_device(): lax.all_to_all(volumes, ('gy', 'gz'), split_axis=0, concat_axis=0, tiled=...  7.86 us
    all_to_all x1, starting transfers between devices, on_device(): lax.all_to_all(volumes, ('gy', 'gz'), split_axis=0, concat_axis=0, tiled=...  6.44 us
    ppermute x8, waiting for transfers between devices, both_ways(): return (lax.ppermute(high, axis, up), lax.ppermute(low, axis, down))  6.08 us
    unnamed x18, local copies, waits for them, and re-layouts  2.55 us
  transfers between devices with their start and end apart: 9, of which 4 were waited for; matrix products, arithmetic and copies ran while one was open for 2% of the time, Pallas kernels for 9%

profile of v1, /device:TPU:1, one launch (start us, length us, event | category | flops | bytes accessed | tf_op | source)
XLA Modules:
  0.0 50.5 jit_solution(14034196016285305982)
XLA Ops:
  0.6 0.6 %copy-done.6 = s32[1,32]{1,0:T(1,128)S(1)} copy-done((s32[1,32]{1,0:T(1,128)S(1)}, s32[1,32]{1,0:T(1,128)}, u32[]{:S(2)}) %copy-start.6) | copy-done | bytes 152
  1.3 0.9 %copy-done = f32[3,16,8,128]{3,2,1,0:T(8,128)S(1)} copy-done((f32[3,16,8,128]{3,2,1,0:T(8,128)S(1)}, f32[3,16,8,128]{3,2,1,0:T(8,128)}, u32[]{:S(2)}) %copy-start) | copy-done | bytes 196632
  2.2 0.9 %copy-done.2 = f32[32,4,512]{2,1,0:T(4,128)S(1)} copy-done((f32[32,4,512]{2,1,0:T(4,128)S(1)}, f32[32,4,512]{2,1,0:T(4,128)}, u32[]{:S(2)}) %copy-start.2) | copy-done | bytes 262168
  3.2 0.5 shard_map.86
  3.6 2.5 %collective-permute-start = (bf16[112,128]{1,0:T(8,128)(2,1)S(1)}, bf16[112,128]{1,0:T(8,128)(2,1)S(1)}, u32[]{:S(2)}, u32[]{:S(2)}) collective-permute-start(bf16[112,128]{1,0:T(8,128)(2,1)S(1)} %get-tuple-element.29), channel_id=1, source_target_pairs={{0,32},{32,64},{64,96},{96,128},{128,160},{160,192},{192,224},{224... | collective-permute-start | bytes 86024 | tf_op jit(solution)/shard_map/ppermute | solution.py:744
  6.2 4.0 %collective-permute-start.1 = (bf16[112,128]{1,0:T(8,128)(2,1)S(1)}, bf16[112,128]{1,0:T(8,128)(2,1)S(1)}, u32[]{:S(2)}, u32[]{:S(2)}) collective-permute-start(bf16[112,128]{1,0:T(8,128)(2,1)S(1)} %get-tuple-element.30), channel_id=1, source_target_pairs={{32,0},{64,32},{96,64},{128,96},{160,128},{192,160},{224,192},{0,2... | collective-permute-start | bytes 86024 | tf_op jit(solution)/shard_map/ppermute | solution.py:744
  10.3 0.2 convert_reduce_fusion
  10.7 1.3 %shard_map.87 = (f32[512,128]{1,0:T(8,128)S(1)}, f32[512,128]{1,0:T(8,128)S(1)}, bf16[128,128]{1,0:T(8,128)(2,1)S(1)}, bf16[512,256]{1,0:T(8,128)(2,1)S(1)}, bf16[6,64,256]{2,1,0:T(8,128)(2,1)S(1)}) custom-call(f32[32,4,512]{2,1,0:T(4,128)S(1)} %copy-done.3, s32[1,32]{1,0:T(1,128)S(1)} %copy-done.6, f32[64,512]{1,0:T(8,128)S(1)} %copy-done.5, ...), custom_call_target="tpu_custom_call" | custom-call | flops 1000000 | bytes 1000000 | tf_op jit(solution)/shard_map/pallas_call | solution.py:89
  12.2 3.7 %collective-permute-start.2 = (bf16[272,128]{1,0:T(8,128)(2,1)S(1)}, bf16[272,128]{1,0:T(8,128)(2,1)S(1)}, u32[]{:S(2)}, u32[]{:S(2)}) collective-permute-start(bf16[272,128]{1,0:T(8,128)(2,1)S(1)} %get-tuple-element.33), channel_id=1, source_target_pairs={{0,8},{8,16},{16,24},{24,0},{1,9},{9,17},{17,25},{25,1},{2,10},{10... | collective-permute-start | bytes 208904 | tf_op jit(solution)/shard_map/ppermute | solution.py:744
  15.9 1.4 %collective-permute-done.2.ylow_ref = bf16[272,128]{1,0:T(8,128)(2,1)S(1)} collective-permute-done((bf16[272,128]{1,0:T(8,128)(2,1)S(1)}, bf16[272,128]{1,0:T(8,128)(2,1)S(1)}, u32[]{:S(2)}, u32[]{:S(2)}) %collective-permute-start.2) | collective-permute-done | bytes 69664 | tf_op jit(solution)/shard_map/ppermute | solution.py:744
  17.3 3.9 %collective-permute-done.3.yhigh_ref = bf16[272,128]{1,0:T(8,128)(2,1)S(1)} collective-permute-done((bf16[272,128]{1,0:T(8,128)(2,1)S(1)}, bf16[272,128]{1,0:T(8,128)(2,1)S(1)}, u32[]{:S(2)}, u32[]{:S(2)}) %collective-permute-start.3) | collective-permute-done | bytes 69664 | tf_op jit(solution)/shard_map/ppermute | solution.py:744
  21.1 0.3 shard_map.89
  21.4 1.4 %collective-permute-start.4 = (bf16[160,128]{1,0:T(8,128)(2,1)S(1)}, bf16[160,128]{1,0:T(8,128)(2,1)S(1)}, u32[]{:S(2)}, u32[]{:S(2)}) collective-permute-start(bf16[160,128]{1,0:T(8,128)(2,1)S(1)} %get-tuple-element.38), channel_id=1, source_target_pairs={{0,1},{1,2},{2,3},{3,4},{4,5},{5,6},{6,7},{7,0},{8,9},{9,10},{10,1... | collective-permute-start | bytes 122888 | tf_op jit(solution)/shard_map/ppermute | solution.py:744
  22.8 2.3 %collective-permute-start.5 = (bf16[160,128]{1,0:T(8,128)(2,1)S(1)}, bf16[160,128]{1,0:T(8,128)(2,1)S(1)}, u32[]{:S(2)}, u32[]{:S(2)}) collective-permute-start(bf16[160,128]{1,0:T(8,128)(2,1)S(1)} %get-tuple-element.39), channel_id=1, source_target_pairs={{1,0},{2,1},{3,2},{4,3},{5,4},{6,5},{7,6},{0,7},{9,8},{10,9},{11,1... | collective-permute-start | bytes 122888 | tf_op jit(solution)/shard_map/ppermute | solution.py:744
  25.1 0.5 %fusion.12.place_ref = bf16[256,256]{1,0:T(8,128)(2,1)S(1)} fusion(s32[256]{0:T(256)S(1)} %get-tuple-element.58, s32[256]{0:T(256)S(1)} %get-tuple-element.59, s32[256]{0:T(256)S(1)} %get-tuple-element.56, s32[256]{0:T(256)S(1)} %get-tuple-element.62, s32[256]{0:T(256)S(1)} %get-tuple-element.57, s32[256]{0:T(256)S(1)} %get-tuple-element.63, s32[256]{0:T(256)S(1)} %eq.52, ...), kind=kLoop, calls=%fused_computation.27 | loop fusion | flops 2621440 | bytes 139008 | tf_op jit(solution)/shard_map/convert_element_type | solution.py:755
  25.6 0.8 %collective-permute-done.4.zlow_ref = bf16[160,128]{1,0:T(8,128)(2,1)S(1)} collective-permute-done((bf16[160,128]{1,0:T(8,128)(2,1)S(1)}, bf16[160,128]{1,0:T(8,128)(2,1)S(1)}, u32[]{:S(2)}, u32[]{:S(2)}) %collective-permute-start.4) | collective-permute-done | bytes 40992 | tf_op jit(solution)/shard_map/ppermute | solution.py:744
  26.5 2.0 %shard_map.90 = (f32[3,128,128]{2,1,0:T(8,128)S(1)}, bf16[32,24,128]{2,1,0:T(8,128)(2,1)}) custom-call(f32[3,20,16,128]{3,2,1,0:T(8,128)S(1)} %get-tuple-element.36.wide_ref, f32[3,8,384]{2,1,0:T(8,128)S(1)} %get-tuple-element.37.own_ref, bf16[160,128]{1,0:T(8,128)(2,1)S(1)} %collective-permute-done.4.zlow_ref, ...), custom_call_target="tpu_custom_call" | custom-call | flops 1000000 | bytes 1000000 | tf_op jit(solution)/shard_map/pallas_call | solution.py:89
  28.5 6.4 %all-to-all-start = ((bf16[32,24,128]{2,1,0:T(8,128)(2,1)}), bf16[32,24,128]{2,1,0:T(8,128)(2,1)S(1)}, u32[]{:S(2)}, u32[]{:S(2)}) async-start(bf16[32,24,128]{2,1,0:T(8,128)(2,1)} %get-tuple-element.40), calls=%async_computation | async-start | bytes 393216 | tf_op jit(solution)/shard_map/all_to_all | solution.py:845
  34.9 0.4 shard_map.91
  35.3 7.9 %all-to-all-done.arrived_ref = bf16[32,24,128]{2,1,0:T(8,128)(2,1)S(1)} async-done(((bf16[32,24,128]{2,1,0:T(8,128)(2,1)}), bf16[32,24,128]{2,1,0:T(8,128)(2,1)S(1)}, u32[]{:S(2)}, u32[]{:S(2)}) %all-to-all-start) | async-done | bytes 196640 | tf_op jit(solution)/shard_map/all_to_all | solution.py:845
  43.2 0.4 shard_map.92
  43.6 3.0 %collective-permute-start.7 = (bf16[64,128]{1,0:T(8,128)(2,1)S(1)}, bf16[64,128]{1,0:T(8,128)(2,1)S(1)}, u32[]{:S(2)}, u32[]{:S(2)}) collective-permute-start(bf16[64,128]{1,0:T(8,128)(2,1)S(1)} %get-tuple-element.55), channel_id=1, source_target_pairs={{32,0},{64,32},{96,64},{128,96},{160,128},{192,160},{224,192},{0,2... | collective-permute-start | bytes 49160 | tf_op jit(solution)/shard_map/ppermute | solution.py:744
  46.6 2.8 %shard_map.93 = (f32[32,4,512]{2,1,0:T(4,128)}, f32[2,128,128]{2,1,0:T(8,128)S(1)}, f32[3,128,128]{2,1,0:T(8,128)}) custom-call(bf16[32,24,128]{2,1,0:T(8,128)(2,1)S(1)} %all-to-all-done.arrived_ref, bf16[3,256,512]{2,1,0:T(8,128)(2,1)S(1)} %get-tuple-element.43.gather_ref, bf16[512,256]{1,0:T(8,128)(2,1)S(1)} %get-tuple-element.44.table_ref, ...), custom_call_target="tpu_custom_call" | custom-call | flops 1000000 | bytes 1000000 | tf_op jit(solution)/shard_map/pallas_call | solution.py:89
  49.4 1.1 %shard_map.94 = f32[32,4,512]{2,1,0:T(4,128)} custom-call(f32[32,4,512]{2,1,0:T(4,128)} %get-tuple-element.52.main_ref, f32[2,128,128]{2,1,0:T(8,128)S(1)} %get-tuple-element.53.ends_ref, bf16[128,128]{1,0:T(8,128)(2,1)S(1)} %get-tuple-element.49.back_ref, bf16[64,128]{1,0:T(8,128)(2,1)S(1)} %collective-permute-done.6.low_ref, ...), custom_call_target="tpu_custom_call", output_to_operand_aliasing={{}: (0, {})} | custom-call | flops 1000000 | bytes 1000000 | tf_op jit(solution)/shard_map/pallas_call | solution.py:89
  (34 shorter events, 0.6 us)
Async XLA Ops:
  0.6 0.7 %copy-start.6 = (s32[1,32]{1,0:T(1,128)S(1)}, s32[1,32]{1,0:T(1,128)}, u32[]{:S(2)}) copy-start(s32[1,32]{1,0:T(1,128)} %cell_ref.3) | copy-start | bytes 388
  1.3 0.9 %copy-start = (f32[3,16,8,128]{3,2,1,0:T(8,128)S(1)}, f32[3,16,8,128]{3,2,1,0:T(8,128)}, u32[]{:S(2)}) copy-start(f32[3,16,8,128]{3,2,1,0:T(8,128)} %param.7) | copy-start | bytes 589828
  2.2 0.9 %copy-start.2 = (f32[32,4,512]{2,1,0:T(4,128)S(1)}, f32[32,4,512]{2,1,0:T(4,128)}, u32[]{:S(2)}) copy-start(f32[32,4,512]{2,1,0:T(4,128)} %acoustic_ref.3) | copy-start | bytes 786436
  3.2 7.1 %copy-start.7 = (s32[1,64]{1,0:T(1,128)S(1)}, s32[1,64]{1,0:T(1,128)}, u32[]{:S(2)}) copy-start(s32[1,64]{1,0:T(1,128)} %param.11) | copy-start | bytes 772
  3.2 7.2 %copy-start.8 = (s32[32,1]{0,1:T(1,128)S(1)}, s32[32,1]{0,1:T(1,128)}, u32[]{:S(2)}) copy-start(s32[32,1]{0,1:T(1,128)} %param.10) | copy-start | bytes 388
  3.2 7.5 %copy-start.3 = (f32[32,4,512]{2,1,0:T(4,128)S(1)}, f32[32,4,512]{2,1,0:T(4,128)}, u32[]{:S(2)}) copy-start(f32[32,4,512]{2,1,0:T(4,128)} %acoustic_ref.3) | copy-start | bytes 786436
  3.2 7.5 %copy-start.5 = (f32[64,512]{1,0:T(8,128)S(1)}, f32[64,512]{1,0:T(8,128)}, u32[]{:S(2)}) copy-start(f32[64,512]{1,0:T(8,128)} %projection_ref.1) | copy-start | bytes 393220
  3.6 7.1 %copy-start.4 = (f32[64,128]{1,0:T(8,128)S(1)}, f32[64,128]{1,0:T(8,128)}, u32[]{:S(2)}) copy-start(f32[64,128]{1,0:T(8,128)} %constant.69.clone.column_ref) | copy-start | bytes 98308
  3.6 8.4 %collective-permute-start = (bf16[112,128]{1,0:T(8,128)(2,1)S(1)}, bf16[112,128]{1,0:T(8,128)(2,1)S(1)}, u32[]{:S(2)}, u32[]{:S(2)}) collective-permute-start(bf16[112,128]{1,0:T(8,128)(2,1)S(1)} %get-tuple-element.29), channel_id=1, source_target_pairs={{0,32},{32,64},{64,96},{96,128},{128,160},{160,192},{192,224},{224... | collective-permute-start | bytes 86024 | tf_op jit(solution)/shard_map/ppermute | solution.py:744
  6.2 5.9 %collective-permute-start.1 = (bf16[112,128]{1,0:T(8,128)(2,1)S(1)}, bf16[112,128]{1,0:T(8,128)(2,1)S(1)}, u32[]{:S(2)}, u32[]{:S(2)}) collective-permute-start(bf16[112,128]{1,0:T(8,128)(2,1)S(1)} %get-tuple-element.30), channel_id=1, source_target_pairs={{32,0},{64,32},{96,64},{128,96},{160,128},{192,160},{224,192},{0,2... | collective-permute-start | bytes 86024 | tf_op jit(solution)/shard_map/ppermute | solution.py:744
  10.7 1.3 %copy-start.1 = (f32[3,16,8,128]{3,2,1,0:T(8,128)S(1)}, f32[3,16,8,128]{3,2,1,0:T(8,128)}, u32[]{:S(2)}) copy-start(f32[3,16,8,128]{3,2,1,0:T(8,128)} %param.7) | copy-start | bytes 589828
  12.2 5.0 %collective-permute-start.2 = (bf16[272,128]{1,0:T(8,128)(2,1)S(1)}, bf16[272,128]{1,0:T(8,128)(2,1)S(1)}, u32[]{:S(2)}, u32[]{:S(2)}) collective-permute-start(bf16[272,128]{1,0:T(8,128)(2,1)S(1)} %get-tuple-element.33), channel_id=1, source_target_pairs={{0,8},{8,16},{16,24},{24,0},{1,9},{9,17},{17,25},{25,1},{2,10},{10... | collective-permute-start | bytes 208904 | tf_op jit(solution)/shard_map/ppermute | solution.py:744
  15.9 5.2 %collective-permute-start.3 = (bf16[272,128]{1,0:T(8,128)(2,1)S(1)}, bf16[272,128]{1,0:T(8,128)(2,1)S(1)}, u32[]{:S(2)}, u32[]{:S(2)}) collective-permute-start(bf16[272,128]{1,0:T(8,128)(2,1)S(1)} %get-tuple-element.34), channel_id=1, source_target_pairs={{8,0},{16,8},{24,16},{0,24},{9,1},{17,9},{25,17},{1,25},{10,2},{18... | collective-permute-start | bytes 208904 | tf_op jit(solution)/shard_map/ppermute | solution.py:744
  21.4 5.0 %collective-permute-start.4 = (bf16[160,128]{1,0:T(8,128)(2,1)S(1)}, bf16[160,128]{1,0:T(8,128)(2,1)S(1)}, u32[]{:S(2)}, u32[]{:S(2)}) collective-permute-start(bf16[160,128]{1,0:T(8,128)(2,1)S(1)} %get-tuple-element.38), channel_id=1, source_target_pairs={{0,1},{1,2},{2,3},{3,4},{4,5},{5,6},{6,7},{7,0},{8,9},{9,10},{10,1... | collective-permute-start | bytes 122888 | tf_op jit(solution)/shard_map/ppermute | solution.py:744
  22.8 3.7 %collective-permute-start.5 = (bf16[160,128]{1,0:T(8,128)(2,1)S(1)}, bf16[160,128]{1,0:T(8,128)(2,1)S(1)}, u32[]{:S(2)}, u32[]{:S(2)}) collective-permute-start(bf16[160,128]{1,0:T(8,128)(2,1)S(1)} %get-tuple-element.39), channel_id=1, source_target_pairs={{1,0},{2,1},{3,2},{4,3},{5,4},{6,5},{7,6},{0,7},{9,8},{10,9},{11,1... | collective-permute-start | bytes 122888 | tf_op jit(solution)/shard_map/ppermute | solution.py:744
  28.5 14.7 %all-to-all-start = ((bf16[32,24,128]{2,1,0:T(8,128)(2,1)}), bf16[32,24,128]{2,1,0:T(8,128)(2,1)S(1)}, u32[]{:S(2)}, u32[]{:S(2)}) async-start(bf16[32,24,128]{2,1,0:T(8,128)(2,1)} %get-tuple-element.40), calls=%async_computation | async-start | bytes 393216 | tf_op jit(solution)/shard_map/all_to_all | solution.py:845
  43.5 5.9 %collective-permute-start.6 = (bf16[64,128]{1,0:T(8,128)(2,1)S(1)}, bf16[64,128]{1,0:T(8,128)(2,1)S(1)}, u32[]{:S(2)}, u32[]{:S(2)}) collective-permute-start(bf16[64,128]{1,0:T(8,128)(2,1)S(1)} %get-tuple-element.54), channel_id=1, source_target_pairs={{0,32},{32,64},{64,96},{96,128},{128,160},{160,192},{192,224},{224... | collective-permute-start | bytes 49160 | tf_op jit(solution)/shard_map/ppermute | solution.py:744
  43.6 5.8 %collective-permute-start.7 = (bf16[64,128]{1,0:T(8,128)(2,1)S(1)}, bf16[64,128]{1,0:T(8,128)(2,1)S(1)}, u32[]{:S(2)}, u32[]{:S(2)}) collective-permute-start(bf16[64,128]{1,0:T(8,128)(2,1)S(1)} %get-tuple-element.55), channel_id=1, source_target_pairs={{32,0},{64,32},{96,64},{128,96},{160,128},{192,160},{224,192},{0,2... | collective-permute-start | bytes 49160 | tf_op jit(solution)/shard_map/ppermute | solution.py:744

commit v2 on v1

--- a/solution.py
+++ b/solution.py
@@ -21,6 +21,8 @@
 LIFT = WAVE_STEP * 0.5 * ORDER * (ORDER + 1) / 2.0
 XV = 48
 YV = 144
+PARTS = 1
+START_GRANT = 56_440_000
 ZV = 32
 
 
@@ -82,7 +84,7 @@
 
 
 def call(
-    kernel, out_shape, *args, scratch=(), far_in=(), far_out=(), alias={}, flops=10**6, moved=10**6
+    kernel, out_shape, *args, scratch=(), far_in=(), far_out=(), alias={}, grant=16 * 2**20
 ):
     near, far = pl.BlockSpec(memory_space=pltpu.VMEM), pl.BlockSpec(memory_space=pl.ANY)
     outs = [far if i in far_out else near for i in range(len(jax.tree.leaves(out_shape)))]
@@ -93,8 +95,8 @@
         out_specs=tuple(outs) if isinstance(out_shape, tuple) else outs[0],
         scratch_shapes=list(scratch),
         input_output_aliases=alias,
-        compiler_params=pltpu.CompilerParams(vmem_limit_bytes=16 * 2**20),
-        cost_estimate=pl.CostEstimate(flops=flops, bytes_accessed=moved, transcendentals=0),
+        compiler_params=pltpu.CompilerParams(vmem_limit_bytes=grant),
+        cost_estimate=pl.CostEstimate(flops=10**6, bytes_accessed=10**6, transcendentals=0),
     )(*args)
 
 
@@ -233,7 +235,7 @@
             out_ref[at : at + K, :] = total
 
 
-def start_kernel(velocity_ref, acoustic_ref, cell_ref, low_ref, high_ref, flow, wave, sems):
+def load_kernel(velocity_ref, acoustic_ref, lines_ref, faces_ref, flow, wave, sems):
     copies = []
     for side, tile in ((0, 0), (1, 3)):
         copies.append((acoustic_ref.at[:, :, tile * LANES : tile * LANES + LANES], wave.at[side]))
@@ -242,27 +244,32 @@
     copies = [pltpu.make_async_copy(a, b, sems.at[i]) for i, (a, b) in enumerate(copies)]
     for copy in copies:
         copy.start()
-    place = jnp.where(cell_matrix(cell_ref), 1.0, 0.0).astype(BF)
     for copy in copies:
         copy.wait()
-    faces = jnp.concatenate(
-        [
-            jnp.where(iota((32, LANES), 1) < FACE, wave[0, :, v, :], wave[1, :, v, :])
-            for v in range(4)
-        ],
-        axis=0,
-    )
-    turned = jnp.transpose(nn(place, faces.astype(BF))).astype(BF)
+    left = iota((32, LANES), 1) < FACE
+    for v in range(4):
+        rows = jnp.where(left, wave[0, :, v, :], wave[1, :, v, :])
+        faces_ref[v * 32 : v * 32 + 32, :] = rows.astype(BF)
+    for side in range(2):
+        for c in range(3):
+            lines_ref[side, c * 16 : c * 16 + 16, :] = flow[side, c].astype(BF)
+
+
+def start_kernel(lines_ref, faces_ref, cell_ref, low_ref, high_ref, place_ref):
+    place = jnp.where(cell_matrix(cell_ref), 1.0, 0.0).astype(BF)
+    turned = jnp.transpose(nn(place, faces_ref[...])).astype(BF)
     low_ref[XV:, :] = turned[:FACE]
     high_ref[XV:, :] = turned[FACE:]
-    for c in range(3):
-        low_ref[c * 16 : c * 16 + 16, :] = flow[0, c].astype(BF)
-        high_ref[c * 16 : c * 16 + 16, :] = flow[1, c].astype(BF)
+    low_ref[0:XV, :] = lines_ref[0]
+    high_ref[0:XV, :] = lines_ref[1]
+    place_ref[...] = place
 
 
 def prepare_kernel(
     acoustic_ref,
+    place_ref,
     cell_ref,
+    slot_ref,
     projection_ref,
     column_ref,
     state_ref,
@@ -270,11 +277,15 @@
     back_ref,
     table_ref,
     faces_ref,
+    targets_ref,
     scratch,
 ):
-    chosen = jnp.where(cell_matrix(cell_ref), 1.0, 0.0)
-    place = chosen.astype(BF)
-    back_ref[...] = jnp.transpose(chosen).astype(BF)
+    slots = jnp.broadcast_to(jnp.concatenate([slot_ref[...]] * 2, axis=1), (32, LANES))
+    named = jnp.where(slots == iota((32, LANES), 0), 1.0, 0.0).astype(BF)
+    cells = jnp.broadcast_to(cell_ref[...], (16, 32)).astype(F32).astype(BF)
+    targets_ref[...] = nn(cells, named)[0:1]
+    place = place_ref[...]
+    back_ref[...] = jnp.transpose(place.astype(F32)).astype(BF)
     high, low = split2(stored_rows(acoustic_ref))
     state_ref[...] = jnp.transpose(nn(place, high) + nn(place, low))
     high, low = split2(projection_ref[...])
@@ -319,7 +330,7 @@
         low_lift(0, own_low - xlow_ref[XV:, :].astype(F32)),
         high_lift(0, own_high - xhigh_ref[XV:, :].astype(F32)),
     )
-    traces, bases = face_pair(state_ref, 1), face_pair(out_ref, 1)
+    faces = packed(1, face_pair(state_ref, 1), face_pair(out_ref, 1))
     spare = jnp.concatenate([targets_ref[...], jnp.zeros((3, LANES), F32)], axis=0)
     for side, (out, first) in enumerate(((low_ref, 0), (high_ref, 6))):
         pieces = []
@@ -328,13 +339,26 @@
                 pieces.append(wide[c, pl.ds(first + y, 20, stride=8), :])
                 pieces.append(spare)
         out[0:YV, :] = jnp.concatenate(pieces, axis=0).astype(BF)
-        out[YV : YV + FACE, :] = traces[side].astype(BF)
-        out[YV + FACE :, :] = bases[side].astype(BF)
+        out[YV:, :] = faces[side]
+
+
+def packed(axis, traces, bases):
+    at_low, at_high = cut_of(axis, traces[0].shape)
+    step = 16 if axis == 1 else 1
+    return (
+        jnp.where(at_low, traces[0], roll(bases[0], step, 1)).astype(BF),
+        jnp.where(at_high, traces[1], roll(bases[1], -step, 1)).astype(BF),
+    )
 
 
 def joined(axis, low, high):
     _, at_high = cut_of(axis, low.shape)
-    return jnp.where(at_high, low.astype(F32), high.astype(F32))
+    low, high = low.astype(F32), high.astype(F32)
+    step = 16 if axis == 1 else 1
+    return (
+        jnp.where(at_high, low, high),
+        jnp.where(at_high, roll(low, step, 1), roll(high, -step, 1)),
+    )
 
 
 def z_kernel(
@@ -377,11 +401,12 @@
         own = nt(picks, rows)
         own_ref[c, :, 0:320] = own[0:8]
         own_ref[c, :, 320:384] = jnp.zeros((8, 64), F32)
-    near_ref[0:FACE, :] = joined(1, ylow_ref[YV : YV + FACE, :], yhigh_ref[YV : YV + FACE, :])
-    near_ref[FACE:, :] = joined(1, ylow_ref[YV + FACE :, :], yhigh_ref[YV + FACE :, :])
+    trace, base = joined(1, ylow_ref[YV:, :], yhigh_ref[YV:, :])
+    near_ref[0:FACE, :] = trace
+    near_ref[FACE:, :] = base
     out_ref[...] = base_ref[...]
     add_pair(out_ref, 1, *boundary_lifts(1, *face_pair(state_ref, 1), near_ref[0:FACE, :]))
-    traces, bases = face_pair(state_ref, 2), face_pair(out_ref, 2)
+    faces = packed(2, face_pair(state_ref, 2), face_pair(out_ref, 2))
     for side, (out, first) in enumerate(((low_ref, 0), (high_ref, 2))):
         pieces = []
         for c in range(3):
@@ -390,8 +415,7 @@
         pieces += [targets_ref[...], jnp.zeros((5, LANES), F32)]
         pieces.append(near_ref[pl.ds(side * (K - 1), K, stride=K), :])
         out[0:ZV, :] = jnp.concatenate(pieces, axis=0).astype(BF)
-        out[ZV : ZV + FACE, :] = traces[side].astype(BF)
-        out[ZV + FACE :, :] = bases[side].astype(BF)
+        out[ZV:, :] = faces[side]
 
 
 def differences(low, high):
@@ -421,14 +445,86 @@
     ]
 
 
+INNER = slice(2, 10)
+
+
+def along_z(values, low_edge, high_edge):
+    axis = values[0].ndim - 1
+    lane = iota(values[0].shape, axis)
+    low = [jnp.where(lane == 0, h, roll(v, 1, axis)) for v, h in zip(values, low_edge)]
+    high = [jnp.where(lane == 127, h, roll(v, -1, axis)) for v, h in zip(values, high_edge)]
+    return low, high
+
+
+def plane(source, x, edges):
+    centre = [source[c, x, INNER, :] for c in range(3)]
+    zlow, zhigh = along_z(centre, edges, edges)
+    low = [
+        [source[c, x - 1, INNER, :] for c in range(3)],
+        [source[c, x, 1:9, :] for c in range(3)],
+        zlow,
+    ]
+    high = [
+        [source[c, x + 1, INNER, :] for c in range(3)],
+        [source[c, x, 3:11, :] for c in range(3)],
+        zhigh,
+    ]
+    return centre, low, high
+
+
+def add_lamb(sums, parts, x, first):
+    i, a = (x // 2) // 4, (x // 2) % 4
+    for c in range(3):
+        at = first + (c * 4 + a) * 8
+        sums[i, at : at + 8, :] = parts[c]
+
+
+def inner_flow_kernel(wide_ref, middle_ref, sums_ref):
+    for y in (1, 10):
+
+        def row(first, at):
+            return [wide_ref[c, first : first + 16, at, :] for c in range(3)]
+
+        centre = row(2, y)
+        nothing = [0.0] * 3
+        zlow, zhigh = along_z(centre, nothing, nothing)
+        low = [row(1, y), row(2, y - 1), zlow]
+        high = [row(3, y), row(2, y + 1), zhigh]
+        new = moved_on(centre, low, high, differences(low, high))
+        for c in range(3):
+            middle_ref[c, 2:18, y, :] = new[c]
+    held = None
+    for x in range(1, 19):
+        centre, low, high = plane(wide_ref, x, [0.0] * 3)
+        diff = differences(low, high)
+        new = moved_on(centre, low, high, diff)
+        for c in range(3):
+            middle_ref[c, x, INNER, :] = new[c]
+        if 2 <= x < 18:
+            parts = lamb(centre, diff)
+            if x % 2 == 0:
+                held = parts
+            else:
+                add_lamb(sums_ref, [p + h for p, h in zip(parts, held)], x - 2, 0)
+
+
 def flow_kernel(
     wide_ref,
     own_ref,
     zlow_ref,
     zhigh_ref,
     place_ref,
+    inner_ref,
+    inner_sums_ref,
+    state_ref,
+    base_ref,
+    near_ref,
+    side_ref,
     out_ref,
     volume_ref,
+    base_out_ref,
+    sides_ref,
+    gather_ref,
     ends,
     halo,
     middle,
@@ -468,67 +564,54 @@
     spread_out(
         moved_on(edge, edge_low, edge_high, differences(edge_low, edge_high)), 1
     )
-
-    def along_z(values, edges):
-        lane = iota(values[0].shape, values[0].ndim - 1)
-        axis = values[0].ndim - 1
-        low = [jnp.where(lane == 0, h, roll(v, 1, axis)) for v, h in zip(values, edges)]
-        high = [jnp.where(lane == 127, h, roll(v, -1, axis)) for v, h in zip(values, edges)]
-        return low, high
-
-    def plane(source, x, level, y):
-        centre = [source[c, x, y, :] for c in range(3)]
-        zlow, zhigh = along_z(centre, [halo[level, c, x, y, :] for c in range(3)])
-        up = slice(y.start + 1, y.stop + 1)
-        down = slice(y.start - 1, y.stop - 1)
-        low = [
-            [source[c, x - 1, y, :] for c in range(3)],
-            [source[c, x, down, :] for c in range(3)],
-            zlow,
-        ]
-        high = [
-            [source[c, x + 1, y, :] for c in range(3)],
-            [source[c, x, up, :] for c in range(3)],
-            zhigh,
-        ]
-        return centre, low, high
-
-    inner = slice(2, 10)
+    end_faces(
+        state_ref,
+        base_ref,
+        near_ref,
+        side_ref,
+        zlow_ref,
+        zhigh_ref,
+        base_out_ref,
+        sides_ref,
+        gather_ref,
+    )
+
+    def sign(dims):
+        return jnp.where(iota(dims, len(dims) - 1) == 0, -1.0, 1.0)
+
+    def growth(speed, signs):
+        return FLOW_STEP * VISCOSITY - (0.5 * FLOW_STEP) * (signs * speed)
+
     for y in (1, 10):
-        def line(source, first, at):
-            return [source[c, first : first + 16, at, :] for c in range(3)]
-
-        centre = line(wide_ref, 2, y)
-        zlow, zhigh = along_z(
-            centre, [halo[0, c, 2:18, y, :] for c in range(3)]
-        )
-        low = [line(wide_ref, 1, y), line(wide_ref, 2, y - 1), zlow]
-        high = [line(wide_ref, 3, y), line(wide_ref, 2, y + 1), zhigh]
-        new = moved_on(centre, low, high, differences(low, high))
+        rate = growth(wide_ref[2, 2:18, y, :], sign((16, LANES)))
         for c in range(3):
-            middle[c, 2:18, y, :] = new[c]
-
-    def add_lamb(parts, x, step):
-        i, a = (x // 2) // 4, (x // 2) % 4
+            middle[c, 2:18, y, :] = inner_ref[c, 2:18, y, :] + rate * halo[0, c, 2:18, y, :]
+    held = None
+    signs = sign((8, LANES))
+    for x in range(1, 19):
+        centre = [wide_ref[c, x, INNER, :] for c in range(3)]
+        edges = [halo[0, c, x, INNER, :] for c in range(3)]
+        rate = growth(centre[2], signs)
         for c in range(3):
-            at = ((step * 3 + c) * 4 + a) * 8
-            sums[i, at : at + 8, :] = parts[c]
-
-    held = None
-    for x in range(1, 19):
-        centre, low, high = plane(wide_ref, x, 0, inner)
-        diff = differences(low, high)
-        new = moved_on(centre, low, high, diff)
-        for c in range(3):
-            middle[c, x, inner, :] = new[c]
+            middle[c, x, INNER, :] = inner_ref[c, x, INNER, :] + rate * edges[c]
         if 2 <= x < 18:
-            parts = lamb(centre, diff)
+            first, second = signs * edges[0], signs * edges[1]
+            parts = [
+                first * centre[2],
+                second * centre[2],
+                -(second * centre[1]) - first * centre[0],
+            ]
             if x % 2 == 0:
                 held = parts
             else:
-                add_lamb([p + h for p, h in zip(parts, held)], x - 2, 0)
+                i, a = ((x - 2) // 2) // 4, ((x - 2) // 2) % 4
+                for c in range(3):
+                    at = (c * 4 + a) * 8
+                    sums[i, at : at + 8, :] = inner_sums_ref[i, at : at + 8, :] + (
+                        parts[c] + held[c]
+                    )
     for x in range(2, 18):
-        centre, low, high = plane(middle, x, 1, inner)
+        centre, low, high = plane(middle, x, [halo[1, c, x, INNER, :] for c in range(3)])
         diff = differences(low, high)
         new = moved_on(centre, low, high, diff)
         for c in range(3):
@@ -537,7 +620,7 @@
         if x % 2 == 0:
             held = parts
         else:
-            add_lamb([p + h for p, h in zip(parts, held)], x - 2, 1)
+            add_lamb(sums, [p + h for p, h in zip(parts, held)], x - 2, 96)
     both = []
     for i in range(2):
         both.append(sums[i, pl.ds(0, 96, stride=2), :] + sums[i, pl.ds(1, 96, stride=2), :])
@@ -575,27 +658,49 @@
     ]
 
 
+def line(ref, at):
+    return ref[0:32, :].astype(F32)[at : at + 1]
+
+
+def placement(owner_ref):
+    owner = jnp.concatenate([owner_ref[...]] * 4, axis=1).astype(F32)
+    across = jnp.broadcast_to(owner, (LANES, LANES))
+    row, column = iota((32, LANES), 0), iota((32, LANES), 1)
+    down = nt(jnp.where(row == column, 1.0, 0.0).astype(BF), across.astype(BF))
+    earlier = jnp.where((across[0:32] == down) & (column < row), 1.0, 0.0)
+    slots = 2.0 * down + jnp.sum(earlier, axis=1, keepdims=True)
+    spread = jnp.where(iota((32, 256), 1) // 8 == iota((32, 256), 0), 1.0, 0.0).astype(BF)
+    slots = tn(slots.astype(BF), spread)
+    slots = jnp.concatenate([slots, slots], axis=0)
+    row, column = iota((256, 256), 0), iota((256, 256), 1)
+    wanted = ((row // 8) * 2 + row % 2).astype(F32)
+    fits = (slots == wanted) & ((column % 8) // 2 == (row % 8) // 2)
+    return jnp.where(fits, 1.0, 0.0).astype(BF)
+
+
 def near_kernel(
-    state_ref,
-    base_ref,
-    near_ref,
-    targets_ref,
-    ylow_ref,
-    yhigh_ref,
-    zlow_ref,
-    zhigh_ref,
-    out_ref,
-    sides_ref,
-    gather_ref,
+    state_ref, near_ref, targets_ref, ylow_ref, yhigh_ref, owner_ref, sides_ref, gather_ref, place_ref
 ):
-    znear = joined(2, zlow_ref[ZV : ZV + FACE, :], zhigh_ref[ZV : ZV + FACE, :])
-    own_y, own_z = face_pair(state_ref, 1), face_pair(state_ref, 2)
+    place_ref[...] = placement(owner_ref)
+    sides_ref[...] = near_ref[FACE:, :] + near_lift(1, near_ref[0:FACE, :], *face_pair(state_ref, 1))
+    groups = [
+        gather_matrix(targets_ref[...]),
+        gather_matrix(line(ylow_ref, 20), line(yhigh_ref, 20), cut_of(1, (256, LANES))[1]),
+    ]
+    for g, parts in enumerate(groups):
+        for z in range(4):
+            gather_ref[g, :, z * LANES : z * LANES + LANES] = parts[z]
+
+
+def end_faces(
+    state_ref, base_ref, near_ref, side_ref, zlow_ref, zhigh_ref, out_ref, sides_ref, gather_ref
+):
+    trace, base = joined(2, zlow_ref[ZV:, :], zhigh_ref[ZV:, :])
+    own = face_pair(state_ref, 2)
     out_ref[...] = base_ref[...]
-    add_pair(out_ref, 2, *boundary_lifts(2, *own_z, znear))
-    ynear = near_ref[0:FACE, :]
-    sides_ref[0:FACE, :] = near_ref[FACE:, :] + near_lift(1, ynear, *own_y)
-    zbase = joined(2, zlow_ref[ZV + FACE :, :], zhigh_ref[ZV + FACE :, :])
-    sides_ref[FACE:, :] = zbase + near_lift(2, znear, *own_z)
+    add_pair(out_ref, 2, *boundary_lifts(2, *own, trace))
+    sides_ref[0:FACE, :] = side_ref[...]
+    sides_ref[FACE:, :] = base + near_lift(2, trace, *own)
     from_low = zlow_ref[0:ZV, :].astype(F32)[24:32]
     from_high = zhigh_ref[0:ZV, :].astype(F32)[24:32]
     at_low, at_high = cut_of(2, (K, LANES))
@@ -603,18 +708,9 @@
     sides_ref[pl.ds(0, K, stride=K), :] += jnp.where(at_low, low_lift(2, jump), 0.0)
     jump = near_ref[pl.ds(K - 1, K, stride=K), :] - roll(from_high, 15, 1)
     sides_ref[pl.ds(K - 1, K, stride=K), :] += jnp.where(at_high, high_lift(2, jump), 0.0)
-
-    def line(ref, at):
-        return ref[0:32, :].astype(F32)[at : at + 1]
-
-    groups = [
-        gather_matrix(targets_ref[...]),
-        gather_matrix(line(ylow_ref, 20), line(yhigh_ref, 20), cut_of(1, (256, LANES))[1]),
-        gather_matrix(line(zlow_ref, 18), line(zhigh_ref, 18), cut_of(2, (256, LANES))[1]),
-    ]
-    for g, parts in enumerate(groups):
-        for z in range(4):
-            gather_ref[g, :, z * LANES : z * LANES + LANES] = parts[z]
+    parts = gather_matrix(line(zlow_ref, 18), line(zhigh_ref, 18), cut_of(2, (256, LANES))[1])
+    for z in range(4):
+        gather_ref[:, z * LANES : z * LANES + LANES] = parts[z]
 
 
 def stacked(summed, starts):
@@ -660,6 +756,7 @@
 def second_kernel(
     arrived_ref,
     gather_ref,
+    end_gather_ref,
     table_ref,
     faces_ref,
     cells_ref,
@@ -675,16 +772,18 @@
     extra,
     total,
     rows_held,
-    sem,
+    sems,
 ):
-    flow_out_ref[...] = flow_ref[...]
+    flow_copy = pltpu.make_async_copy(flow_ref, flow_out_ref, sems.at[0])
+    flow_copy.start()
     source = GAIN * nn(table_ref[...], cells_ref[...])
     state[...] = base_ref[...] - source[:, 0:LANES]
     extra[...] = source[:, LANES:]
     near = []
     for axis in (1, 2):
         rows = arrived_ref[:, 8 * axis : 8 * axis + 8, :].reshape(256, LANES)
-        cells = stacked(tn(rows, gather_ref[axis]), (by_side(axis),))
+        gather = gather_ref[1] if axis == 1 else end_gather_ref[...]
+        cells = stacked(tn(rows, gather), (by_side(axis),))
         at_low, at_high = cut_of(axis, (FACE, LANES))
         face = jnp.where(
             at_high,
@@ -699,15 +798,20 @@
         add_pair(total, axis, low_lift(axis, own_low - low), high_lift(axis, own_high - high))
     own_low, own_high = face_pair(state, 0)
     add_pair(total, 0, low_lift(0, own_low), high_lift(0, own_high))
-    high, low = split2(jnp.transpose(total[...]))
     back = back_ref[...]
-    rows = nn(back, high) + nn(back, low)
-    ends_ref[0] = rows[:, 0:LANES]
-    ends_ref[1] = rows[:, 3 * LANES :]
+
+    def turned(first, last):
+        high, low = split2(jnp.transpose(total[first:last, :]))
+        return nn(back, high) + nn(back, low)
+
+    rows = turned(LANES, 3 * LANES)
     for v in range(4):
         rows_held[:, v, :] = rows[v * 32 : v * 32 + 32, :]
-    copy = pltpu.make_async_copy(rows_held, out_ref, sem)
+    copy = pltpu.make_async_copy(rows_held, out_ref.at[:, :, LANES : 3 * LANES], sems.at[1])
     copy.start()
+    ends_ref[0] = turned(0, LANES)
+    ends_ref[1] = turned(3 * LANES, ROWS)
+    flow_copy.wait()
     copy.wait()
 
 
@@ -725,14 +829,16 @@
         total = ends_ref[side] + jnp.where(left if side == 0 else ~left, rows, 0.0)
         for v in range(4):
             held[side, :, v, :] = total[v * 32 : v * 32 + 32, :]
-        copies.append(
-            pltpu.make_async_copy(
-                held.at[side],
-                out_ref.at[:, :, tile * LANES : tile * LANES + LANES],
-                sems.at[side],
+        for part in range(PARTS):
+            some = slice(part * 32 // PARTS, (part + 1) * 32 // PARTS)
+            copies.append(
+                pltpu.make_async_copy(
+                    held.at[side, some],
+                    out_ref.at[some, :, tile * LANES : tile * LANES + LANES],
+                    sems.at[side * PARTS + part],
+                )
             )
-        )
-        copies[-1].start()
+            copies[-1].start()
     for copy in copies:
         copy.wait()
 
@@ -742,24 +848,6 @@
     up = [(i, (i + 1) % count) for i in range(count)]
     down = [(b, a) for a, b in up]
     return lax.ppermute(high, axis, up), lax.ppermute(low, axis, down)
-
-
-def placement(owner_index):
-    owners = owner_index[:, 0]
-    order = jnp.arange(32, dtype=jnp.int32)
-    same = (owners[:, None] == owners[None, :]) & (order[None, :] < order[:, None])
-    slots = owners * 2 + jnp.sum(same.astype(jnp.int32), axis=1)
-    row, column = iota((256, 256), 0), iota((256, 256), 1)
-    wanted = (row // 8) * 2 + row % 2
-    fits = (jnp.repeat(slots, 8)[None, :] == wanted) & ((column % 8) // 2 == (row % 8) // 2)
-    return fits.astype(BF)
-
-
-def slot_cells(slot_element, element_cell):
-    element = jnp.arange(32, dtype=jnp.int32)
-    named = slot_element[0][:, None] == element[None, :]
-    targets = jnp.sum(jnp.where(named, element_cell, 0), axis=1).astype(F32)
-    return jnp.concatenate([targets, jnp.zeros((64,), F32)])[None, :]
 
 
 def on_device(velocity, acoustic, projection, owner_index, slot_element, element_cell):
@@ -768,21 +856,24 @@
     state = shape(ROWS, LANES)
     column = jnp.asarray(np.broadcast_to(DERIV.T.reshape(FACE, 1), (FACE, LANES)), F32)
     send = shape(XV + FACE, LANES, dtype=BF)
-    xlow, xhigh = call(
-        start_kernel,
-        (send, send),
+    chosen = shape(LANES, LANES, dtype=BF)
+    lines, faces = call(
+        load_kernel,
+        (shape(2, XV, LANES, dtype=BF), shape(LANES, LANES, dtype=BF)),
         velocity,
         acoustic,
-        element_cell,
         far_in=(0, 1),
+        grant=START_GRANT,
         scratch=[
             pltpu.VMEM((2, 3, 16, LANES), F32),
             pltpu.VMEM((2, 32, 4, LANES), F32),
             pltpu.SemaphoreType.DMA((4,)),
         ],
     )
+    chosen = shape(LANES, LANES, dtype=BF)
+    xlow, xhigh, chosen = call(start_kernel, (send, send, chosen), lines, faces, element_cell)
     xlow, xhigh = both_ways(xlow, xhigh, "gx")
-    first, base, back, table, faces = call(
+    first, base, back, table, faces, targets = call(
         prepare_kernel,
         (
             state,
@@ -790,16 +881,17 @@
             shape(LANES, LANES, dtype=BF),
             shape(ROWS, 256, dtype=BF),
             shape(6, FACE, 256, dtype=BF),
+            shape(1, LANES),
         ),
         acoustic,
+        chosen,
         element_cell,
+        slot_element,
         projection,
         column,
         scratch=[pltpu.VMEM((2, ROWS, LANES), F32)],
     )
-    place = placement(owner_index)
-    targets = slot_cells(slot_element, element_cell)
-    send = shape(YV + 2 * FACE, LANES, dtype=BF)
+    send = shape(YV + FACE, LANES, dtype=BF)
     ylow, yhigh, base = call(
         y_kernel,
         (send, send, state),
@@ -812,7 +904,7 @@
         scratch=[pltpu.VMEM((3, 160, LANES), F32)],
     )
     ylow, yhigh = both_ways(ylow, yhigh, "gy")
-    send = shape(ZV + 2 * FACE, LANES, dtype=BF)
+    send = shape(ZV + FACE, LANES, dtype=BF)
     wide, own, zlow, zhigh, base, near = call(
         z_kernel,
         (shape(3, 20, 16, LANES), shape(3, 8, 384), send, send, state, shape(2 * FACE, LANES)),
@@ -827,14 +919,39 @@
         scratch=[pltpu.VMEM((2, YV, LANES), F32)],
     )
     zlow, zhigh = both_ways(zlow, zhigh, "gz")
-    flow, volumes = call(
+    middle, sums = call(
+        inner_flow_kernel, (shape(3, 20, 16, LANES), shape(2, 96, LANES)), wide
+    )
+    side, gather, place = call(
+        near_kernel,
+        (shape(FACE, LANES), shape(2, 256, 512, dtype=BF), shape(256, 256, dtype=BF)),
+        first,
+        near,
+        targets,
+        ylow,
+        yhigh,
+        owner_index.reshape(1, 32),
+    )
+    flow, volumes, base, sides, end_gather = call(
         flow_kernel,
-        (shape(3, 128, LANES), shape(32, 24, LANES, dtype=BF)),
+        (
+            shape(3, 128, LANES),
+            shape(32, 24, LANES, dtype=BF),
+            state,
+            shape(2 * FACE, LANES),
+            shape(256, 512, dtype=BF),
+        ),
         wide,
         own,
         zlow,
         zhigh,
         place,
+        middle,
+        sums,
+        first,
+        base,
+        near,
+        side,
         scratch=[
             pltpu.VMEM((3, 8, 384), F32),
             pltpu.VMEM((2, 3, 20, 16, LANES), F32),
@@ -843,18 +960,6 @@
         ],
     )
     arrived = lax.all_to_all(volumes, ("gy", "gz"), split_axis=0, concat_axis=0, tiled=True)
-    base, sides, gather = call(
-        near_kernel,
-        (state, shape(2 * FACE, LANES), shape(3, 256, 512, dtype=BF)),
-        first,
-        base,
-        near,
-        targets,
-        ylow,
-        yhigh,
-        zlow,
-        zhigh,
-    )
     low, high, cells = call(
         send_kernel, (face, face, shape(256, 256, dtype=BF)), arrived, gather, faces, base
     )
@@ -864,6 +969,7 @@
         (shape(*acoustic.shape), shape(2, LANES, LANES), shape(3, 128, LANES)),
         arrived,
         gather,
+        end_gather,
         table,
         faces,
         cells,
@@ -872,9 +978,9 @@
         column,
         back,
         flow,
-        far_out=(0,),
+        far_out=(0, 2),
         scratch=[pltpu.VMEM((ROWS, LANES), F32)] * 3
-        + [pltpu.VMEM(acoustic.shape, F32), pltpu.SemaphoreType.DMA],
+        + [pltpu.VMEM((32, 4, 2 * LANES), F32), pltpu.SemaphoreType.DMA((2,))],
     )
     out = call(
         last_kernel,
@@ -887,7 +993,7 @@
         far_in=(0,),
         far_out=(0,),
         alias={0: 0},
-        scratch=[pltpu.VMEM((2, 32, 4, LANES), F32), pltpu.SemaphoreType.DMA((2,))],
+        scratch=[pltpu.VMEM((2, 32, 4, LANES), F32), pltpu.SemaphoreType.DMA((2 * PARTS,))],
     )
     return flow.reshape(3, 16, 8, LANES), out
 

time: 50.7 us -> 46.6 us (0.919)
  blocking collectives: 0 us -> 13.8 us
  waiting for transfers between devices: 13.9 us -> 5.08 us
  starting transfers between devices: 23.4 us -> 17.5 us
  local copies, waits for them, and re-layouts: 2.71 us -> 0.68 us
  other arithmetic: 0.84 us -> 0 us
    all_to_all x0 -> x1, blocking collectives: none -> 13.8 us  [on_device(): lax.all_to_all(volumes, ('gy', 'gz'), split_axis=0, concat_axis=0, tiled=...]
    all_to_all x1 -> x0, waiting for transfers between devices: 7.86 us -> none  [on_device(): lax.all_to_all(volumes, ('gy', 'gz'), split_axis=0, concat_axis=0, tiled=...]
    all_to_all x1 -> x0, starting transfers between devices: 6.44 us -> none  [on_device(): lax.all_to_all(volumes, ('gy', 'gz'), split_axis=0, concat_axis=0, tiled=...]
    unnamed x18 -> x14, local copies, waits for them, and re-layouts: 2.55 us -> 0.68 us
    ppermute x8, waiting for transfers between devices: 6.08 us -> 5.08 us  [both_ways(): return (lax.ppermute(high, axis, up), lax.ppermute(low, axis, down))]
    convert_element_type x2 -> x0, other arithmetic: 0.54 us -> none  [the longest x1 0.54 us: placement(): return fits.astype(BF)]
    pallas_call x9 -> x11, Pallas kernels: 8.76 us -> 8.71 us  [call(): pl.pallas_call(kernel, out_shape=out_shape, in_specs=[far if i in far_in...]
  transfers between devices with their start and end apart: 9 -> 8, of which waited for: 4 -> 2; matrix products, arithmetic and copies ran while one was open for 2% -> 0% of each run, Pallas kernels for 9% -> 10%
where the time goes in v2:
time: 46.6 us; the launch traced here: 46.5 us
  starting transfers between devices  17.5 us (38%)
  blocking collectives  13.8 us (30%)
  Pallas kernels  8.71 us (19%)
  waiting for transfers between devices  5.08 us (11%)
  between operations  0.82 us (2%)
  local copies, waits for them, and re-layouts  0.68 us (1%)
    ppermute x8, starting transfers between devices, both_ways(): return (lax.ppermute(high, axis, up), lax.ppermute(low, axis, down))  17.5 us
    all_to_all x1, blocking collectives, on_device(): lax.all_to_all(volumes, ('gy', 'gz'), split_axis=0, concat_axis=0, tiled=...  13.8 us
    pallas_call x11, Pallas kernels, call(): pl.pallas_call(kernel, out_shape=out_shape, in_specs=[far if i in far_in...  8.71 us
    ppermute x8, waiting for transfers between devices, both_ways(): return (lax.ppermute(high, axis, up), lax.ppermute(low, axis, down))  5.08 us
  transfers between devices with their start and end apart: 8, of which 2 were waited for; matrix products, arithmetic and copies ran while one was open for 0% of the time, Pallas kernels for 10%

profile of v2, /device:TPU:1, one launch (start us, length us, event | category | flops | bytes accessed | tf_op | source)
XLA Modules:
  0.0 46.5 jit_solution(3523347730055825780)
XLA Ops:
  0.7 1.0 %shard_map.86 = (bf16[2,48,128]{2,1,0:T(8,128)(2,1)S(1)}, bf16[128,128]{1,0:T(8,128)(2,1)S(1)}) custom-call(f32[3,128,128]{2,1,0:T(8,128)} %bitcast.3, f32[32,4,512]{2,1,0:T(4,128)} %acoustic_ref.3), custom_call_target="tpu_custom_call" | custom-call | flops 1000000 | bytes 1000000 | tf_op jit(solution)/shard_map/pallas_call | solution.py:91
  1.7 0.0 copy-start.2
  1.7 0.3 shard_map.87
  2.0 2.5 %collective-permute-start = (bf16[112,128]{1,0:T(8,128)(2,1)S(1)}, bf16[112,128]{1,0:T(8,128)(2,1)S(1)}, u32[]{:S(2)}, u32[]{:S(2)}) collective-permute-start(bf16[112,128]{1,0:T(8,128)(2,1)S(1)} %get-tuple-element.40), channel_id=1, source_target_pairs={{0,32},{32,64},{64,96},{96,128},{128,160},{160,192},{192,224},{224... | collective-permute-start | bytes 86024 | tf_op jit(solution)/shard_map/ppermute | solution.py:850
  4.5 4.0 %collective-permute-start.1 = (bf16[112,128]{1,0:T(8,128)(2,1)S(1)}, bf16[112,128]{1,0:T(8,128)(2,1)S(1)}, u32[]{:S(2)}, u32[]{:S(2)}) collective-permute-start(bf16[112,128]{1,0:T(8,128)(2,1)S(1)} %get-tuple-element.41), channel_id=1, source_target_pairs={{32,0},{64,32},{96,64},{128,96},{160,128},{192,160},{224,192},{0,2... | collective-permute-start | bytes 86024 | tf_op jit(solution)/shard_map/ppermute | solution.py:850
  8.6 0.0 copy-start
  8.6 1.3 %shard_map.88 = (f32[512,128]{1,0:T(8,128)S(1)}, f32[512,128]{1,0:T(8,128)S(1)}, bf16[128,128]{1,0:T(8,128)(2,1)S(1)}, bf16[512,256]{1,0:T(8,128)(2,1)S(1)}, bf1...) custom-call(f32[32,4,512]{2,1,0:T(4,128)S(1)} %copy-done.1, bf16[128,128]{1,0:T(8,128)(2,1)S(1)} %get-tuple-element.42.place_ref, ...), custom_call_target="tpu_custom_call" | custom-call | flops 1000000 | bytes 1000000 | tf_op jit(solution)/shard_map/pallas_call | solution.py:91
  9.9 0.2 shard_map.89
  10.1 4.0 %collective-permute-start.2 = (bf16[208,128]{1,0:T(8,128)(2,1)S(1)}, bf16[208,128]{1,0:T(8,128)(2,1)S(1)}, u32[]{:S(2)}, u32[]{:S(2)}) collective-permute-start(bf16[208,128]{1,0:T(8,128)(2,1)S(1)} %get-tuple-element.46), channel_id=1, source_target_pairs={{0,8},{8,16},{16,24},{24,0},{1,9},{9,17},{17,25},{25,1},{2,10},{10... | collective-permute-start | bytes 159752 | tf_op jit(solution)/shard_map/ppermute | solution.py:850
  14.1 1.2 %collective-permute-done.2.ylow_ref = bf16[208,128]{1,0:T(8,128)(2,1)S(1)} collective-permute-done((bf16[208,128]{1,0:T(8,128)(2,1)S(1)}, bf16[208,128]{1,0:T(8,128)(2,1)S(1)}, u32[]{:S(2)}, u32[]{:S(2)}) %collective-permute-start.2) | collective-permute-done | bytes 53280 | tf_op jit(solution)/shard_map/ppermute | solution.py:850
  15.4 3.8 %collective-permute-done.3.yhigh_ref = bf16[208,128]{1,0:T(8,128)(2,1)S(1)} collective-permute-done((bf16[208,128]{1,0:T(8,128)(2,1)S(1)}, bf16[208,128]{1,0:T(8,128)(2,1)S(1)}, u32[]{:S(2)}, u32[]{:S(2)}) %collective-permute-start.3) | collective-permute-done | bytes 53280 | tf_op jit(solution)/shard_map/ppermute | solution.py:850
  19.2 0.3 shard_map.90
  19.5 1.4 %collective-permute-start.4 = (bf16[96,128]{1,0:T(8,128)(2,1)S(1)}, bf16[96,128]{1,0:T(8,128)(2,1)S(1)}, u32[]{:S(2)}, u32[]{:S(2)}) collective-permute-start(bf16[96,128]{1,0:T(8,128)(2,1)S(1)} %get-tuple-element.51), channel_id=1, source_target_pairs={{0,1},{1,2},{2,3},{3,4},{4,5},{5,6},{6,7},{7,0},{8,9},{9,10},{10,1... | collective-permute-start | bytes 73736 | tf_op jit(solution)/shard_map/ppermute | solution.py:850
  20.9 2.3 %collective-permute-start.5 = (bf16[96,128]{1,0:T(8,128)(2,1)S(1)}, bf16[96,128]{1,0:T(8,128)(2,1)S(1)}, u32[]{:S(2)}, u32[]{:S(2)}) collective-permute-start(bf16[96,128]{1,0:T(8,128)(2,1)S(1)} %get-tuple-element.52), channel_id=1, source_target_pairs={{1,0},{2,1},{3,2},{4,3},{5,4},{6,5},{7,6},{0,7},{9,8},{10,9},{11,1... | collective-permute-start | bytes 73736 | tf_op jit(solution)/shard_map/ppermute | solution.py:850
  23.2 0.5 %shard_map.92 = (f32[3,20,16,128]{3,2,1,0:T(8,128)S(1)}, f32[2,96,128]{2,1,0:T(8,128)S(1)}) custom-call(f32[3,20,16,128]{3,2,1,0:T(8,128)S(1)} %get-tuple-element.49.wide_ref), custom_call_target="tpu_custom_call" | custom-call | flops 1000000 | bytes 1000000 | tf_op jit(solution)/shard_map/pallas_call | solution.py:91
  23.7 0.6 %copy-done.6 = s32[32,1]{0,1:T(1,128)S(1)} copy-done((s32[32,1]{0,1:T(1,128)S(1)}, s32[32,1]{0,1:T(1,128)}, u32[]{:S(2)}) %copy-start.6) | copy-done | bytes 152
  24.4 0.6 %shard_map.91 = (f32[64,128]{1,0:T(8,128)S(1)}, bf16[2,256,512]{2,1,0:T(8,128)(2,1)S(1)}, bf16[256,256]{1,0:T(8,128)(2,1)S(1)}) custom-call(f32[512,128]{1,0:T(8,128)S(1)} %get-tuple-element.43.state_ref, f32[128,128]{1,0:T(8,128)S(1)} %get-tuple-element.53.near_ref, f32[1,128]{1,0:T(1,128)S(1)} %get-tuple-element.45.targets_ref, ...), custom_call_target="tpu_custom_call" | custom-call | flops 1000000 | bytes 1000000 | tf_op jit(solution)/shard_map/pallas_call | solution.py:91
  25.0 1.1 %shard_map.93 = (f32[3,128,128]{2,1,0:T(8,128)S(1)}, bf16[32,24,128]{2,1,0:T(8,128)(2,1)S(1)}, f32[512,128]{1,0:T(8,128)S(1)}, f32[128,128]{1,0:T(8,128)S(1)}, bf16[256,512]{1,0:T(8,128)(2,1)S(1)}) custom-call(f32[3,20,16,128]{3,2,1,0:T(8,128)S(1)} %get-tuple-element.49.wide_ref, f32[3,8,384]{2,1,0:T(8,128)S(1)} %get-tuple-element.50.own_ref, ...), custom_call_target="tpu_custom_call" | custom-call | flops 1000000 | bytes 1000000 | tf_op jit(solution)/shard_map/pallas_call | solution.py:91
  26.1 13.8 %all_to_all.5.arrived_ref = bf16[32,24,128]{2,1,0:T(8,128)(2,1)S(1)} all-to-all(bf16[32,24,128]{2,1,0:T(8,128)(2,1)S(1)} %get-tuple-element.59), channel_id=1, replica_groups=mesh['gx'=8,'gy'=4,'gz'=8] {'gy','gz'}, dimensions={0} | all-to-all | bytes 393216 | tf_op jit(solution)/shard_map/all_to_all | solution.py:962
  39.8 0.4 shard_map.94
  40.2 0.1 collective-permute-start.6
  40.3 3.1 %collective-permute-start.7 = (bf16[64,128]{1,0:T(8,128)(2,1)S(1)}, bf16[64,128]{1,0:T(8,128)(2,1)S(1)}, u32[]{:S(2)}, u32[]{:S(2)}) collective-permute-start(bf16[64,128]{1,0:T(8,128)(2,1)S(1)} %get-tuple-element.73), channel_id=1, source_target_pairs={{32,0},{64,32},{96,64},{128,96},{160,128},{192,160},{224,192},{0,2... | collective-permute-start | bytes 49160 | tf_op jit(solution)/shard_map/ppermute | solution.py:850
  43.4 2.0 %shard_map.95 = (f32[32,4,512]{2,1,0:T(4,128)}, f32[2,128,128]{2,1,0:T(8,128)S(1)}, f32[3,128,128]{2,1,0:T(8,128)}) custom-call(bf16[32,24,128]{2,1,0:T(8,128)(2,1)S(1)} %all_to_all.5.arrived_ref, bf16[2,256,512]{2,1,0:T(8,128)(2,1)S(1)} %get-tuple-element.60.gather_ref, bf16[256,512]{1,0:T(8,128)(2,1)S(1)} %get-tuple-element.61.end_gather_ref, ...), custom_call_target="tpu_custom_call" | custom-call | flops 1000000 | bytes 1000000 | tf_op jit(solution)/shard_map/pallas_call | solution.py:91
  45.4 1.1 %shard_map.96 = f32[32,4,512]{2,1,0:T(4,128)} custom-call(f32[32,4,512]{2,1,0:T(4,128)} %get-tuple-element.70.main_ref, f32[2,128,128]{2,1,0:T(8,128)S(1)} %get-tuple-element.71.ends_ref, bf16[128,128]{1,0:T(8,128)(2,1)S(1)} %get-tuple-element.67.back_ref, bf16[64,128]{1,0:T(8,128)(2,1)S(1)} %collective-permute-done.6.low_ref, ...), custom_call_target="tpu_custom_call", output_to_operand_aliasing={{}: (0, {})} | custom-call | flops 1000000 | bytes 1000000 | tf_op jit(solution)/shard_map/pallas_call | solution.py:91
  (18 shorter events, 0.0 us)
Async XLA Ops:
  0.6 1.1 %copy-start.4 = (s32[1,32]{1,0:T(1,128)S(1)}, s32[1,32]{1,0:T(1,128)}, u32[]{:S(2)}) copy-start(s32[1,32]{1,0:T(1,128)} %cell_ref.3) | copy-start | bytes 388
  0.6 7.9 %copy-start.1 = (f32[32,4,512]{2,1,0:T(4,128)S(1)}, f32[32,4,512]{2,1,0:T(4,128)}, u32[]{:S(2)}) copy-start(f32[32,4,512]{2,1,0:T(4,128)} %acoustic_ref.3) | copy-start | bytes 786436
  0.7 7.9 %copy-start.3 = (f32[64,512]{1,0:T(8,128)S(1)}, f32[64,512]{1,0:T(8,128)}, u32[]{:S(2)}) copy-start(f32[64,512]{1,0:T(8,128)} %projection_ref.1) | copy-start | bytes 393220
  1.7 6.9 %copy-start.2 = (f32[64,128]{1,0:T(8,128)S(1)}, f32[64,128]{1,0:T(8,128)}, u32[]{:S(2)}) copy-start(f32[64,128]{1,0:T(8,128)} %constant.2.clone.column_ref) | copy-start | bytes 98308
  2.0 7.9 %collective-permute-start = (bf16[112,128]{1,0:T(8,128)(2,1)S(1)}, bf16[112,128]{1,0:T(8,128)(2,1)S(1)}, u32[]{:S(2)}, u32[]{:S(2)}) collective-permute-start(bf16[112,128]{1,0:T(8,128)(2,1)S(1)} %get-tuple-element.40), channel_id=1, source_target_pairs={{0,32},{32,64},{64,96},{96,128},{128,160},{160,192},{192,224},{224... | collective-permute-start | bytes 86024 | tf_op jit(solution)/shard_map/ppermute | solution.py:850
  4.5 4.1 %copy-start.5 = (s32[1,64]{1,0:T(1,128)S(1)}, s32[1,64]{1,0:T(1,128)}, u32[]{:S(2)}) copy-start(s32[1,64]{1,0:T(1,128)} %slot_ref.1) | copy-start | bytes 772
  4.5 5.4 %collective-permute-start.1 = (bf16[112,128]{1,0:T(8,128)(2,1)S(1)}, bf16[112,128]{1,0:T(8,128)(2,1)S(1)}, u32[]{:S(2)}, u32[]{:S(2)}) collective-permute-start(bf16[112,128]{1,0:T(8,128)(2,1)S(1)} %get-tuple-element.41), channel_id=1, source_target_pairs={{32,0},{64,32},{96,64},{128,96},{160,128},{192,160},{224,192},{0,2... | collective-permute-start | bytes 86024 | tf_op jit(solution)/shard_map/ppermute | solution.py:850
  8.6 1.3 %copy-start = (f32[3,16,8,128]{3,2,1,0:T(8,128)S(1)}, f32[3,16,8,128]{3,2,1,0:T(8,128)}, u32[]{:S(2)}) copy-start(f32[3,16,8,128]{3,2,1,0:T(8,128)} %param.7) | copy-start | bytes 589828
  10.1 5.2 %collective-permute-start.2 = (bf16[208,128]{1,0:T(8,128)(2,1)S(1)}, bf16[208,128]{1,0:T(8,128)(2,1)S(1)}, u32[]{:S(2)}, u32[]{:S(2)}) collective-permute-start(bf16[208,128]{1,0:T(8,128)(2,1)S(1)} %get-tuple-element.46), channel_id=1, source_target_pairs={{0,8},{8,16},{16,24},{24,0},{1,9},{9,17},{17,25},{25,1},{2,10},{10... | collective-permute-start | bytes 159752 | tf_op jit(solution)/shard_map/ppermute | solution.py:850
  14.1 5.1 %collective-permute-start.3 = (bf16[208,128]{1,0:T(8,128)(2,1)S(1)}, bf16[208,128]{1,0:T(8,128)(2,1)S(1)}, u32[]{:S(2)}, u32[]{:S(2)}) collective-permute-start(bf16[208,128]{1,0:T(8,128)(2,1)S(1)} %get-tuple-element.47), channel_id=1, source_target_pairs={{8,0},{16,8},{24,16},{0,24},{9,1},{17,9},{25,17},{1,25},{10,2},{18... | collective-permute-start | bytes 159752 | tf_op jit(solution)/shard_map/ppermute | solution.py:850
  19.5 5.5 %collective-permute-start.4 = (bf16[96,128]{1,0:T(8,128)(2,1)S(1)}, bf16[96,128]{1,0:T(8,128)(2,1)S(1)}, u32[]{:S(2)}, u32[]{:S(2)}) collective-permute-start(bf16[96,128]{1,0:T(8,128)(2,1)S(1)} %get-tuple-element.51), channel_id=1, source_target_pairs={{0,1},{1,2},{2,3},{3,4},{4,5},{5,6},{6,7},{7,0},{8,9},{9,10},{10,1... | collective-permute-start | bytes 73736 | tf_op jit(solution)/shard_map/ppermute | solution.py:850
  20.9 4.1 %collective-permute-start.5 = (bf16[96,128]{1,0:T(8,128)(2,1)S(1)}, bf16[96,128]{1,0:T(8,128)(2,1)S(1)}, u32[]{:S(2)}, u32[]{:S(2)}) collective-permute-start(bf16[96,128]{1,0:T(8,128)(2,1)S(1)} %get-tuple-element.52), channel_id=1, source_target_pairs={{1,0},{2,1},{3,2},{4,3},{5,4},{6,5},{7,6},{0,7},{9,8},{10,9},{11,1... | collective-permute-start | bytes 73736 | tf_op jit(solution)/shard_map/ppermute | solution.py:850
  23.7 0.7 %copy-start.6 = (s32[32,1]{0,1:T(1,128)S(1)}, s32[32,1]{0,1:T(1,128)}, u32[]{:S(2)}) copy-start(s32[32,1]{0,1:T(1,128)} %param.10) | copy-start | bytes 388
  40.2 5.2 %collective-permute-start.6 = (bf16[64,128]{1,0:T(8,128)(2,1)S(1)}, bf16[64,128]{1,0:T(8,128)(2,1)S(1)}, u32[]{:S(2)}, u32[]{:S(2)}) collective-permute-start(bf16[64,128]{1,0:T(8,128)(2,1)S(1)} %get-tuple-element.72), channel_id=1, source_target_pairs={{0,32},{32,64},{64,96},{96,128},{128,160},{160,192},{192,224},{224... | collective-permute-start | bytes 49160 | tf_op jit(solution)/shard_map/ppermute | solution.py:850
  40.3 5.2 %collective-permute-start.7 = (bf16[64,128]{1,0:T(8,128)(2,1)S(1)}, bf16[64,128]{1,0:T(8,128)(2,1)S(1)}, u32[]{:S(2)}, u32[]{:S(2)}) collective-permute-start(bf16[64,128]{1,0:T(8,128)(2,1)S(1)} %get-tuple-element.73), channel_id=1, source_target_pairs={{32,0},{64,32},{96,64},{128,96},{160,128},{192,160},{224,192},{0,2... | collective-permute-start | bytes 49160 | tf_op jit(solution)/shard_map/ppermute | solution.py:850

commit v3 on v2

--- a/solution.py
+++ b/solution.py
@@ -20,7 +20,7 @@
 GAIN = WAVE_STEP * SOURCE_GAIN
 LIFT = WAVE_STEP * 0.5 * ORDER * (ORDER + 1) / 2.0
 XV = 48
-YV = 144
+YV = 120
 PARTS = 1
 START_GRANT = 56_440_000
 ZV = 32
@@ -270,24 +270,48 @@
     place_ref,
     cell_ref,
     slot_ref,
-    projection_ref,
     column_ref,
     state_ref,
     base_ref,
-    back_ref,
-    table_ref,
-    faces_ref,
     targets_ref,
-    scratch,
 ):
     slots = jnp.broadcast_to(jnp.concatenate([slot_ref[...]] * 2, axis=1), (32, LANES))
     named = jnp.where(slots == iota((32, LANES), 0), 1.0, 0.0).astype(BF)
     cells = jnp.broadcast_to(cell_ref[...], (16, 32)).astype(F32).astype(BF)
     targets_ref[...] = nn(cells, named)[0:1]
     place = place_ref[...]
-    back_ref[...] = jnp.transpose(place.astype(F32)).astype(BF)
     high, low = split2(stored_rows(acoustic_ref))
     state_ref[...] = jnp.transpose(nn(place, high) + nn(place, low))
+    volume_part(state_ref, base_ref, column_ref)
+    for axis in (1, 2):
+        add_pair(base_ref, axis, *inside_lifts(axis, *face_pair(state_ref, axis)))
+
+
+def chunk_matrix(rows, low_row, high_row):
+    row, column = iota((rows, 9 * LANES), 0), iota((rows, 9 * LANES), 1)
+    chunk, lane = column // LANES, column % LANES
+    fits = ((row == low_row(chunk)) & (lane == 0)) | ((row == high_row(chunk)) & (lane == 127))
+    return jnp.where(fits, 1.0, 0.0).astype(BF)
+
+
+def table_kernel(
+    order_ref,
+    chosen_ref,
+    projection_ref,
+    owner_ref,
+    back_ref,
+    table_ref,
+    faces_ref,
+    place_ref,
+    first_ref,
+    second_ref,
+    scratch,
+):
+    del order_ref
+    back_ref[...] = jnp.transpose(chosen_ref[...].astype(F32)).astype(BF)
+    place_ref[...] = placement(owner_ref)
+    first_ref[...] = chunk_matrix(2 * ZV, lambda m: 2 * m + 1, lambda m: ZV + 2 * m)
+    second_ref[...] = chunk_matrix(80, lambda m: 8 * m + 1, lambda m: 8 * m + 6)
     high, low = split2(projection_ref[...])
     row, column = iota((64, 64), 0), iota((64, 64), 1)
     order = jnp.where(column == (row % 16) * 4 + row // 16, 1.0, 0.0).astype(BF)
@@ -301,9 +325,6 @@
         for axis in range(3):
             for side, face in enumerate(face_pair(scratch.at[i], axis)):
                 faces_ref[2 * axis + side, :, lane] = face.astype(BF)
-    volume_part(state_ref, base_ref, column_ref)
-    for axis in (1, 2):
-        add_pair(base_ref, axis, *inside_lifts(axis, *face_pair(state_ref, axis)))
 
 
 def y_kernel(
@@ -331,13 +352,13 @@
         high_lift(0, own_high - xhigh_ref[XV:, :].astype(F32)),
     )
     faces = packed(1, face_pair(state_ref, 1), face_pair(out_ref, 1))
-    spare = jnp.concatenate([targets_ref[...], jnp.zeros((3, LANES), F32)], axis=0)
-    for side, (out, first) in enumerate(((low_ref, 0), (high_ref, 6))):
+    spare = jnp.concatenate([targets_ref[...], jnp.zeros((5, LANES), F32)], axis=0)
+    for side, (out, near, far) in enumerate(((low_ref, 0, 1), (high_ref, 7, 6))):
         pieces = []
-        for y in range(2):
-            for c in range(3):
-                pieces.append(wide[c, pl.ds(first + y, 20, stride=8), :])
-                pieces.append(spare)
+        for c in range(3):
+            pieces.append(wide[c, pl.ds(8 + near, 18, stride=8), :])
+            pieces.append(spare)
+            pieces.append(wide[c, pl.ds(16 + far, 16, stride=8), :])
         out[0:YV, :] = jnp.concatenate(pieces, axis=0).astype(BF)
         out[YV:, :] = faces[side]
 
@@ -362,6 +383,7 @@
 
 
 def z_kernel(
+    order_ref,
     velocity_ref,
     xlow_ref,
     xhigh_ref,
@@ -378,6 +400,7 @@
     near_ref,
     held,
 ):
+    del order_ref
     held[0] = ylow_ref[0:YV, :].astype(F32)
     held[1] = yhigh_ref[0:YV, :].astype(F32)
     for c in range(3):
@@ -388,10 +411,13 @@
             wide_ref[c, 18 + x, 2:10, :] = high[x * 8 : x * 8 + 8]
         for x in range(16):
             wide_ref[c, 2 + x, 2:10, :] = velocity_ref[c, x * 8 : x * 8 + 8, :]
-        for y in range(2):
-            for side in range(2):
-                rows = held[side, y * 72 + c * 24 : y * 72 + c * 24 + 20, :]
-                wide_ref[c, :, y + 10 * side, :] = rows
+        for x in (0, 1, 18, 19):
+            wide_ref[c, x, 0:2, :] = jnp.zeros((2, LANES), F32)
+            wide_ref[c, x, 10:12, :] = jnp.zeros((2, LANES), F32)
+        for side in range(2):
+            at = c * 40
+            wide_ref[c, 1:19, 1 + 9 * side, :] = held[side, at : at + 18, :]
+            wide_ref[c, 2:18, 11 * side, :] = held[side, at + 24 : at + 40, :]
         wide_ref[c, :, 12:16, :] = jnp.zeros((20, 4, LANES), F32)
     row, column = iota((16, LANES), 0), iota((16, LANES), 1)
     picks = ((row < 2) & (column == row)) | ((row >= 2) & (row < 4) & (column == row + 124))
@@ -518,13 +544,11 @@
     inner_sums_ref,
     state_ref,
     base_ref,
-    near_ref,
-    side_ref,
+    first_ref,
+    second_ref,
     out_ref,
     volume_ref,
     base_out_ref,
-    sides_ref,
-    gather_ref,
     ends,
     halo,
     middle,
@@ -539,18 +563,18 @@
             ends[c, 0:2, lane] = low[at : at + 2]
             ends[c, 2:6, lane] = own_ref[c, 0:4, lane]
             ends[c, 6:8, lane] = high[at : at + 2]
-    row, column = iota((16, LANES), 0), iota((16, LANES), 1)
-    spots = ((row == 1) & (column == 0)) | ((row == 6) & (column == 127))
-    spots = jnp.where(spots, 1.0, 0.0).astype(BF)
-    zeros = jnp.zeros((8, 384), F32)
-
-    def spread_out(values, level):
+
+    def spread_out(rows, spots, level):
+        values = tn(rows, spots)
         for c in range(3):
-            both = jnp.concatenate([values[c], zeros], axis=0).astype(BF)
-            halo[level, c] = tn(both, spots)[0:320].reshape(20, 16, LANES)
-
+            for j in range(3):
+                at = (3 * c + j) * LANES
+                part = values[:, at : at + LANES].reshape(8, 16, LANES)
+                halo[level, c, j * 8 : j * 8 + 8] = part
+
+    both = jnp.concatenate([zlow_ref[0:ZV, :], zhigh_ref[0:ZV, :]], axis=0)
+    spread_out(both, first_ref[...], 0)
     edge = [ends[c] for c in range(3)]
-    spread_out(edge, 0)
     edge_low = [
         [roll(e, 16, 1) for e in edge],
         [roll(e, 1, 1) for e in edge],
@@ -561,20 +585,13 @@
         [roll(e, -1, 1) for e in edge],
         [roll(e, -1, 0) for e in edge],
     ]
-    spread_out(
-        moved_on(edge, edge_low, edge_high, differences(edge_low, edge_high)), 1
-    )
-    end_faces(
-        state_ref,
-        base_ref,
-        near_ref,
-        side_ref,
-        zlow_ref,
-        zhigh_ref,
-        base_out_ref,
-        sides_ref,
-        gather_ref,
-    )
+    new = moved_on(edge, edge_low, edge_high, differences(edge_low, edge_high))
+    rows = [new[c][:, j * LANES : j * LANES + LANES] for c in range(3) for j in range(3)]
+    rows = jnp.concatenate(rows + [jnp.zeros((8, LANES), F32)], axis=0)
+    spread_out(rows.astype(BF), second_ref[...], 1)
+    trace, _ = joined(2, zlow_ref[ZV:, :], zhigh_ref[ZV:, :])
+    base_out_ref[...] = base_ref[...]
+    add_pair(base_out_ref, 2, *boundary_lifts(2, *face_pair(state_ref, 2), trace))
 
     def sign(dims):
         return jnp.where(iota(dims, len(dims) - 1) == 0, -1.0, 1.0)
@@ -678,29 +695,21 @@
     return jnp.where(fits, 1.0, 0.0).astype(BF)
 
 
-def near_kernel(
-    state_ref, near_ref, targets_ref, ylow_ref, yhigh_ref, owner_ref, sides_ref, gather_ref, place_ref
-):
-    place_ref[...] = placement(owner_ref)
+def near_kernel(state_ref, near_ref, targets_ref, ylow_ref, yhigh_ref, sides_ref, gather_ref):
     sides_ref[...] = near_ref[FACE:, :] + near_lift(1, near_ref[0:FACE, :], *face_pair(state_ref, 1))
     groups = [
         gather_matrix(targets_ref[...]),
-        gather_matrix(line(ylow_ref, 20), line(yhigh_ref, 20), cut_of(1, (256, LANES))[1]),
+        gather_matrix(line(ylow_ref, 18), line(yhigh_ref, 18), cut_of(1, (256, LANES))[1]),
     ]
     for g, parts in enumerate(groups):
         for z in range(4):
             gather_ref[g, :, z * LANES : z * LANES + LANES] = parts[z]
 
 
-def end_faces(
-    state_ref, base_ref, near_ref, side_ref, zlow_ref, zhigh_ref, out_ref, sides_ref, gather_ref
-):
+def end_faces(state_ref, near_ref, side_ref, zlow_ref, zhigh_ref, sides_ref):
     trace, base = joined(2, zlow_ref[ZV:, :], zhigh_ref[ZV:, :])
-    own = face_pair(state_ref, 2)
-    out_ref[...] = base_ref[...]
-    add_pair(out_ref, 2, *boundary_lifts(2, *own, trace))
     sides_ref[0:FACE, :] = side_ref[...]
-    sides_ref[FACE:, :] = base + near_lift(2, trace, *own)
+    sides_ref[FACE:, :] = base + near_lift(2, trace, *face_pair(state_ref, 2))
     from_low = zlow_ref[0:ZV, :].astype(F32)[24:32]
     from_high = zhigh_ref[0:ZV, :].astype(F32)[24:32]
     at_low, at_high = cut_of(2, (K, LANES))
@@ -709,8 +718,7 @@
     jump = near_ref[pl.ds(K - 1, K, stride=K), :] - roll(from_high, 15, 1)
     sides_ref[pl.ds(K - 1, K, stride=K), :] += jnp.where(at_high, high_lift(2, jump), 0.0)
     parts = gather_matrix(line(zlow_ref, 18), line(zhigh_ref, 18), cut_of(2, (256, LANES))[1])
-    for z in range(4):
-        gather_ref[:, z * LANES : z * LANES + LANES] = parts[z]
+    return jnp.concatenate(parts, axis=1)
 
 
 def stacked(summed, starts):
@@ -756,18 +764,22 @@
 def second_kernel(
     arrived_ref,
     gather_ref,
-    end_gather_ref,
     table_ref,
     faces_ref,
     cells_ref,
     base_ref,
-    sides_ref,
+    first_ref,
+    near_ref,
+    side_ref,
+    zlow_ref,
+    zhigh_ref,
     column_ref,
     back_ref,
     flow_ref,
     out_ref,
     ends_ref,
     flow_out_ref,
+    sides_ref,
     state,
     extra,
     total,
@@ -776,13 +788,14 @@
 ):
     flow_copy = pltpu.make_async_copy(flow_ref, flow_out_ref, sems.at[0])
     flow_copy.start()
+    end_gather = end_faces(first_ref, near_ref, side_ref, zlow_ref, zhigh_ref, sides_ref)
     source = GAIN * nn(table_ref[...], cells_ref[...])
     state[...] = base_ref[...] - source[:, 0:LANES]
     extra[...] = source[:, LANES:]
     near = []
     for axis in (1, 2):
         rows = arrived_ref[:, 8 * axis : 8 * axis + 8, :].reshape(256, LANES)
-        gather = gather_ref[1] if axis == 1 else end_gather_ref[...]
+        gather = gather_ref[1] if axis == 1 else end_gather
         cells = stacked(tn(rows, gather), (by_side(axis),))
         at_low, at_high = cut_of(axis, (FACE, LANES))
         face = jnp.where(
@@ -818,11 +831,9 @@
 def last_kernel(
     main_ref, ends_ref, back_ref, low_ref, high_ref, out_ref, held, sems
 ):
-    low, high = low_ref[...].astype(F32), high_ref[...].astype(F32)
-    parts = jnp.concatenate([-low_lift(0, low), -high_lift(0, high)], axis=0)
-    high, low = split2(jnp.transpose(parts))
-    back = back_ref[...]
-    rows = nn(back, high) + nn(back, low)
+    rows = nt(back_ref[...], jnp.concatenate([low_ref[...], high_ref[...]], axis=0))
+    across = jnp.concatenate([rows[32:64], rows[0:32], jnp.zeros((64, LANES), F32)], axis=0)
+    rows = LIFT * (rows + jnp.where(iota((LANES, LANES), 1) < FACE, across, -across))
     left = iota((LANES, LANES), 1) < FACE
     copies = []
     for side, tile in ((0, 0), (1, 3)):
@@ -873,23 +884,14 @@
     chosen = shape(LANES, LANES, dtype=BF)
     xlow, xhigh, chosen = call(start_kernel, (send, send, chosen), lines, faces, element_cell)
     xlow, xhigh = both_ways(xlow, xhigh, "gx")
-    first, base, back, table, faces, targets = call(
+    first, base, targets = call(
         prepare_kernel,
-        (
-            state,
-            state,
-            shape(LANES, LANES, dtype=BF),
-            shape(ROWS, 256, dtype=BF),
-            shape(6, FACE, 256, dtype=BF),
-            shape(1, LANES),
-        ),
+        (state, state, shape(1, LANES)),
         acoustic,
         chosen,
         element_cell,
         slot_element,
-        projection,
         column,
-        scratch=[pltpu.VMEM((2, ROWS, LANES), F32)],
     )
     send = shape(YV + FACE, LANES, dtype=BF)
     ylow, yhigh, base = call(
@@ -904,10 +906,28 @@
         scratch=[pltpu.VMEM((3, 160, LANES), F32)],
     )
     ylow, yhigh = both_ways(ylow, yhigh, "gy")
+    back, table, faces, place, spots, later_spots = call(
+        table_kernel,
+        (
+            shape(LANES, LANES, dtype=BF),
+            shape(ROWS, 256, dtype=BF),
+            shape(6, FACE, 256, dtype=BF),
+            shape(256, 256, dtype=BF),
+            shape(2 * ZV, 9 * LANES, dtype=BF),
+            shape(80, 9 * LANES, dtype=BF),
+        ),
+        base,
+        chosen,
+        projection,
+        owner_index.reshape(1, 32),
+        far_in=(0,),
+        scratch=[pltpu.VMEM((2, ROWS, LANES), F32)],
+    )
     send = shape(ZV + FACE, LANES, dtype=BF)
     wide, own, zlow, zhigh, base, near = call(
         z_kernel,
         (shape(3, 20, 16, LANES), shape(3, 8, 384), send, send, state, shape(2 * FACE, LANES)),
+        spots,
         velocity,
         xlow,
         xhigh,
@@ -916,31 +936,25 @@
         first,
         base,
         targets,
+        far_in=(0,),
         scratch=[pltpu.VMEM((2, YV, LANES), F32)],
     )
     zlow, zhigh = both_ways(zlow, zhigh, "gz")
     middle, sums = call(
         inner_flow_kernel, (shape(3, 20, 16, LANES), shape(2, 96, LANES)), wide
     )
-    side, gather, place = call(
+    side, gather = call(
         near_kernel,
-        (shape(FACE, LANES), shape(2, 256, 512, dtype=BF), shape(256, 256, dtype=BF)),
+        (shape(FACE, LANES), shape(2, 256, 512, dtype=BF)),
         first,
         near,
         targets,
         ylow,
         yhigh,
-        owner_index.reshape(1, 32),
-    )
-    flow, volumes, base, sides, end_gather = call(
+    )
+    flow, volumes, base = call(
         flow_kernel,
-        (
-            shape(3, 128, LANES),
-            shape(32, 24, LANES, dtype=BF),
-            state,
-            shape(2 * FACE, LANES),
-            shape(256, 512, dtype=BF),
-        ),
+        (shape(3, 128, LANES), shape(32, 24, LANES, dtype=BF), state),
         wide,
         own,
         zlow,
@@ -950,15 +964,16 @@
         sums,
         first,
         base,
-        near,
-        side,
+        spots,
+        later_spots,
         scratch=[
             pltpu.VMEM((3, 8, 384), F32),
-            pltpu.VMEM((2, 3, 20, 16, LANES), F32),
+            pltpu.VMEM((2, 3, 24, 16, LANES), F32),
             pltpu.VMEM((3, 20, 16, LANES), F32),
             pltpu.VMEM((2, 192, LANES), F32),
         ],
     )
+    volumes, side, gather = lax.optimization_barrier((volumes, side, gather))
     arrived = lax.all_to_all(volumes, ("gy", "gz"), split_axis=0, concat_axis=0, tiled=True)
     low, high, cells = call(
         send_kernel, (face, face, shape(256, 256, dtype=BF)), arrived, gather, faces, base
@@ -969,17 +984,21 @@
         (shape(*acoustic.shape), shape(2, LANES, LANES), shape(3, 128, LANES)),
         arrived,
         gather,
-        end_gather,
         table,
         faces,
         cells,
         base,
-        sides,
+        first,
+        near,
+        side,
+        zlow,
+        zhigh,
         column,
         back,
         flow,
         far_out=(0, 2),
-        scratch=[pltpu.VMEM((ROWS, LANES), F32)] * 3
+        scratch=[pltpu.VMEM((2 * FACE, LANES), F32)]
+        + [pltpu.VMEM((ROWS, LANES), F32)] * 3
         + [pltpu.VMEM((32, 4, 2 * LANES), F32), pltpu.SemaphoreType.DMA((2,))],
     )
     out = call(

time: 46.6 us -> 46.4 us (level)
  waiting for transfers between devices: 5.08 us -> 3.83 us
  blocking collectives: 13.8 us -> 14.4 us
    ppermute x8, waiting for transfers between devices: 5.08 us -> 3.83 us  [both_ways(): return (lax.ppermute(high, axis, up), lax.ppermute(low, axis, down))]
    all_to_all x1, blocking collectives: 13.8 us -> 14.4 us  [on_device(): lax.all_to_all(volumes, ('gy', 'gz'), split_axis=0, concat_axis=0, tiled=...]
    pallas_call x11 -> x12, Pallas kernels: 8.71 us -> 8.96 us  [call(): pl.pallas_call(kernel, out_shape=out_shape, in_specs=[far if i in far_in...]
  transfers between devices with their start and end apart: 8 -> 8, of which waited for: 2 -> 2; matrix products, arithmetic and copies ran while one was open for 0% -> 0% of each run, Pallas kernels for 10% -> 11%
where the time goes in v3:
time: 46.4 us; the launch traced here: 46.2 us
  starting transfers between devices  17.6 us (38%)
  blocking collectives  14.4 us (31%)
  Pallas kernels  8.96 us (19%)
  waiting for transfers between devices  3.83 us (8%)
  between operations  0.78 us (2%)
  local copies, waits for them, and re-layouts  0.68 us (1%)
    ppermute x8, starting transfers between devices, both_ways(): return (lax.ppermute(high, axis, up), lax.ppermute(low, axis, down))  17.6 us
    all_to_all x1, blocking collectives, on_device(): lax.all_to_all(volumes, ('gy', 'gz'), split_axis=0, concat_axis=0, tiled=...  14.4 us
    pallas_call x12, Pallas kernels, call(): pl.pallas_call(kernel, out_shape=out_shape, in_specs=[far if i in far_in...  8.96 us
    ppermute x8, waiting for transfers between devices, both_ways(): return (lax.ppermute(high, axis, up), lax.ppermute(low, axis, down))  3.83 us
  transfers between devices with their start and end apart: 8, of which 2 were waited for; matrix products, arithmetic and copies ran while one was open for 0% of the time, Pallas kernels for 11%

profile of v3, /device:TPU:1, one launch (start us, length us, event | category | flops | bytes accessed | tf_op | source)
XLA Modules:
  0.0 46.2 jit_solution(5259967196702805469)
XLA Ops:
  0.7 1.0 %shard_map.86 = (bf16[2,48,128]{2,1,0:T(8,128)(2,1)S(1)}, bf16[128,128]{1,0:T(8,128)(2,1)S(1)}) custom-call(f32[3,128,128]{2,1,0:T(8,128)} %bitcast.3, f32[32,4,512]{2,1,0:T(4,128)} %acoustic_ref.3), custom_call_target="tpu_custom_call" | custom-call | flops 1000000 | bytes 1000000 | tf_op jit(solution)/shard_map/pallas_call | solution.py:91
  1.7 0.3 shard_map.87
  2.0 2.5 %collective-permute-start = (bf16[112,128]{1,0:T(8,128)(2,1)S(1)}, bf16[112,128]{1,0:T(8,128)(2,1)S(1)}, u32[]{:S(2)}, u32[]{:S(2)}) collective-permute-start(bf16[112,128]{1,0:T(8,128)(2,1)S(1)} %get-tuple-element.43), channel_id=1, source_target_pairs={{0,32},{32,64},{64,96},{96,128},{128,160},{160,192},{192,224},{224... | collective-permute-start | bytes 86024 | tf_op jit(solution)/shard_map/ppermute | solution.py:861
  4.6 4.0 %collective-permute-start.1 = (bf16[112,128]{1,0:T(8,128)(2,1)S(1)}, bf16[112,128]{1,0:T(8,128)(2,1)S(1)}, u32[]{:S(2)}, u32[]{:S(2)}) collective-permute-start(bf16[112,128]{1,0:T(8,128)(2,1)S(1)} %get-tuple-element.44), channel_id=1, source_target_pairs={{32,0},{64,32},{96,64},{128,96},{160,128},{192,160},{224,192},{0,2... | collective-permute-start | bytes 86024 | tf_op jit(solution)/shard_map/ppermute | solution.py:861
  8.6 1.1 %shard_map.88 = (f32[512,128]{1,0:T(8,128)S(1)}, f32[512,128]{1,0:T(8,128)S(1)}, f32[1,128]{1,0:T(1,128)S(1)}) custom-call(f32[32,4,512]{2,1,0:T(4,128)S(1)} %copy-done.1, bf16[128,128]{1,0:T(8,128)(2,1)S(1)} %get-tuple-element.45.place_ref.chosen_ref, s32[1,32]{1,0:T(1,128)S(1)} %copy-done.4, s32[1,64]{1,0:T(1,128)S(1)} %copy-done.5, f32[64,128]{1,0:T(8,128)S(1)} %copy-done.2), custom_call_target="tpu_custom_call" | custom-call | flops 1000000 | bytes 1000000 | tf_op jit(solution)/shard_map/pallas_call | solution.py:91
  9.7 0.0 collective-permute-done.xlow_ref
  9.8 0.2 shard_map.89
  9.9 4.2 %collective-permute-start.2 = (bf16[184,128]{1,0:T(8,128)(2,1)S(1)}, bf16[184,128]{1,0:T(8,128)(2,1)S(1)}, u32[]{:S(2)}, u32[]{:S(2)}) collective-permute-start(bf16[184,128]{1,0:T(8,128)(2,1)S(1)} %get-tuple-element.51), channel_id=1, source_target_pairs={{0,8},{8,16},{16,24},{24,0},{1,9},{9,17},{17,25},{25,1},{2,10},{10... | collective-permute-start | bytes 141320 | tf_op jit(solution)/shard_map/ppermute | solution.py:861
  14.2 0.7 %copy-done.6 = s32[32,1]{0,1:T(1,128)S(1)} copy-done((s32[32,1]{0,1:T(1,128)S(1)}, s32[32,1]{0,1:T(1,128)}, u32[]{:S(2)}) %copy-start.6) | copy-done | bytes 152
  14.8 1.0 %shard_map.90 = (bf16[128,128]{1,0:T(8,128)(2,1)S(1)}, bf16[512,256]{1,0:T(8,128)(2,1)S(1)}, bf16[6,64,256]{2,1,0:T(8,128)(2,1)S(1)}, bf16[256,256]{1,0:T(8,128)...) custom-call(f32[512,128]{1,0:T(8,128)S(1)} %get-tuple-element.49.order_ref.base_ref, ...), custom_call_target="tpu_custom_call" | custom-call | flops 1000000 | bytes 1000000 | tf_op jit(solution)/shard_map/pallas_call | solution.py:91
  15.8 3.4 %collective-permute-done.3.yhigh_ref = bf16[184,128]{1,0:T(8,128)(2,1)S(1)} collective-permute-done((bf16[184,128]{1,0:T(8,128)(2,1)S(1)}, bf16[184,128]{1,0:T(8,128)(2,1)S(1)}, u32[]{:S(2)}, u32[]{:S(2)}) %collective-permute-start.3) | collective-permute-done | bytes 47136 | tf_op jit(solution)/shard_map/ppermute | solution.py:861
  19.2 0.3 shard_map.91
  19.5 1.4 %collective-permute-start.4 = (bf16[96,128]{1,0:T(8,128)(2,1)S(1)}, bf16[96,128]{1,0:T(8,128)(2,1)S(1)}, u32[]{:S(2)}, u32[]{:S(2)}) collective-permute-start(bf16[96,128]{1,0:T(8,128)(2,1)S(1)} %get-tuple-element.55), channel_id=1, source_target_pairs={{0,1},{1,2},{2,3},{3,4},{4,5},{5,6},{6,7},{7,0},{8,9},{9,10},{10,1... | collective-permute-start | bytes 73736 | tf_op jit(solution)/shard_map/ppermute | solution.py:861
  20.9 2.3 %collective-permute-start.5 = (bf16[96,128]{1,0:T(8,128)(2,1)S(1)}, bf16[96,128]{1,0:T(8,128)(2,1)S(1)}, u32[]{:S(2)}, u32[]{:S(2)}) collective-permute-start(bf16[96,128]{1,0:T(8,128)(2,1)S(1)} %get-tuple-element.56), channel_id=1, source_target_pairs={{1,0},{2,1},{3,2},{4,3},{5,4},{6,5},{7,6},{0,7},{9,8},{10,9},{11,1... | collective-permute-start | bytes 73736 | tf_op jit(solution)/shard_map/ppermute | solution.py:861
  23.1 0.5 %shard_map.92 = (f32[3,20,16,128]{3,2,1,0:T(8,128)S(1)}, f32[2,96,128]{2,1,0:T(8,128)S(1)}) custom-call(f32[3,20,16,128]{3,2,1,0:T(8,128)S(1)} %get-tuple-element.53.wide_ref), custom_call_target="tpu_custom_call" | custom-call | flops 1000000 | bytes 1000000 | tf_op jit(solution)/shard_map/pallas_call | solution.py:91
  23.7 0.3 shard_map.94
  23.9 0.4 collective-permute-done.4.zlow_ref
  24.4 0.9 %shard_map.93 = (f32[3,128,128]{2,1,0:T(8,128)S(1)}, bf16[32,24,128]{2,1,0:T(8,128)(2,1)S(1)}, f32[512,128]{1,0:T(8,128)S(1)}) custom-call(f32[3,20,16,128]{3,2,1,0:T(8,128)S(1)} %get-tuple-element.53.wide_ref, f32[3,8,384]{2,1,0:T(8,128)S(1)} %get-tuple-element.54.own_ref, bf16[96,128]{1,0:T(8,128)(2,1)S(1)} %collective-permute-done.4.zlow_ref, ...), custom_call_target="tpu_custom_call" | custom-call | flops 1000000 | bytes 1000000 | tf_op jit(solution)/shard_map/pallas_call | solution.py:91
  25.2 14.4 %all_to_all.5.arrived_ref = bf16[32,24,128]{2,1,0:T(8,128)(2,1)S(1)} all-to-all(bf16[32,24,128]{2,1,0:T(8,128)(2,1)S(1)} %get-tuple-element.66), channel_id=1, replica_groups=mesh['gx'=8,'gy'=4,'gz'=8] {'gy','gz'}, dimensions={0} | all-to-all | bytes 393216 | tf_op jit(solution)/shard_map/all_to_all | solution.py:977
  39.6 0.4 shard_map.95
  39.9 0.1 collective-permute-start.6
  40.0 3.1 %collective-permute-start.7 = (bf16[64,128]{1,0:T(8,128)(2,1)S(1)}, bf16[64,128]{1,0:T(8,128)(2,1)S(1)}, u32[]{:S(2)}, u32[]{:S(2)}) collective-permute-start(bf16[64,128]{1,0:T(8,128)(2,1)S(1)} %get-tuple-element.79), channel_id=1, source_target_pairs={{32,0},{64,32},{96,64},{128,96},{160,128},{192,160},{224,192},{0,2... | collective-permute-start | bytes 49160 | tf_op jit(solution)/shard_map/ppermute | solution.py:861
  43.1 2.2 %shard_map.96 = (f32[32,4,512]{2,1,0:T(4,128)}, f32[2,128,128]{2,1,0:T(8,128)S(1)}, f32[3,128,128]{2,1,0:T(8,128)}) custom-call(bf16[32,24,128]{2,1,0:T(8,128)(2,1)S(1)} %all_to_all.5.arrived_ref, bf16[2,256,512]{2,1,0:T(8,128)(2,1)S(1)} %get-tuple-element.67.gather_ref, bf16[512,256]{1,0:T(8,128)(2,1)S(1)} %get-tuple-element.68.table_ref, ...), custom_call_target="tpu_custom_call" | custom-call | flops 1000000 | bytes 1000000 | tf_op jit(solution)/shard_map/pallas_call | solution.py:91
  45.3 0.9 %shard_map.97 = f32[32,4,512]{2,1,0:T(4,128)} custom-call(f32[32,4,512]{2,1,0:T(4,128)} %get-tuple-element.76.main_ref, f32[2,128,128]{2,1,0:T(8,128)S(1)} %get-tuple-element.77.ends_ref, bf16[128,128]{1,0:T(8,128)(2,1)S(1)} %get-tuple-element.73.back_ref, bf16[64,128]{1,0:T(8,128)(2,1)S(1)} %collective-permute-done.6.low_ref, ...), custom_call_target="tpu_custom_call", output_to_operand_aliasing={{}: (0, {})} | custom-call | flops 1000000 | bytes 1000000 | tf_op jit(solution)/shard_map/pallas_call | solution.py:91
  (19 shorter events, 0.0 us)
Async XLA Ops:
  0.6 1.1 %copy-start.4 = (s32[1,32]{1,0:T(1,128)S(1)}, s32[1,32]{1,0:T(1,128)}, u32[]{:S(2)}) copy-start(s32[1,32]{1,0:T(1,128)} %cell_ref.3) | copy-start | bytes 388
  0.6 7.9 %copy-start.1 = (f32[32,4,512]{2,1,0:T(4,128)S(1)}, f32[32,4,512]{2,1,0:T(4,128)}, u32[]{:S(2)}) copy-start(f32[32,4,512]{2,1,0:T(4,128)} %acoustic_ref.3) | copy-start | bytes 786436
  0.7 7.9 %copy-start.5 = (s32[1,64]{1,0:T(1,128)S(1)}, s32[1,64]{1,0:T(1,128)}, u32[]{:S(2)}) copy-start(s32[1,64]{1,0:T(1,128)} %slot_ref.1) | copy-start | bytes 772
  1.7 6.9 %copy-start.2 = (f32[64,128]{1,0:T(8,128)S(1)}, f32[64,128]{1,0:T(8,128)}, u32[]{:S(2)}) copy-start(f32[64,128]{1,0:T(8,128)} %constant.2.clone.column_ref) | copy-start | bytes 98308
  1.7 8.0 %copy-start = (f32[3,16,8,128]{3,2,1,0:T(8,128)S(1)}, f32[3,16,8,128]{3,2,1,0:T(8,128)}, u32[]{:S(2)}) copy-start(f32[3,16,8,128]{3,2,1,0:T(8,128)} %param.7) | copy-start | bytes 589828
  2.0 7.7 %collective-permute-start = (bf16[112,128]{1,0:T(8,128)(2,1)S(1)}, bf16[112,128]{1,0:T(8,128)(2,1)S(1)}, u32[]{:S(2)}, u32[]{:S(2)}) collective-permute-start(bf16[112,128]{1,0:T(8,128)(2,1)S(1)} %get-tuple-element.43), channel_id=1, source_target_pairs={{0,32},{32,64},{64,96},{96,128},{128,160},{160,192},{192,224},{224... | collective-permute-start | bytes 86024 | tf_op jit(solution)/shard_map/ppermute | solution.py:861
  4.6 5.2 %collective-permute-start.1 = (bf16[112,128]{1,0:T(8,128)(2,1)S(1)}, bf16[112,128]{1,0:T(8,128)(2,1)S(1)}, u32[]{:S(2)}, u32[]{:S(2)}) collective-permute-start(bf16[112,128]{1,0:T(8,128)(2,1)S(1)} %get-tuple-element.44), channel_id=1, source_target_pairs={{32,0},{64,32},{96,64},{128,96},{160,128},{192,160},{224,192},{0,2... | collective-permute-start | bytes 86024 | tf_op jit(solution)/shard_map/ppermute | solution.py:861
  9.8 4.4 %copy-start.3 = (f32[64,512]{1,0:T(8,128)S(1)}, f32[64,512]{1,0:T(8,128)}, u32[]{:S(2)}) copy-start(f32[64,512]{1,0:T(8,128)} %projection_ref.1) | copy-start | bytes 393220
  9.9 5.9 %collective-permute-start.2 = (bf16[184,128]{1,0:T(8,128)(2,1)S(1)}, bf16[184,128]{1,0:T(8,128)(2,1)S(1)}, u32[]{:S(2)}, u32[]{:S(2)}) collective-permute-start(bf16[184,128]{1,0:T(8,128)(2,1)S(1)} %get-tuple-element.51), channel_id=1, source_target_pairs={{0,8},{8,16},{16,24},{24,0},{1,9},{9,17},{17,25},{25,1},{2,10},{10... | collective-permute-start | bytes 141320 | tf_op jit(solution)/shard_map/ppermute | solution.py:861
  14.2 5.0 %collective-permute-start.3 = (bf16[184,128]{1,0:T(8,128)(2,1)S(1)}, bf16[184,128]{1,0:T(8,128)(2,1)S(1)}, u32[]{:S(2)}, u32[]{:S(2)}) collective-permute-start(bf16[184,128]{1,0:T(8,128)(2,1)S(1)} %get-tuple-element.52), channel_id=1, source_target_pairs={{8,0},{16,8},{24,16},{0,24},{9,1},{17,9},{25,17},{1,25},{10,2},{18... | collective-permute-start | bytes 141320 | tf_op jit(solution)/shard_map/ppermute | solution.py:861
  14.2 0.7 %copy-start.6 = (s32[32,1]{0,1:T(1,128)S(1)}, s32[32,1]{0,1:T(1,128)}, u32[]{:S(2)}) copy-start(s32[32,1]{0,1:T(1,128)} %param.10) | copy-start | bytes 388
  19.5 4.9 %collective-permute-start.4 = (bf16[96,128]{1,0:T(8,128)(2,1)S(1)}, bf16[96,128]{1,0:T(8,128)(2,1)S(1)}, u32[]{:S(2)}, u32[]{:S(2)}) collective-permute-start(bf16[96,128]{1,0:T(8,128)(2,1)S(1)} %get-tuple-element.55), channel_id=1, source_target_pairs={{0,1},{1,2},{2,3},{3,4},{4,5},{5,6},{6,7},{7,0},{8,9},{9,10},{10,1... | collective-permute-start | bytes 73736 | tf_op jit(solution)/shard_map/ppermute | solution.py:861
  20.9 3.5 %collective-permute-start.5 = (bf16[96,128]{1,0:T(8,128)(2,1)S(1)}, bf16[96,128]{1,0:T(8,128)(2,1)S(1)}, u32[]{:S(2)}, u32[]{:S(2)}) collective-permute-start(bf16[96,128]{1,0:T(8,128)(2,1)S(1)} %get-tuple-element.56), channel_id=1, source_target_pairs={{1,0},{2,1},{3,2},{4,3},{5,4},{6,5},{7,6},{0,7},{9,8},{10,9},{11,1... | collective-permute-start | bytes 73736 | tf_op jit(solution)/shard_map/ppermute | solution.py:861
  39.9 5.4 %collective-permute-start.6 = (bf16[64,128]{1,0:T(8,128)(2,1)S(1)}, bf16[64,128]{1,0:T(8,128)(2,1)S(1)}, u32[]{:S(2)}, u32[]{:S(2)}) collective-permute-start(bf16[64,128]{1,0:T(8,128)(2,1)S(1)} %get-tuple-element.78), channel_id=1, source_target_pairs={{0,32},{32,64},{64,96},{96,128},{128,160},{160,192},{192,224},{224... | collective-permute-start | bytes 49160 | tf_op jit(solution)/shard_map/ppermute | solution.py:861
  40.0 5.3 %collective-permute-start.7 = (bf16[64,128]{1,0:T(8,128)(2,1)S(1)}, bf16[64,128]{1,0:T(8,128)(2,1)S(1)}, u32[]{:S(2)}, u32[]{:S(2)}) collective-permute-start(bf16[64,128]{1,0:T(8,128)(2,1)S(1)} %get-tuple-element.79), channel_id=1, source_target_pairs={{32,0},{64,32},{96,64},{128,96},{160,128},{192,160},{224,192},{0,2... | collective-permute-start | bytes 49160 | tf_op jit(solution)/shard_map/ppermute | solution.py:861

commit v4 on v3

--- a/solution.py
+++ b/solution.py
@@ -19,11 +19,11 @@
 SOURCE_GAIN = 25.0
 GAIN = WAVE_STEP * SOURCE_GAIN
 LIFT = WAVE_STEP * 0.5 * ORDER * (ORDER + 1) / 2.0
-XV = 48
-YV = 120
+XV = 96
+YV = 240
 PARTS = 1
 START_GRANT = 56_440_000
-ZV = 32
+ZV = 64
 
 
 def legendre_table(points, order):
@@ -62,6 +62,11 @@
     return high, (value - high.astype(F32)).astype(BF)
 
 
+def restored(ref, rows, first, count):
+    high = ref[first : first + count, :].astype(F32)
+    return high + ref[rows // 2 + first : rows // 2 + first + count, :].astype(F32)
+
+
 def nn(a, b):
     return lax.dot_general(a, b, (((1,), (0,)), ((), ())), preferred_element_type=F32)
 
@@ -206,7 +211,19 @@
         ref[pl.ds(K - 1, FACE, stride=K), :] += high
 
 
-def volume_part(state_ref, out_ref, column_ref, extra_ref=None):
+def derivative_columns():
+    row = iota((K, LANES), 0)
+    columns = []
+    for m in range(K):
+        column = jnp.zeros((K, LANES), F32)
+        for b in range(K):
+            column = jnp.where(row == b, float(DERIV[b, m]), column)
+        columns.append(column)
+    return columns
+
+
+def volume_part(state_ref, out_ref, extra_ref=None):
+    columns = derivative_columns()
     for a in range(K):
         rows = [state_ref[a * FACE + b * K : a * FACE + b * K + K, :] for b in range(K)]
         along_y = [swapped(r, 1) for r in rows]
@@ -219,7 +236,7 @@
             for m in range(K):
                 total = total + float(DERIV[b, m]) * along_y[m]
             for m in range(K):
-                total = total + column_ref[m * K : m * K + K, :] * jnp.broadcast_to(
+                total = total + columns[m] * jnp.broadcast_to(
                     along_z[b][m : m + 1, :], (K, LANES)
                 )
             out_ref[at : at + K, :] = total
@@ -252,7 +269,9 @@
         faces_ref[v * 32 : v * 32 + 32, :] = rows.astype(BF)
     for side in range(2):
         for c in range(3):
-            lines_ref[side, c * 16 : c * 16 + 16, :] = flow[side, c].astype(BF)
+            high, low = split2(flow[side, c])
+            lines_ref[side, c * 16 : c * 16 + 16, :] = high
+            lines_ref[side, XV // 2 + c * 16 : XV // 2 + c * 16 + 16, :] = low
 
 
 def start_kernel(lines_ref, faces_ref, cell_ref, low_ref, high_ref, place_ref):
@@ -270,7 +289,6 @@
     place_ref,
     cell_ref,
     slot_ref,
-    column_ref,
     state_ref,
     base_ref,
     targets_ref,
@@ -282,16 +300,21 @@
     place = place_ref[...]
     high, low = split2(stored_rows(acoustic_ref))
     state_ref[...] = jnp.transpose(nn(place, high) + nn(place, low))
-    volume_part(state_ref, base_ref, column_ref)
+    volume_part(state_ref, base_ref)
     for axis in (1, 2):
         add_pair(base_ref, axis, *inside_lifts(axis, *face_pair(state_ref, axis)))
 
 
-def chunk_matrix(rows, low_row, high_row):
-    row, column = iota((rows, 9 * LANES), 0), iota((rows, 9 * LANES), 1)
-    chunk, lane = column // LANES, column % LANES
-    fits = ((row == low_row(chunk)) & (lane == 0)) | ((row == high_row(chunk)) & (lane == 127))
-    return jnp.where(fits, 1.0, 0.0).astype(BF)
+def chunk_matrix(out_ref, held, low_rows, high_rows):
+    rows = out_ref.shape[0]
+    held[0:rows, :] = jnp.zeros((rows, 9 * LANES), F32)
+    lane = iota((1, LANES), 1)
+    for places, at in ((low_rows, 0), (high_rows, LANES - 1)):
+        spot = jnp.where(lane == at, 1.0, 0.0)
+        for m in range(9):
+            for row in places(m):
+                held[row : row + 1, m * LANES : m * LANES + LANES] = spot
+    out_ref[...] = held[0:rows, :].astype(BF)
 
 
 def table_kernel(
@@ -306,12 +329,24 @@
     first_ref,
     second_ref,
     scratch,
+    held,
 ):
     del order_ref
     back_ref[...] = jnp.transpose(chosen_ref[...].astype(F32)).astype(BF)
     place_ref[...] = placement(owner_ref)
-    first_ref[...] = chunk_matrix(2 * ZV, lambda m: 2 * m + 1, lambda m: ZV + 2 * m)
-    second_ref[...] = chunk_matrix(80, lambda m: 8 * m + 1, lambda m: 8 * m + 6)
+    half = ZV // 2
+    chunk_matrix(
+        first_ref,
+        held,
+        lambda m: (2 * m + 1, half + 2 * m + 1),
+        lambda m: (ZV + 2 * m, ZV + half + 2 * m),
+    )
+    chunk_matrix(
+        second_ref,
+        held,
+        lambda m: (8 * m + 1, 80 + 8 * m + 1),
+        lambda m: (8 * m + 6, 80 + 8 * m + 6),
+    )
     high, low = split2(projection_ref[...])
     row, column = iota((64, 64), 0), iota((64, 64), 1)
     order = jnp.where(column == (row % 16) * 4 + row // 16, 1.0, 0.0).astype(BF)
@@ -340,9 +375,9 @@
     wide,
 ):
     for c in range(3):
-        wide[c, 0:16, :] = xlow_ref[c * 16 : c * 16 + 16, :].astype(F32)
+        wide[c, 0:16, :] = restored(xlow_ref, XV, c * 16, 16)
         wide[c, 16:144, :] = velocity_ref[c]
-        wide[c, 144:160, :] = xhigh_ref[c * 16 : c * 16 + 16, :].astype(F32)
+        wide[c, 144:160, :] = restored(xhigh_ref, XV, c * 16, 16)
     own_low, own_high = face_pair(state_ref, 0)
     out_ref[...] = base_ref[...]
     add_pair(
@@ -359,7 +394,9 @@
             pieces.append(wide[c, pl.ds(8 + near, 18, stride=8), :])
             pieces.append(spare)
             pieces.append(wide[c, pl.ds(16 + far, 16, stride=8), :])
-        out[0:YV, :] = jnp.concatenate(pieces, axis=0).astype(BF)
+        high, low = split2(jnp.concatenate(pieces, axis=0))
+        out[0 : YV // 2, :] = high
+        out[YV // 2 : YV, :] = low
         out[YV:, :] = faces[side]
 
 
@@ -401,11 +438,11 @@
     held,
 ):
     del order_ref
-    held[0] = ylow_ref[0:YV, :].astype(F32)
-    held[1] = yhigh_ref[0:YV, :].astype(F32)
+    held[0] = restored(ylow_ref, YV, 0, YV // 2)
+    held[1] = restored(yhigh_ref, YV, 0, YV // 2)
     for c in range(3):
-        low = xlow_ref[c * 16 : c * 16 + 16, :].astype(F32)
-        high = xhigh_ref[c * 16 : c * 16 + 16, :].astype(F32)
+        low = restored(xlow_ref, XV, c * 16, 16)
+        high = restored(xhigh_ref, XV, c * 16, 16)
         for x in range(2):
             wide_ref[c, x, 2:10, :] = low[x * 8 : x * 8 + 8]
             wide_ref[c, 18 + x, 2:10, :] = high[x * 8 : x * 8 + 8]
@@ -423,8 +460,8 @@
     picks = ((row < 2) & (column == row)) | ((row >= 2) & (row < 4) & (column == row + 124))
     picks = jnp.where(picks, 1.0, 0.0).astype(BF)
     for c in range(3):
-        rows = wide_ref[c].reshape(320, LANES).astype(BF)
-        own = nt(picks, rows)
+        high, low = split2(wide_ref[c].reshape(320, LANES))
+        own = nt(picks, high) + nt(picks, low)
         own_ref[c, :, 0:320] = own[0:8]
         own_ref[c, :, 320:384] = jnp.zeros((8, 64), F32)
     trace, base = joined(1, ylow_ref[YV:, :], yhigh_ref[YV:, :])
@@ -440,7 +477,9 @@
                 pieces.append(own_ref[c, first : first + 2, j * 128 : j * 128 + 128])
         pieces += [targets_ref[...], jnp.zeros((5, LANES), F32)]
         pieces.append(near_ref[pl.ds(side * (K - 1), K, stride=K), :])
-        out[0:ZV, :] = jnp.concatenate(pieces, axis=0).astype(BF)
+        high, low = split2(jnp.concatenate(pieces, axis=0))
+        out[0 : ZV // 2, :] = high
+        out[ZV // 2 : ZV, :] = low
         out[ZV:, :] = faces[side]
 
 
@@ -554,8 +593,8 @@
     middle,
     sums,
 ):
-    low = zlow_ref[0:ZV, :].astype(F32)
-    high = zhigh_ref[0:ZV, :].astype(F32)
+    low = restored(zlow_ref, ZV, 0, ZV // 2)
+    high = restored(zhigh_ref, ZV, 0, ZV // 2)
     for c in range(3):
         for j in range(3):
             lane = slice(j * 128, j * 128 + 128)
@@ -588,7 +627,7 @@
     new = moved_on(edge, edge_low, edge_high, differences(edge_low, edge_high))
     rows = [new[c][:, j * LANES : j * LANES + LANES] for c in range(3) for j in range(3)]
     rows = jnp.concatenate(rows + [jnp.zeros((8, LANES), F32)], axis=0)
-    spread_out(rows.astype(BF), second_ref[...], 1)
+    spread_out(jnp.concatenate(split2(rows), axis=0), second_ref[...], 1)
     trace, _ = joined(2, zlow_ref[ZV:, :], zhigh_ref[ZV:, :])
     base_out_ref[...] = base_ref[...]
     add_pair(base_out_ref, 2, *boundary_lifts(2, *face_pair(state_ref, 2), trace))
@@ -710,8 +749,8 @@
     trace, base = joined(2, zlow_ref[ZV:, :], zhigh_ref[ZV:, :])
     sides_ref[0:FACE, :] = side_ref[...]
     sides_ref[FACE:, :] = base + near_lift(2, trace, *face_pair(state_ref, 2))
-    from_low = zlow_ref[0:ZV, :].astype(F32)[24:32]
-    from_high = zhigh_ref[0:ZV, :].astype(F32)[24:32]
+    from_low = zlow_ref[0:32, :].astype(F32)[24:32]
+    from_high = zhigh_ref[0:32, :].astype(F32)[24:32]
     at_low, at_high = cut_of(2, (K, LANES))
     jump = near_ref[pl.ds(0, K, stride=K), :] - roll(from_low, -15, 1)
     sides_ref[pl.ds(0, K, stride=K), :] += jnp.where(at_low, low_lift(2, jump), 0.0)
@@ -773,7 +812,6 @@
     side_ref,
     zlow_ref,
     zhigh_ref,
-    column_ref,
     back_ref,
     flow_ref,
     out_ref,
@@ -804,7 +842,7 @@
             nn(faces_ref[2 * axis], cells),
         )
         near.append(sides_ref[(axis - 1) * FACE : axis * FACE, :] - GAIN * face)
-    volume_part(state, total, column_ref, extra)
+    volume_part(state, total, extra)
     for axis in (1, 2):
         own_low, own_high = face_pair(state, axis)
         low, high = outer(axis, own_low, own_high, near[axis - 1])
@@ -865,7 +903,6 @@
     velocity = velocity.reshape(3, 128, LANES)
     face = shape(FACE, LANES, dtype=BF)
     state = shape(ROWS, LANES)
-    column = jnp.asarray(np.broadcast_to(DERIV.T.reshape(FACE, 1), (FACE, LANES)), F32)
     send = shape(XV + FACE, LANES, dtype=BF)
     chosen = shape(LANES, LANES, dtype=BF)
     lines, faces = call(
@@ -891,7 +928,6 @@
         chosen,
         element_cell,
         slot_element,
-        column,
     )
     send = shape(YV + FACE, LANES, dtype=BF)
     ylow, yhigh, base = call(
@@ -914,14 +950,14 @@
             shape(6, FACE, 256, dtype=BF),
             shape(256, 256, dtype=BF),
             shape(2 * ZV, 9 * LANES, dtype=BF),
-            shape(80, 9 * LANES, dtype=BF),
+            shape(160, 9 * LANES, dtype=BF),
         ),
         base,
         chosen,
         projection,
         owner_index.reshape(1, 32),
         far_in=(0,),
-        scratch=[pltpu.VMEM((2, ROWS, LANES), F32)],
+        scratch=[pltpu.VMEM((2, ROWS, LANES), F32), pltpu.VMEM((160, 9 * LANES), F32)],
     )
     send = shape(ZV + FACE, LANES, dtype=BF)
     wide, own, zlow, zhigh, base, near = call(
@@ -937,7 +973,7 @@
         base,
         targets,
         far_in=(0,),
-        scratch=[pltpu.VMEM((2, YV, LANES), F32)],
+        scratch=[pltpu.VMEM((2, YV // 2, LANES), F32)],
     )
     zlow, zhigh = both_ways(zlow, zhigh, "gz")
     middle, sums = call(
@@ -993,7 +1029,6 @@
         side,
         zlow,
         zhigh,
-        column,
         back,
         flow,
         far_out=(0, 2),

time: 46.4 us -> 47.1 us (1.015)
  waiting for transfers between devices: 3.83 us -> 4.64 us
    ppermute x8, waiting for transfers between devices: 3.83 us -> 4.64 us  [both_ways(): return (lax.ppermute(high, axis, up), lax.ppermute(low, axis, down))]
  transfers between devices with their start and end apart: 8 -> 8, of which waited for: 2 -> 4; matrix products, arithmetic and copies ran while one was open for 0% -> 0% of each run, Pallas kernels for 11% -> 10%
where the time goes in v4:
time: 47.1 us; the launch traced here: 46.9 us
  starting transfers between devices  17.6 us (37%)
  blocking collectives  14.4 us (31%)
  Pallas kernels  8.76 us (19%)
  waiting for transfers between devices  4.64 us (10%)
  between operations  0.76 us (2%)
  local copies, waits for them, and re-layouts  0.68 us (1%)
    ppermute x8, starting transfers between devices, both_ways(): return (lax.ppermute(high, axis, up), lax.ppermute(low, axis, down))  17.6 us
    all_to_all x1, blocking collectives, on_device(): lax.all_to_all(volumes, ('gy', 'gz'), split_axis=0, concat_axis=0, tiled=...  14.4 us
    pallas_call x12, Pallas kernels, call(): pl.pallas_call(kernel, out_shape=out_shape, in_specs=[far if i in far_in...  8.76 us
    ppermute x8, waiting for transfers between devices, both_ways(): return (lax.ppermute(high, axis, up), lax.ppermute(low, axis, down))  4.64 us
  transfers between devices with their start and end apart: 8, of which 4 were waited for; matrix products, arithmetic and copies ran while one was open for 0% of the time, Pallas kernels for 10%

profile of v4, /device:TPU:1, one launch (start us, length us, event | category | flops | bytes accessed | tf_op | source)
XLA Modules:
  0.0 46.9 jit_solution(5485653777824444329)
XLA Ops:
  0.7 1.0 %shard_map.77 = (bf16[2,96,128]{2,1,0:T(8,128)(2,1)S(1)}, bf16[128,128]{1,0:T(8,128)(2,1)S(1)}) custom-call(f32[3,128,128]{2,1,0:T(8,128)} %bitcast.3, f32[32,4,512]{2,1,0:T(4,128)} %acoustic_ref.3), custom_call_target="tpu_custom_call" | custom-call | flops 1000000 | bytes 1000000 | tf_op jit(solution)/shard_map/pallas_call | solution.py:96
  1.7 0.3 shard_map.78
  2.0 2.5 %collective-permute-start = (bf16[160,128]{1,0:T(8,128)(2,1)S(1)}, bf16[160,128]{1,0:T(8,128)(2,1)S(1)}, u32[]{:S(2)}, u32[]{:S(2)}) collective-permute-start(bf16[160,128]{1,0:T(8,128)(2,1)S(1)} %get-tuple-element.43), channel_id=1, source_target_pairs={{0,32},{32,64},{64,96},{96,128},{128,160},{160,192},{192,224},{224... | collective-permute-start | bytes 122888 | tf_op jit(solution)/shard_map/ppermute | solution.py:899
  4.5 4.0 %collective-permute-start.1 = (bf16[160,128]{1,0:T(8,128)(2,1)S(1)}, bf16[160,128]{1,0:T(8,128)(2,1)S(1)}, u32[]{:S(2)}, u32[]{:S(2)}) collective-permute-start(bf16[160,128]{1,0:T(8,128)(2,1)S(1)} %get-tuple-element.44), channel_id=1, source_target_pairs={{32,0},{64,32},{96,64},{128,96},{160,128},{192,160},{224,192},{0,2... | collective-permute-start | bytes 122888 | tf_op jit(solution)/shard_map/ppermute | solution.py:899
  8.6 1.1 %shard_map.79 = (f32[512,128]{1,0:T(8,128)S(1)}, f32[512,128]{1,0:T(8,128)S(1)}, f32[1,128]{1,0:T(1,128)S(1)}) custom-call(f32[32,4,512]{2,1,0:T(4,128)S(1)} %copy-done.1, bf16[128,128]{1,0:T(8,128)(2,1)S(1)} %get-tuple-element.45.place_ref.chosen_ref, s32[1,32]{1,0:T(1,128)S(1)} %copy-done.3, s32[1,64]{1,0:T(1,128)S(1)} %copy-done.4), custom_call_target="tpu_custom_call" | custom-call | flops 1000000 | bytes 1000000 | tf_op jit(solution)/shard_map/pallas_call | solution.py:96
  9.7 0.2 collective-permute-done.xlow_ref
  9.9 0.2 shard_map.80
  10.1 4.2 %collective-permute-start.2 = (bf16[304,128]{1,0:T(8,128)(2,1)S(1)}, bf16[304,128]{1,0:T(8,128)(2,1)S(1)}, u32[]{:S(2)}, u32[]{:S(2)}) collective-permute-start(bf16[304,128]{1,0:T(8,128)(2,1)S(1)} %get-tuple-element.51), channel_id=1, source_target_pairs={{0,8},{8,16},{16,24},{24,0},{1,9},{9,17},{17,25},{25,1},{2,10},{10... | collective-permute-start | bytes 233480 | tf_op jit(solution)/shard_map/ppermute | solution.py:899
  14.3 0.7 %copy-done.5 = s32[32,1]{0,1:T(1,128)S(1)} copy-done((s32[32,1]{0,1:T(1,128)S(1)}, s32[32,1]{0,1:T(1,128)}, u32[]{:S(2)}) %copy-start.5) | copy-done | bytes 152
  15.0 0.7 %shard_map.81 = (bf16[128,128]{1,0:T(8,128)(2,1)S(1)}, bf16[512,256]{1,0:T(8,128)(2,1)S(1)}, bf16[6,64,256]{2,1,0:T(8,128)(2,1)S(1)}, bf16[256,256]{1,0:T(8,128)...) custom-call(f32[512,128]{1,0:T(8,128)S(1)} %get-tuple-element.49.order_ref.base_ref, ...), custom_call_target="tpu_custom_call" | custom-call | flops 1000000 | bytes 1000000 | tf_op jit(solution)/shard_map/pallas_call | solution.py:96
  15.7 3.9 %collective-permute-done.3.yhigh_ref = bf16[304,128]{1,0:T(8,128)(2,1)S(1)} collective-permute-done((bf16[304,128]{1,0:T(8,128)(2,1)S(1)}, bf16[304,128]{1,0:T(8,128)(2,1)S(1)}, u32[]{:S(2)}, u32[]{:S(2)}) %collective-permute-start.3) | collective-permute-done | bytes 77856 | tf_op jit(solution)/shard_map/ppermute | solution.py:899
  19.6 0.4 shard_map.82
  20.0 1.4 %collective-permute-start.4 = (bf16[128,128]{1,0:T(8,128)(2,1)S(1)}, bf16[128,128]{1,0:T(8,128)(2,1)S(1)}, u32[]{:S(2)}, u32[]{:S(2)}) collective-permute-start(bf16[128,128]{1,0:T(8,128)(2,1)S(1)} %get-tuple-element.55), channel_id=1, source_target_pairs={{0,1},{1,2},{2,3},{3,4},{4,5},{5,6},{6,7},{7,0},{8,9},{9,10},{10,1... | collective-permute-start | bytes 98312 | tf_op jit(solution)/shard_map/ppermute | solution.py:899
  21.4 2.3 %collective-permute-start.5 = (bf16[128,128]{1,0:T(8,128)(2,1)S(1)}, bf16[128,128]{1,0:T(8,128)(2,1)S(1)}, u32[]{:S(2)}, u32[]{:S(2)}) collective-permute-start(bf16[128,128]{1,0:T(8,128)(2,1)S(1)} %get-tuple-element.56), channel_id=1, source_target_pairs={{1,0},{2,1},{3,2},{4,3},{5,4},{6,5},{7,6},{0,7},{9,8},{10,9},{11,1... | collective-permute-start | bytes 98312 | tf_op jit(solution)/shard_map/ppermute | solution.py:899
  23.6 0.5 %shard_map.83 = (f32[3,20,16,128]{3,2,1,0:T(8,128)S(1)}, f32[2,96,128]{2,1,0:T(8,128)S(1)}) custom-call(f32[3,20,16,128]{3,2,1,0:T(8,128)S(1)} %get-tuple-element.53.wide_ref), custom_call_target="tpu_custom_call" | custom-call | flops 1000000 | bytes 1000000 | tf_op jit(solution)/shard_map/pallas_call | solution.py:96
  24.2 0.3 shard_map.85
  24.4 0.5 %collective-permute-done.4.zlow_ref = bf16[128,128]{1,0:T(8,128)(2,1)S(1)} collective-permute-done((bf16[128,128]{1,0:T(8,128)(2,1)S(1)}, bf16[128,128]{1,0:T(8,128)(2,1)S(1)}, u32[]{:S(2)}, u32[]{:S(2)}) %collective-permute-start.4) | collective-permute-done | bytes 32800 | tf_op jit(solution)/shard_map/ppermute | solution.py:899
  25.0 0.9 %shard_map.84 = (f32[3,128,128]{2,1,0:T(8,128)S(1)}, bf16[32,24,128]{2,1,0:T(8,128)(2,1)S(1)}, f32[512,128]{1,0:T(8,128)S(1)}) custom-call(f32[3,20,16,128]{3,2,1,0:T(8,128)S(1)} %get-tuple-element.53.wide_ref, f32[3,8,384]{2,1,0:T(8,128)S(1)} %get-tuple-element.54.own_ref, bf16[128,128]{1,0:T(8,128)(2,1)S(1)} %collective-permute-done.4.zlow_ref, ...), custom_call_target="tpu_custom_call" | custom-call | flops 1000000 | bytes 1000000 | tf_op jit(solution)/shard_map/pallas_call | solution.py:96
  25.8 14.4 %all_to_all.5.arrived_ref = bf16[32,24,128]{2,1,0:T(8,128)(2,1)S(1)} all-to-all(bf16[32,24,128]{2,1,0:T(8,128)(2,1)S(1)} %get-tuple-element.66), channel_id=1, replica_groups=mesh['gx'=8,'gy'=4,'gz'=8] {'gy','gz'}, dimensions={0} | all-to-all | bytes 393216 | tf_op jit(solution)/shard_map/all_to_all | solution.py:1013
  40.3 0.4 shard_map.86
  40.6 0.1 collective-permute-start.6
  40.7 3.1 %collective-permute-start.7 = (bf16[64,128]{1,0:T(8,128)(2,1)S(1)}, bf16[64,128]{1,0:T(8,128)(2,1)S(1)}, u32[]{:S(2)}, u32[]{:S(2)}) collective-permute-start(bf16[64,128]{1,0:T(8,128)(2,1)S(1)} %get-tuple-element.79), channel_id=1, source_target_pairs={{32,0},{64,32},{96,64},{128,96},{160,128},{192,160},{224,192},{0,2... | collective-permute-start | bytes 49160 | tf_op jit(solution)/shard_map/ppermute | solution.py:899
  43.8 2.1 %shard_map.87 = (f32[32,4,512]{2,1,0:T(4,128)}, f32[2,128,128]{2,1,0:T(8,128)S(1)}, f32[3,128,128]{2,1,0:T(8,128)}) custom-call(bf16[32,24,128]{2,1,0:T(8,128)(2,1)S(1)} %all_to_all.5.arrived_ref, bf16[2,256,512]{2,1,0:T(8,128)(2,1)S(1)} %get-tuple-element.67.gather_ref, bf16[512,256]{1,0:T(8,128)(2,1)S(1)} %get-tuple-element.68.table_ref, ...), custom_call_target="tpu_custom_call" | custom-call | flops 1000000 | bytes 1000000 | tf_op jit(solution)/shard_map/pallas_call | solution.py:96
  46.0 0.9 %shard_map.88 = f32[32,4,512]{2,1,0:T(4,128)} custom-call(f32[32,4,512]{2,1,0:T(4,128)} %get-tuple-element.76.main_ref, f32[2,128,128]{2,1,0:T(8,128)S(1)} %get-tuple-element.77.ends_ref, bf16[128,128]{1,0:T(8,128)(2,1)S(1)} %get-tuple-element.73.back_ref, bf16[64,128]{1,0:T(8,128)(2,1)S(1)} %collective-permute-done.6.low_ref, ...), custom_call_target="tpu_custom_call", output_to_operand_aliasing={{}: (0, {})} | custom-call | flops 1000000 | bytes 1000000 | tf_op jit(solution)/shard_map/pallas_call | solution.py:96
  (17 shorter events, 0.1 us)
Async XLA Ops:
  0.6 1.1 %copy-start.3 = (s32[1,32]{1,0:T(1,128)S(1)}, s32[1,32]{1,0:T(1,128)}, u32[]{:S(2)}) copy-start(s32[1,32]{1,0:T(1,128)} %cell_ref.3) | copy-start | bytes 388
  0.6 7.9 %copy-start.1 = (f32[32,4,512]{2,1,0:T(4,128)S(1)}, f32[32,4,512]{2,1,0:T(4,128)}, u32[]{:S(2)}) copy-start(f32[32,4,512]{2,1,0:T(4,128)} %acoustic_ref.3) | copy-start | bytes 786436
  0.7 7.9 %copy-start.4 = (s32[1,64]{1,0:T(1,128)S(1)}, s32[1,64]{1,0:T(1,128)}, u32[]{:S(2)}) copy-start(s32[1,64]{1,0:T(1,128)} %slot_ref.1) | copy-start | bytes 772
  1.7 8.2 %copy-start = (f32[3,16,8,128]{3,2,1,0:T(8,128)S(1)}, f32[3,16,8,128]{3,2,1,0:T(8,128)}, u32[]{:S(2)}) copy-start(f32[3,16,8,128]{3,2,1,0:T(8,128)} %param.6) | copy-start | bytes 589828
  2.0 7.9 %collective-permute-start = (bf16[160,128]{1,0:T(8,128)(2,1)S(1)}, bf16[160,128]{1,0:T(8,128)(2,1)S(1)}, u32[]{:S(2)}, u32[]{:S(2)}) collective-permute-start(bf16[160,128]{1,0:T(8,128)(2,1)S(1)} %get-tuple-element.43), channel_id=1, source_target_pairs={{0,32},{32,64},{64,96},{96,128},{128,160},{160,192},{192,224},{224... | collective-permute-start | bytes 122888 | tf_op jit(solution)/shard_map/ppermute | solution.py:899
  4.5 5.3 %collective-permute-start.1 = (bf16[160,128]{1,0:T(8,128)(2,1)S(1)}, bf16[160,128]{1,0:T(8,128)(2,1)S(1)}, u32[]{:S(2)}, u32[]{:S(2)}) collective-permute-start(bf16[160,128]{1,0:T(8,128)(2,1)S(1)} %get-tuple-element.44), channel_id=1, source_target_pairs={{32,0},{64,32},{96,64},{128,96},{160,128},{192,160},{224,192},{0,2... | collective-permute-start | bytes 122888 | tf_op jit(solution)/shard_map/ppermute | solution.py:899
  9.9 4.4 %copy-start.2 = (f32[64,512]{1,0:T(8,128)S(1)}, f32[64,512]{1,0:T(8,128)}, u32[]{:S(2)}) copy-start(f32[64,512]{1,0:T(8,128)} %projection_ref.1) | copy-start | bytes 393220
  10.1 5.7 %collective-permute-start.2 = (bf16[304,128]{1,0:T(8,128)(2,1)S(1)}, bf16[304,128]{1,0:T(8,128)(2,1)S(1)}, u32[]{:S(2)}, u32[]{:S(2)}) collective-permute-start(bf16[304,128]{1,0:T(8,128)(2,1)S(1)} %get-tuple-element.51), channel_id=1, source_target_pairs={{0,8},{8,16},{16,24},{24,0},{1,9},{9,17},{17,25},{25,1},{2,10},{10... | collective-permute-start | bytes 233480 | tf_op jit(solution)/shard_map/ppermute | solution.py:899
  14.3 5.3 %collective-permute-start.3 = (bf16[304,128]{1,0:T(8,128)(2,1)S(1)}, bf16[304,128]{1,0:T(8,128)(2,1)S(1)}, u32[]{:S(2)}, u32[]{:S(2)}) collective-permute-start(bf16[304,128]{1,0:T(8,128)(2,1)S(1)} %get-tuple-element.52), channel_id=1, source_target_pairs={{8,0},{16,8},{24,16},{0,24},{9,1},{17,9},{25,17},{1,25},{10,2},{18... | collective-permute-start | bytes 233480 | tf_op jit(solution)/shard_map/ppermute | solution.py:899
  14.3 0.7 %copy-start.5 = (s32[32,1]{0,1:T(1,128)S(1)}, s32[32,1]{0,1:T(1,128)}, u32[]{:S(2)}) copy-start(s32[32,1]{0,1:T(1,128)} %param.9) | copy-start | bytes 388
  20.0 5.0 %collective-permute-start.4 = (bf16[128,128]{1,0:T(8,128)(2,1)S(1)}, bf16[128,128]{1,0:T(8,128)(2,1)S(1)}, u32[]{:S(2)}, u32[]{:S(2)}) collective-permute-start(bf16[128,128]{1,0:T(8,128)(2,1)S(1)} %get-tuple-element.55), channel_id=1, source_target_pairs={{0,1},{1,2},{2,3},{3,4},{4,5},{5,6},{6,7},{7,0},{8,9},{9,10},{10,1... | collective-permute-start | bytes 98312 | tf_op jit(solution)/shard_map/ppermute | solution.py:899
  21.4 3.6 %collective-permute-start.5 = (bf16[128,128]{1,0:T(8,128)(2,1)S(1)}, bf16[128,128]{1,0:T(8,128)(2,1)S(1)}, u32[]{:S(2)}, u32[]{:S(2)}) collective-permute-start(bf16[128,128]{1,0:T(8,128)(2,1)S(1)} %get-tuple-element.56), channel_id=1, source_target_pairs={{1,0},{2,1},{3,2},{4,3},{5,4},{6,5},{7,6},{0,7},{9,8},{10,9},{11,1... | collective-permute-start | bytes 98312 | tf_op jit(solution)/shard_map/ppermute | solution.py:899
  40.6 5.3 %collective-permute-start.6 = (bf16[64,128]{1,0:T(8,128)(2,1)S(1)}, bf16[64,128]{1,0:T(8,128)(2,1)S(1)}, u32[]{:S(2)}, u32[]{:S(2)}) collective-permute-start(bf16[64,128]{1,0:T(8,128)(2,1)S(1)} %get-tuple-element.78), channel_id=1, source_target_pairs={{0,32},{32,64},{64,96},{96,128},{128,160},{160,192},{192,224},{224... | collective-permute-start | bytes 49160 | tf_op jit(solution)/shard_map/ppermute | solution.py:899
  40.7 5.3 %collective-permute-start.7 = (bf16[64,128]{1,0:T(8,128)(2,1)S(1)}, bf16[64,128]{1,0:T(8,128)(2,1)S(1)}, u32[]{:S(2)}, u32[]{:S(2)}) collective-permute-start(bf16[64,128]{1,0:T(8,128)(2,1)S(1)} %get-tuple-element.79), channel_id=1, source_target_pairs={{32,0},{64,32},{96,64},{128,96},{160,128},{192,160},{224,192},{0,2... | collective-permute-start | bytes 49160 | tf_op jit(solution)/shard_map/ppermute | solution.py:899

commit v5 on v4

--- a/solution.py
+++ b/solution.py
@@ -453,7 +453,10 @@
             wide_ref[c, x, 10:12, :] = jnp.zeros((2, LANES), F32)
         for side in range(2):
             at = c * 40
-            wide_ref[c, 1:19, 1 + 9 * side, :] = held[side, at : at + 18, :]
+            row = 1 + 9 * side
+            wide_ref[c, 1:17, row, :] = held[side, at : at + 16, :]
+            for x in (17, 18):
+                wide_ref[c, x, row : row + 1, :] = held[side, at + x - 1 : at + x, :]
             wide_ref[c, 2:18, 11 * side, :] = held[side, at + 24 : at + 40, :]
         wide_ref[c, :, 12:16, :] = jnp.zeros((20, 4, LANES), F32)
     row, column = iota((16, LANES), 0), iota((16, LANES), 1)
@@ -939,7 +942,7 @@
         first,
         base,
         targets,
-        scratch=[pltpu.VMEM((3, 160, LANES), F32)],
+        scratch=[pltpu.VMEM((3, 208, LANES), F32)],
     )
     ylow, yhigh = both_ways(ylow, yhigh, "gy")
     back, table, faces, place, spots, later_spots = call(

time: 47.1 us -> 47.1 us (level)
  no operation moved by 1% of the time
where the time goes in v5:
time: 47.1 us; the launch traced here: 46.9 us
  starting transfers between devices  17.6 us (37%)
  blocking collectives  14.4 us (31%)
  Pallas kernels  8.77 us (19%)
  waiting for transfers between devices  4.64 us (10%)
  between operations  0.76 us (2%)
  local copies, waits for them, and re-layouts  0.68 us (1%)
    ppermute x8, starting transfers between devices, both_ways(): return (lax.ppermute(high, axis, up), lax.ppermute(low, axis, down))  17.6 us
    all_to_all x1, blocking collectives, on_device(): lax.all_to_all(volumes, ('gy', 'gz'), split_axis=0, concat_axis=0, tiled=...  14.4 us
    pallas_call x12, Pallas kernels, call(): pl.pallas_call(kernel, out_shape=out_shape, in_specs=[far if i in far_in...  8.77 us
    ppermute x8, waiting for transfers between devices, both_ways(): return (lax.ppermute(high, axis, up), lax.ppermute(low, axis, down))  4.64 us
  transfers between devices with their start and end apart: 8, of which 4 were waited for; matrix products, arithmetic and copies ran while one was open for 0% of the time, Pallas kernels for 10%

profile of v5, /device:TPU:1, one launch (start us, length us, event | category | flops | bytes accessed | tf_op | source)
XLA Modules:
  0.0 46.9 jit_solution(16847766846281695028)
XLA Ops:
  0.7 1.0 %shard_map.77 = (bf16[2,96,128]{2,1,0:T(8,128)(2,1)S(1)}, bf16[128,128]{1,0:T(8,128)(2,1)S(1)}) custom-call(f32[3,128,128]{2,1,0:T(8,128)} %bitcast.3, f32[32,4,512]{2,1,0:T(4,128)} %acoustic_ref.3), custom_call_target="tpu_custom_call" | custom-call | flops 1000000 | bytes 1000000 | tf_op jit(solution)/shard_map/pallas_call | solution.py:96
  1.7 0.3 shard_map.78
  2.0 2.5 %collective-permute-start = (bf16[160,128]{1,0:T(8,128)(2,1)S(1)}, bf16[160,128]{1,0:T(8,128)(2,1)S(1)}, u32[]{:S(2)}, u32[]{:S(2)}) collective-permute-start(bf16[160,128]{1,0:T(8,128)(2,1)S(1)} %get-tuple-element.43), channel_id=1, source_target_pairs={{0,32},{32,64},{64,96},{96,128},{128,160},{160,192},{192,224},{224... | collective-permute-start | bytes 122888 | tf_op jit(solution)/shard_map/ppermute | solution.py:902
  4.5 4.0 %collective-permute-start.1 = (bf16[160,128]{1,0:T(8,128)(2,1)S(1)}, bf16[160,128]{1,0:T(8,128)(2,1)S(1)}, u32[]{:S(2)}, u32[]{:S(2)}) collective-permute-start(bf16[160,128]{1,0:T(8,128)(2,1)S(1)} %get-tuple-element.44), channel_id=1, source_target_pairs={{32,0},{64,32},{96,64},{128,96},{160,128},{192,160},{224,192},{0,2... | collective-permute-start | bytes 122888 | tf_op jit(solution)/shard_map/ppermute | solution.py:902
  8.6 1.1 %shard_map.79 = (f32[512,128]{1,0:T(8,128)S(1)}, f32[512,128]{1,0:T(8,128)S(1)}, f32[1,128]{1,0:T(1,128)S(1)}) custom-call(f32[32,4,512]{2,1,0:T(4,128)S(1)} %copy-done.1, bf16[128,128]{1,0:T(8,128)(2,1)S(1)} %get-tuple-element.45.place_ref.chosen_ref, s32[1,32]{1,0:T(1,128)S(1)} %copy-done.3, s32[1,64]{1,0:T(1,128)S(1)} %copy-done.4), custom_call_target="tpu_custom_call" | custom-call | flops 1000000 | bytes 1000000 | tf_op jit(solution)/shard_map/pallas_call | solution.py:96
  9.7 0.2 collective-permute-done.xlow_ref
  9.9 0.2 shard_map.80
  10.1 4.2 %collective-permute-start.2 = (bf16[304,128]{1,0:T(8,128)(2,1)S(1)}, bf16[304,128]{1,0:T(8,128)(2,1)S(1)}, u32[]{:S(2)}, u32[]{:S(2)}) collective-permute-start(bf16[304,128]{1,0:T(8,128)(2,1)S(1)} %get-tuple-element.51), channel_id=1, source_target_pairs={{0,8},{8,16},{16,24},{24,0},{1,9},{9,17},{17,25},{25,1},{2,10},{10... | collective-permute-start | bytes 233480 | tf_op jit(solution)/shard_map/ppermute | solution.py:902
  14.3 0.7 %copy-done.5 = s32[32,1]{0,1:T(1,128)S(1)} copy-done((s32[32,1]{0,1:T(1,128)S(1)}, s32[32,1]{0,1:T(1,128)}, u32[]{:S(2)}) %copy-start.5) | copy-done | bytes 152
  15.0 0.7 %shard_map.81 = (bf16[128,128]{1,0:T(8,128)(2,1)S(1)}, bf16[512,256]{1,0:T(8,128)(2,1)S(1)}, bf16[6,64,256]{2,1,0:T(8,128)(2,1)S(1)}, bf16[256,256]{1,0:T(8,128)...) custom-call(f32[512,128]{1,0:T(8,128)S(1)} %get-tuple-element.49.order_ref.base_ref, ...), custom_call_target="tpu_custom_call" | custom-call | flops 1000000 | bytes 1000000 | tf_op jit(solution)/shard_map/pallas_call | solution.py:96
  15.7 3.9 %collective-permute-done.3.yhigh_ref = bf16[304,128]{1,0:T(8,128)(2,1)S(1)} collective-permute-done((bf16[304,128]{1,0:T(8,128)(2,1)S(1)}, bf16[304,128]{1,0:T(8,128)(2,1)S(1)}, u32[]{:S(2)}, u32[]{:S(2)}) %collective-permute-start.3) | collective-permute-done | bytes 77856 | tf_op jit(solution)/shard_map/ppermute | solution.py:902
  19.6 0.4 shard_map.82
  20.0 1.4 %collective-permute-start.4 = (bf16[128,128]{1,0:T(8,128)(2,1)S(1)}, bf16[128,128]{1,0:T(8,128)(2,1)S(1)}, u32[]{:S(2)}, u32[]{:S(2)}) collective-permute-start(bf16[128,128]{1,0:T(8,128)(2,1)S(1)} %get-tuple-element.55), channel_id=1, source_target_pairs={{0,1},{1,2},{2,3},{3,4},{4,5},{5,6},{6,7},{7,0},{8,9},{9,10},{10,1... | collective-permute-start | bytes 98312 | tf_op jit(solution)/shard_map/ppermute | solution.py:902
  21.4 2.3 %collective-permute-start.5 = (bf16[128,128]{1,0:T(8,128)(2,1)S(1)}, bf16[128,128]{1,0:T(8,128)(2,1)S(1)}, u32[]{:S(2)}, u32[]{:S(2)}) collective-permute-start(bf16[128,128]{1,0:T(8,128)(2,1)S(1)} %get-tuple-element.56), channel_id=1, source_target_pairs={{1,0},{2,1},{3,2},{4,3},{5,4},{6,5},{7,6},{0,7},{9,8},{10,9},{11,1... | collective-permute-start | bytes 98312 | tf_op jit(solution)/shard_map/ppermute | solution.py:902
  23.6 0.5 %shard_map.83 = (f32[3,20,16,128]{3,2,1,0:T(8,128)S(1)}, f32[2,96,128]{2,1,0:T(8,128)S(1)}) custom-call(f32[3,20,16,128]{3,2,1,0:T(8,128)S(1)} %get-tuple-element.53.wide_ref), custom_call_target="tpu_custom_call" | custom-call | flops 1000000 | bytes 1000000 | tf_op jit(solution)/shard_map/pallas_call | solution.py:96
  24.2 0.3 shard_map.85
  24.4 0.5 %collective-permute-done.4.zlow_ref = bf16[128,128]{1,0:T(8,128)(2,1)S(1)} collective-permute-done((bf16[128,128]{1,0:T(8,128)(2,1)S(1)}, bf16[128,128]{1,0:T(8,128)(2,1)S(1)}, u32[]{:S(2)}, u32[]{:S(2)}) %collective-permute-start.4) | collective-permute-done | bytes 32800 | tf_op jit(solution)/shard_map/ppermute | solution.py:902
  24.9 0.9 %shard_map.84 = (f32[3,128,128]{2,1,0:T(8,128)S(1)}, bf16[32,24,128]{2,1,0:T(8,128)(2,1)S(1)}, f32[512,128]{1,0:T(8,128)S(1)}) custom-call(f32[3,20,16,128]{3,2,1,0:T(8,128)S(1)} %get-tuple-element.53.wide_ref, f32[3,8,384]{2,1,0:T(8,128)S(1)} %get-tuple-element.54.own_ref, bf16[128,128]{1,0:T(8,128)(2,1)S(1)} %collective-permute-done.4.zlow_ref, ...), custom_call_target="tpu_custom_call" | custom-call | flops 1000000 | bytes 1000000 | tf_op jit(solution)/shard_map/pallas_call | solution.py:96
  25.8 14.4 %all_to_all.5.arrived_ref = bf16[32,24,128]{2,1,0:T(8,128)(2,1)S(1)} all-to-all(bf16[32,24,128]{2,1,0:T(8,128)(2,1)S(1)} %get-tuple-element.66), channel_id=1, replica_groups=mesh['gx'=8,'gy'=4,'gz'=8] {'gy','gz'}, dimensions={0} | all-to-all | bytes 393216 | tf_op jit(solution)/shard_map/all_to_all | solution.py:1016
  40.3 0.4 shard_map.86
  40.6 0.1 collective-permute-start.6
  40.7 3.1 %collective-permute-start.7 = (bf16[64,128]{1,0:T(8,128)(2,1)S(1)}, bf16[64,128]{1,0:T(8,128)(2,1)S(1)}, u32[]{:S(2)}, u32[]{:S(2)}) collective-permute-start(bf16[64,128]{1,0:T(8,128)(2,1)S(1)} %get-tuple-element.79), channel_id=1, source_target_pairs={{32,0},{64,32},{96,64},{128,96},{160,128},{192,160},{224,192},{0,2... | collective-permute-start | bytes 49160 | tf_op jit(solution)/shard_map/ppermute | solution.py:902
  43.8 2.1 %shard_map.87 = (f32[32,4,512]{2,1,0:T(4,128)}, f32[2,128,128]{2,1,0:T(8,128)S(1)}, f32[3,128,128]{2,1,0:T(8,128)}) custom-call(bf16[32,24,128]{2,1,0:T(8,128)(2,1)S(1)} %all_to_all.5.arrived_ref, bf16[2,256,512]{2,1,0:T(8,128)(2,1)S(1)} %get-tuple-element.67.gather_ref, bf16[512,256]{1,0:T(8,128)(2,1)S(1)} %get-tuple-element.68.table_ref, ...), custom_call_target="tpu_custom_call" | custom-call | flops 1000000 | bytes 1000000 | tf_op jit(solution)/shard_map/pallas_call | solution.py:96
  46.0 0.9 %shard_map.88 = f32[32,4,512]{2,1,0:T(4,128)} custom-call(f32[32,4,512]{2,1,0:T(4,128)} %get-tuple-element.76.main_ref, f32[2,128,128]{2,1,0:T(8,128)S(1)} %get-tuple-element.77.ends_ref, bf16[128,128]{1,0:T(8,128)(2,1)S(1)} %get-tuple-element.73.back_ref, bf16[64,128]{1,0:T(8,128)(2,1)S(1)} %collective-permute-done.6.low_ref, ...), custom_call_target="tpu_custom_call", output_to_operand_aliasing={{}: (0, {})} | custom-call | flops 1000000 | bytes 1000000 | tf_op jit(solution)/shard_map/pallas_call | solution.py:96
  (17 shorter events, 0.1 us)
Async XLA Ops:
  0.6 1.1 %copy-start.3 = (s32[1,32]{1,0:T(1,128)S(1)}, s32[1,32]{1,0:T(1,128)}, u32[]{:S(2)}) copy-start(s32[1,32]{1,0:T(1,128)} %cell_ref.3) | copy-start | bytes 388
  0.6 7.9 %copy-start.1 = (f32[32,4,512]{2,1,0:T(4,128)S(1)}, f32[32,4,512]{2,1,0:T(4,128)}, u32[]{:S(2)}) copy-start(f32[32,4,512]{2,1,0:T(4,128)} %acoustic_ref.3) | copy-start | bytes 786436
  0.7 7.9 %copy-start.4 = (s32[1,64]{1,0:T(1,128)S(1)}, s32[1,64]{1,0:T(1,128)}, u32[]{:S(2)}) copy-start(s32[1,64]{1,0:T(1,128)} %slot_ref.1) | copy-start | bytes 772
  1.7 8.2 %copy-start = (f32[3,16,8,128]{3,2,1,0:T(8,128)S(1)}, f32[3,16,8,128]{3,2,1,0:T(8,128)}, u32[]{:S(2)}) copy-start(f32[3,16,8,128]{3,2,1,0:T(8,128)} %param.6) | copy-start | bytes 589828
  2.0 7.9 %collective-permute-start = (bf16[160,128]{1,0:T(8,128)(2,1)S(1)}, bf16[160,128]{1,0:T(8,128)(2,1)S(1)}, u32[]{:S(2)}, u32[]{:S(2)}) collective-permute-start(bf16[160,128]{1,0:T(8,128)(2,1)S(1)} %get-tuple-element.43), channel_id=1, source_target_pairs={{0,32},{32,64},{64,96},{96,128},{128,160},{160,192},{192,224},{224... | collective-permute-start | bytes 122888 | tf_op jit(solution)/shard_map/ppermute | solution.py:902
  4.5 5.3 %collective-permute-start.1 = (bf16[160,128]{1,0:T(8,128)(2,1)S(1)}, bf16[160,128]{1,0:T(8,128)(2,1)S(1)}, u32[]{:S(2)}, u32[]{:S(2)}) collective-permute-start(bf16[160,128]{1,0:T(8,128)(2,1)S(1)} %get-tuple-element.44), channel_id=1, source_target_pairs={{32,0},{64,32},{96,64},{128,96},{160,128},{192,160},{224,192},{0,2... | collective-permute-start | bytes 122888 | tf_op jit(solution)/shard_map/ppermute | solution.py:902
  9.9 4.4 %copy-start.2 = (f32[64,512]{1,0:T(8,128)S(1)}, f32[64,512]{1,0:T(8,128)}, u32[]{:S(2)}) copy-start(f32[64,512]{1,0:T(8,128)} %projection_ref.1) | copy-start | bytes 393220
  10.1 5.7 %collective-permute-start.2 = (bf16[304,128]{1,0:T(8,128)(2,1)S(1)}, bf16[304,128]{1,0:T(8,128)(2,1)S(1)}, u32[]{:S(2)}, u32[]{:S(2)}) collective-permute-start(bf16[304,128]{1,0:T(8,128)(2,1)S(1)} %get-tuple-element.51), channel_id=1, source_target_pairs={{0,8},{8,16},{16,24},{24,0},{1,9},{9,17},{17,25},{25,1},{2,10},{10... | collective-permute-start | bytes 233480 | tf_op jit(solution)/shard_map/ppermute | solution.py:902
  14.3 5.3 %collective-permute-start.3 = (bf16[304,128]{1,0:T(8,128)(2,1)S(1)}, bf16[304,128]{1,0:T(8,128)(2,1)S(1)}, u32[]{:S(2)}, u32[]{:S(2)}) collective-permute-start(bf16[304,128]{1,0:T(8,128)(2,1)S(1)} %get-tuple-element.52), channel_id=1, source_target_pairs={{8,0},{16,8},{24,16},{0,24},{9,1},{17,9},{25,17},{1,25},{10,2},{18... | collective-permute-start | bytes 233480 | tf_op jit(solution)/shard_map/ppermute | solution.py:902
  14.3 0.7 %copy-start.5 = (s32[32,1]{0,1:T(1,128)S(1)}, s32[32,1]{0,1:T(1,128)}, u32[]{:S(2)}) copy-start(s32[32,1]{0,1:T(1,128)} %param.9) | copy-start | bytes 388
  20.0 5.0 %collective-permute-start.4 = (bf16[128,128]{1,0:T(8,128)(2,1)S(1)}, bf16[128,128]{1,0:T(8,128)(2,1)S(1)}, u32[]{:S(2)}, u32[]{:S(2)}) collective-permute-start(bf16[128,128]{1,0:T(8,128)(2,1)S(1)} %get-tuple-element.55), channel_id=1, source_target_pairs={{0,1},{1,2},{2,3},{3,4},{4,5},{5,6},{6,7},{7,0},{8,9},{9,10},{10,1... | collective-permute-start | bytes 98312 | tf_op jit(solution)/shard_map/ppermute | solution.py:902
  21.4 3.6 %collective-permute-start.5 = (bf16[128,128]{1,0:T(8,128)(2,1)S(1)}, bf16[128,128]{1,0:T(8,128)(2,1)S(1)}, u32[]{:S(2)}, u32[]{:S(2)}) collective-permute-start(bf16[128,128]{1,0:T(8,128)(2,1)S(1)} %get-tuple-element.56), channel_id=1, source_target_pairs={{1,0},{2,1},{3,2},{4,3},{5,4},{6,5},{7,6},{0,7},{9,8},{10,9},{11,1... | collective-permute-start | bytes 98312 | tf_op jit(solution)/shard_map/ppermute | solution.py:902
  40.6 5.3 %collective-permute-start.6 = (bf16[64,128]{1,0:T(8,128)(2,1)S(1)}, bf16[64,128]{1,0:T(8,128)(2,1)S(1)}, u32[]{:S(2)}, u32[]{:S(2)}) collective-permute-start(bf16[64,128]{1,0:T(8,128)(2,1)S(1)} %get-tuple-element.78), channel_id=1, source_target_pairs={{0,32},{32,64},{64,96},{96,128},{128,160},{160,192},{192,224},{224... | collective-permute-start | bytes 49160 | tf_op jit(solution)/shard_map/ppermute | solution.py:902
  40.7 5.3 %collective-permute-start.7 = (bf16[64,128]{1,0:T(8,128)(2,1)S(1)}, bf16[64,128]{1,0:T(8,128)(2,1)S(1)}, u32[]{:S(2)}, u32[]{:S(2)}) collective-permute-start(bf16[64,128]{1,0:T(8,128)(2,1)S(1)} %get-tuple-element.79), channel_id=1, source_target_pairs={{32,0},{64,32},{96,64},{128,96},{160,128},{192,160},{224,192},{0,2... | collective-permute-start | bytes 49160 | tf_op jit(solution)/shard_map/ppermute | solution.py:902
